TPU v7x, 32 devices: a whole 2x2x4 slice. The times are simulated.
32 devices in a mesh: gx: 8 (over z, x), gy: 4 (over y, core).
Axes of the slice: x: 2, y: 2, z: 4, core: 2. Of those that a mesh axis runs over, the one named last changes fastest.
Arguments:
- residual: float32 [2, 256, 192, 256], P(None, 'gx', 'gy'), may hold values from -6 to 6
- accum_diag: float32 [2, 256, 192, 256], P(None, 'gx', 'gy'), may hold values from 2 to 4
- accum_cross: float32 [2, 256, 192, 256], P(None, 'gx', 'gy'), may hold values from -1 to 1
- mask: int32 [256, 192, 256], P('gx', 'gy'), may hold values from 0 to 1
- trans_x: float32 [256, 192, 256], P('gx', 'gy'), may hold values from 0.1 to 10
- trans_y: float32 [256, 192, 256], P('gx', 'gy'), may hold values from 0.1 to 10
- trans_z: float32 [256, 192, 256], P('gx', 'gy'), may hold values from 0.1 to 10
- frac_flow: float32 [256, 192, 256], P('gx', 'gy'), may hold values from 0 to 1
- split_layer: int32 [32, 24], P('gx', 'gy'), may hold values from 64 to 191
- coarse_inverse: float32 [8, 192, 192], P('gx'), may hold values from -0.0034179688 to 0.0034179688
Outputs:
- correction: float32 [2, 256, 192, 256], P(None, 'gx', 'gy')
All inputs are finite; a program needn't handle non-finite values.
Results may differ from a plain program's by a relative error of at most 0.00027.
Values sent between devices are 32-bit elements; how exact they have to be, the bound alone decides.
No kernel may reach another device: no remote copies, remote signals or barrier semaphores. Data moves between devices by JAX's collectives and lax.ppermute only.
A program may use at most 192 MiB of HBM per device.

v0:
```python
import jax
import jax.numpy as jnp
from jax import lax
from jax.sharding import PartitionSpec as P

relaxation = 2.0 / 3.0


def extended(array, sides, width):
    for axis, dim in sides:
        count, length = (lax.axis_size(axis), array.shape[dim])
        up = [(i, (i + 1) % count) for i in range(count - 1)]
        down = [(j, i) for i, j in up]
        last = lax.slice_in_dim(array, length - width, length, axis=dim)
        leading = lax.slice_in_dim(array, 0, width, axis=dim)
        before = lax.ppermute(last, axis, up)
        after = lax.ppermute(leading, axis, down)
        array = jnp.concatenate([before, array, after], axis=dim)
    return array


def forward(field, along):
    size = field.shape[along]
    moved = lax.slice_in_dim(field, 1, size, axis=along)
    zero_shape = list(field.shape)
    zero_shape[along] = 1
    return jnp.concatenate([moved, jnp.zeros(zero_shape, field.dtype)], axis=along)


def backward(field, along):
    size = field.shape[along]
    moved = lax.slice_in_dim(field, 0, size - 1, axis=along)
    zero_shape = list(field.shape)
    zero_shape[along] = 1
    return jnp.concatenate([jnp.zeros(zero_shape, field.dtype), moved], axis=along)


def face_coefs(active, tran_x, tran_y, tran_z):
    face_x = tran_x * active * forward(active, 0)
    face_y = tran_y * active * forward(active, 1)
    face_z = tran_z * active * forward(active, 2)
    return (face_x, face_y, face_z)


def face_total(face_x, face_y, face_z):
    return (
        face_x + backward(face_x, 0) + face_y + backward(face_y, 1) + face_z + backward(face_z, 2)
    )


def net_flux(field, face_x, face_y, face_z):
    beside = face_x * forward(field, 0) + backward(face_x, 0) * backward(field, 0)
    beside = beside + face_y * forward(field, 1) + backward(face_y, 1) * backward(field, 1)
    beside = beside + face_z * forward(field, 2) + backward(face_z, 2) * backward(field, 2)
    return face_total(face_x, face_y, face_z) * field - beside


def weighted(face_x, face_y, face_z, fraction):
    return (
        face_x * (fraction + forward(fraction, 0)) * 0.5,
        face_y * (fraction + forward(fraction, 1)) * 0.5,
        face_z * (fraction + forward(fraction, 2)) * 0.5,
    )


def below_split(split_layer, layers):
    levels = jnp.arange(layers, dtype=jnp.int32)
    return (levels[None, None, :] < split_layer[:, :, None]).astype(jnp.float32)


def restrict(field, split_layer):
    rows_b = field.shape[0] // 8
    cols_b = field.shape[1] // 8
    layers = field.shape[2]
    blocks = field.reshape(rows_b, 8, cols_b, 8, layers).sum(axis=(1, 3))
    lower_part = below_split(split_layer, layers)
    return jnp.stack(
        [jnp.sum(blocks * lower_part, axis=-1), jnp.sum(blocks * (1.0 - lower_part), axis=-1)],
        axis=-1,
    )


def prolong(values, split_layer, layers):
    rows_b = values.shape[0]
    cols_b = values.shape[1]
    lower_part = below_split(split_layer, layers)
    cellwise = values[:, :, 0:1] * lower_part + values[:, :, 1:2] * (1.0 - lower_part)
    spread = jnp.broadcast_to(cellwise[:, None, :, None, :], (rows_b, 8, cols_b, 8, layers))
    return spread.reshape(rows_b * 8, cols_b * 8, layers)


def pressure_border(field):
    return extended(field, (("gx", 0), ("gy", 1)), 1)


def inner(field):
    return field[1:-1, 1:-1]


def shards(
    residual,
    accum_diag,
    accum_cross,
    mask,
    trans_x,
    trans_y,
    trans_z,
    frac_flow,
    split_layer,
    coarse_inverse,
):
    active = mask.astype(jnp.float32)
    pressure_res, saturation_res = (residual[0], residual[1])
    diag_pp, diag_ss = (accum_diag[0], accum_diag[1])
    cross_ps, cross_sp = (accum_cross[0], accum_cross[1])
    weighting = cross_ps / diag_ss
    pressure_rhs = active * (pressure_res - weighting * saturation_res)
    schur_diag = active * (diag_pp - weighting * cross_sp) + (1.0 - active)
    stacked = jnp.stack([active, trans_x, trans_y, frac_flow])
    bordered = extended(stacked, (("gx", 1), ("gy", 2)), 1)
    tz_bordered = jnp.pad(trans_z, ((1, 1), (1, 1), (0, 0)))
    face_x, face_y, face_z = face_coefs(bordered[0], bordered[1], bordered[2], tz_bordered)
    wface_x, wface_y, wface_z = weighted(face_x, face_y, face_z, bordered[3])
    diagonal = schur_diag + inner(face_total(face_x, face_y, face_z))
    sweep_one = relaxation * pressure_rhs / diagonal
    one_bordered = pressure_border(sweep_one)
    sweep_two = (
        sweep_one
        + relaxation
        * (
            pressure_rhs
            - schur_diag * sweep_one
            - inner(net_flux(one_bordered, face_x, face_y, face_z))
        )
        / diagonal
    )
    two_bordered = pressure_border(sweep_two)
    remain = (
        pressure_rhs
        - schur_diag * sweep_two
        - inner(net_flux(two_bordered, face_x, face_y, face_z))
    )
    rows_b = split_layer.shape[0]
    cols_b = split_layer.shape[1]
    agg_count = rows_b * cols_b * 2
    local_coarse = restrict(remain, split_layer).reshape(agg_count)
    matrix = coarse_inverse[0]
    gathered = lax.all_gather(local_coarse, "gy", axis=0, tiled=True)
    full_corr = jnp.dot(matrix, gathered, precision=lax.Precision.HIGHEST)
    own_part = lax.dynamic_slice_in_dim(full_corr, lax.axis_index("gy") * agg_count, agg_count)
    corrected = sweep_two + active * prolong(
        own_part.reshape(rows_b, cols_b, 2), split_layer, remain.shape[2]
    )
    three_bordered = pressure_border(corrected)
    jac_p = diag_pp * corrected + inner(net_flux(three_bordered, face_x, face_y, face_z))
    jac_s = cross_sp * corrected + inner(net_flux(three_bordered, wface_x, wface_y, wface_z))
    update_p = pressure_res - jac_p
    update_s = saturation_res - jac_s
    determinant = diag_pp * diag_ss - cross_ps * cross_sp
    out_p = corrected + (diag_ss * update_p - cross_ps * update_s) / determinant
    out_s = (diag_pp * update_s - cross_sp * update_p) / determinant
    return jnp.stack([out_p, out_s])


def solution(mesh):
    placed = (
        P(None, "gx", "gy", None),
        P(None, "gx", "gy", None),
        P(None, "gx", "gy", None),
        P("gx", "gy", None),
        P("gx", "gy", None),
        P("gx", "gy", None),
        P("gx", "gy", None),
        P("gx", "gy", None),
        P("gx", "gy"),
        P("gx", None, None),
    )
    return jax.shard_map(
        shards, mesh=mesh, in_specs=placed, out_specs=P(None, "gx", "gy", None), check_vma=False
    )
```

profile of v0, /device:TPU:0, one launch (start us, length us, event | category | flops | bytes accessed | tf_op | source)
XLA Modules:
  0.0 179.7 jit_solution(7700247394145718991)
XLA Ops:
  3.4 4.9 %collective-permute-start = (f32[4,1,48,256]{3,2,1,0:T(8,128)S(1)}, f32[4,1,48,256]{3,2,1,0:T(8,128)S(1)}, u32[]{:S(2)}, u32[]{:S(2)}) collective-permute-start(f32[4,1,48,256]{3,2,1,0:T(8,128)S(1)} %get-tuple-element.32), channel_id=1, source_target_pairs={{0,4},{4,8},{8,12},{12,16},{16,20},{20,24},{24,28},{1,5},{5,9},{9,... | collective-permute-start | bytes 589832 | tf_op jit(solution)/shard_map/ppermute | solution.py:16
  9.5 2.9 %collective-permute-done = f32[4,1,48,256]{3,2,1,0:T(8,128)S(1)} collective-permute-done((f32[4,1,48,256]{3,2,1,0:T(8,128)S(1)}, f32[4,1,48,256]{3,2,1,0:T(8,128)S(1)}, u32[]{:S(2)}, u32[]{:S(2)}) %collective-permute-start) | collective-permute-done | bytes 196640 | tf_op jit(solution)/shard_map/ppermute | solution.py:16
  12.4 4.0 %collective-permute-done.1 = f32[4,1,48,256]{3,2,1,0:T(8,128)S(1)} collective-permute-done((f32[4,1,48,256]{3,2,1,0:T(8,128)S(1)}, f32[4,1,48,256]{3,2,1,0:T(8,128)S(1)}, u32[]{:S(2)}, u32[]{:S(2)}) %collective-permute-start.1) | collective-permute-done | bytes 196640 | tf_op jit(solution)/shard_map/ppermute | solution.py:17
  19.3 3.7 %collective-permute-done.3 = f32[4,34,1,256]{3,2,1,0:T(1,128)S(1)} collective-permute-done((f32[4,34,1,256]{3,2,1,0:T(1,128)S(1)}, f32[4,34,1,256]{3,2,1,0:T(1,128)S(1)}, u32[]{:S(2)}, u32[]{:S(2)}) %collective-permute-start.3) | collective-permute-done | bytes 139296 | tf_op jit(solution)/shard_map/ppermute | solution.py:17
  23.0 3.2 %pad_maximum_fusion = f32[4,34,50,256]{3,2,1,0:T(8,128)S(1)} fusion(f32[4,34,1,256]{3,2,1,0:T(1,128)S(1)} %collective-permute-done.3, f32[4,1,48,256]{3,2,1,0:T(8,128)S(1)} %collective-permute-done.1, f32[1,32,48,256]{3,2,1,0:T(8,128)S(1)} %bitcast.156, f32[1,32,48,256]{3,2,1,0:T(8,128)S(1)} %bitcast.159, f32[1,32,48,256]{3,2,1,0:T(8,128)S(1)} %bitcast.162, ...), kind=kLoop, calls=%fused_computation | loop fusion | flops 12185600 | bytes 13926400 | tf_op jit(solution)/shard_map/concatenate | solution.py:18
  30.5 3.3 %multiply_multiply_fusion.1 = (f32[34,50,256]{2,1,0:T(8,128)}, f32[34,50,256]{2,1,0:T(8,128)S(1)}, f32[34,50,256]{2,1,0:T(8,128)S(1)}, f32[34,50,256]{2,1,0:T(8,128)}, f32[34,50,256]{2,1,0:T(8,128)S(1)}) fusion(f32[34,49,256]{2,1,0:T(8,128)S(1)} %slice.339, f32[4,34,50,256]{3,2,1,0:T(8,128)S(1)} %pad_maximum_fusion, f32[34,49,256]{2,1,0:T(8,128)S(1)} %slice.282, ...), kind=kLoop, calls=%fused_computation.37 | loop fusion | flops 5222400 | bytes 25809632 | tf_op jit(solution)/shard_map/mul | solution.py:61
  35.2 2.5 %copy-done.16 = f32[2,32,48,256]{3,2,1,0:T(8,128)S(1)} copy-done((f32[2,32,48,256]{3,2,1,0:T(8,128)S(1)}, f32[2,32,48,256]{3,2,1,0:T(8,128)}, u32[]{:S(2)}) %copy-start.16) | copy-done | bytes 3145752
  38.7 4.6 %multiply_divide_fusion = (f32[32,48,256]{2,1,0:T(8,128)S(1)}, f32[32,48,256]{2,1,0:T(8,128)S(1)}, f32[32,48,256]{2,1,0:T(8,128)S(1)}) fusion(f32[34,50,256]{2,1,0:T(8,128)S(1)} %pad_add_fusion, f32[2,32,48,256]{3,2,1,0:T(8,128)S(1)} %copy-done.16, f32[2,32,48,256]{3,2,1,0:T(8,128)S(1)} %copy-done.17, s32[32,48,256]{2,1,0:T(8,128)} %param.13, ...), kind=kLoop, calls=%fused_computation.131 | loop fusion | flops 5111808 | bytes 17301504 | tf_op jit(solution)/shard_map/div | solution.py:125
  43.3 4.5 %collective-permute-start.4 = (f32[1,48,256]{2,1,0:T(8,128)S(1)}, f32[1,48,256]{2,1,0:T(8,128)S(1)}, u32[]{:S(2)}, u32[]{:S(2)}) collective-permute-start(f32[1,48,256]{2,1,0:T(8,128)S(1)} %get-tuple-element.66), channel_id=1, source_target_pairs={{0,4},{4,8},{8,12},{12,16},{16,20},{20,24},{24,28},{1,5},{5,9},{9,... | collective-permute-start | bytes 147464 | tf_op jit(solution)/shard_map/ppermute | solution.py:16
  49.5 4.7 %collective-permute-done.5 = f32[1,48,256]{2,1,0:T(8,128)S(1)} collective-permute-done((f32[1,48,256]{2,1,0:T(8,128)S(1)}, f32[1,48,256]{2,1,0:T(8,128)S(1)}, u32[]{:S(2)}, u32[]{:S(2)}) %collective-permute-start.5) | collective-permute-done | bytes 49184 | tf_op jit(solution)/shard_map/ppermute | solution.py:17
  54.3 4.4 %collective-permute-start.6 = (f32[34,1,256]{2,1,0:T(1,128)S(1)}, f32[34,1,256]{2,1,0:T(1,128)S(1)}, u32[]{:S(2)}, u32[]{:S(2)}) collective-permute-start(f32[34,1,256]{2,1,0:T(1,128)S(1)} %get-tuple-element.60), channel_id=1, source_target_pairs={{0,1},{1,2},{2,3},{4,5},{5,6},{6,7},{8,9},{9,10},{10,11},{12,13},{... | collective-permute-start | bytes 104456 | tf_op jit(solution)/shard_map/ppermute | solution.py:16
  59.9 2.3 %collective-permute-done.7 = f32[34,1,256]{2,1,0:T(1,128)S(1)} collective-permute-done((f32[34,1,256]{2,1,0:T(1,128)S(1)}, f32[34,1,256]{2,1,0:T(1,128)S(1)}, u32[]{:S(2)}, u32[]{:S(2)}) %collective-permute-start.7) | collective-permute-done | bytes 34848 | tf_op jit(solution)/shard_map/ppermute | solution.py:17
  62.3 2.7 %select_maximum_fusion.11 = (f32[34,50,256]{2,1,0:T(8,128)}, f32[34,50,256]{2,1,0:T(8,128)S(1)}, f32[34,50,256]{2,1,0:T(8,128)}, f32[34,50,256]{2,1,0:T(8,128)}) fusion(f32[34,1,256]{2,1,0:T(1,128)S(1)} %collective-permute-done.7, f32[1,48,256]{2,1,0:T(8,128)S(1)} %collective-permute-done.5, f32[32,48,256]{2,1,0:T(8,128)S(1)} %get-tuple-element.19, ...), kind=kLoop, calls=%fused_computation.22 | loop fusion | flops 8268800 | bytes 8704000 | tf_op jit(solution)/shard_map/concatenate | solution.py:18
  67.4 6.9 %fusion.29 = f32[32,48,256]{2,1,0:T(8,128)S(1)} fusion(f32[33,50,256]{2,1,0:T(8,128)S(1)} %get-tuple-element.44, f32[34,50,256]{2,1,0:T(8,128)S(1)} %get-tuple-element.53, f32[34,50,255]{2,1,0:T(8,128)S(1)} %get-tuple-element.46, f32[34,50,255]{2,1,0:T(8,128)S(1)} %get-tuple-element.45, f32[34,50,256]{2,1,0:T(8,128)} %get-tuple-element.59, ...), kind=kLoop, calls=%fused_computation.72 | loop fusion | flops 8650752 | bytes 27588688 | tf_op jit(solution)/shard_map/add | solution.py:128
  74.4 5.0 %collective-permute-start.8 = (f32[1,48,256]{2,1,0:T(8,128)S(1)}, f32[1,48,256]{2,1,0:T(8,128)S(1)}, u32[]{:S(2)}, u32[]{:S(2)}) collective-permute-start(f32[1,48,256]{2,1,0:T(8,128)S(1)} %get-tuple-element.64), channel_id=1, source_target_pairs={{0,4},{4,8},{8,12},{12,16},{16,20},{20,24},{24,28},{1,5},{5,9},{9,... | collective-permute-start | bytes 147464 | tf_op jit(solution)/shard_map/ppermute | solution.py:16
  81.1 4.3 %collective-permute-done.9 = f32[1,48,256]{2,1,0:T(8,128)S(1)} collective-permute-done((f32[1,48,256]{2,1,0:T(8,128)S(1)}, f32[1,48,256]{2,1,0:T(8,128)S(1)}, u32[]{:S(2)}, u32[]{:S(2)}) %collective-permute-start.9) | collective-permute-done | bytes 49184 | tf_op jit(solution)/shard_map/ppermute | solution.py:17
  85.4 3.1 %collective-permute-start.10 = (f32[34,1,256]{2,1,0:T(1,128)S(1)}, f32[34,1,256]{2,1,0:T(1,128)S(1)}, u32[]{:S(2)}, u32[]{:S(2)}) collective-permute-start(f32[34,1,256]{2,1,0:T(1,128)S(1)} %get-tuple-element.57), channel_id=1, source_target_pairs={{0,1},{1,2},{2,3},{4,5},{5,6},{6,7},{8,9},{9,10},{10,11},{12,13},{... | collective-permute-start | bytes 104456 | tf_op jit(solution)/shard_map/ppermute | solution.py:16
  92.5 4.6 %select_maximum_fusion.8 = (f32[34,50,256]{2,1,0:T(8,128)}, f32[34,50,256]{2,1,0:T(8,128)S(1)}, f32[34,50,256]{2,1,0:T(8,128)}, f32[34,50,256]{2,1,0:T(8,128)}) fusion(f32[34,1,256]{2,1,0:T(1,128)S(1)} %collective-permute-done.11, f32[1,48,256]{2,1,0:T(8,128)S(1)} %collective-permute-done.9, f32[32,48,256]{2,1,0:T(8,128)} %copy-done.10, ...), kind=kLoop, calls=%fused_computation.12 | loop fusion | flops 8268800 | bytes 8704000 | tf_op jit(solution)/shard_map/concatenate | solution.py:18
  102.2 7.1 %fusion.37 = f32[32,48,256]{2,1,0:T(8,128)} fusion(f32[33,50,256]{2,1,0:T(8,128)S(1)} %get-tuple-element.40, f32[34,50,256]{2,1,0:T(8,128)S(1)} %get-tuple-element.51, f32[34,50,255]{2,1,0:T(8,128)S(1)} %get-tuple-element.42, f32[34,50,255]{2,1,0:T(8,128)S(1)} %get-tuple-element.41, f32[34,50,256]{2,1,0:T(8,128)} %get-tuple-element.56, ...), kind=kLoop, calls=%fused_computation.80 | loop fusion | flops 6291456 | bytes 29161552 | tf_op jit(solution)/shard_map/sub | solution.py:139
  111.5 8.3 %all-reduce.31 = f32[192]{0:T(256)S(1)} all-reduce(f32[192]{0:T(256)S(1)} %dynamic-update-slice), channel_id=1, replica_groups=mesh['gx'=8,'gy'=4] {'gy'}, use_global_device_ids=true, to_apply=%add.31 | all-reduce | flops 192 | bytes 1536
  121.6 1.9 %multiply_add_fusion.1 = f32[32,48,256]{2,1,0:T(8,128)S(1)} fusion(f32[32,48,256]{2,1,0:T(8,128)S(1)} %copy-done.12, f32[32,48,256]{2,1,0:T(8,128)S(1)} %bitcast.164, s32[32,48,256]{2,1,0:T(8,128)} %param.13), kind=kLoop, calls=%fused_computation.130 | loop fusion | flops 1179648 | bytes 6291456 | tf_op jit(solution)/shard_map/add | solution.py:151
  123.6 2.9 %collective-permute-start.12 = (f32[1,48,256]{2,1,0:T(8,128)S(1)}, f32[1,48,256]{2,1,0:T(8,128)S(1)}, u32[]{:S(2)}, u32[]{:S(2)}) collective-permute-start(f32[1,48,256]{2,1,0:T(8,128)S(1)} %get-tuple-element.62), channel_id=1, source_target_pairs={{0,4},{4,8},{8,12},{12,16},{16,20},{20,24},{24,28},{1,5},{5,9},{9,... | collective-permute-start | bytes 147464 | tf_op jit(solution)/shard_map/ppermute | solution.py:16
  128.2 4.3 %collective-permute-done.13 = f32[1,48,256]{2,1,0:T(8,128)S(1)} collective-permute-done((f32[1,48,256]{2,1,0:T(8,128)S(1)}, f32[1,48,256]{2,1,0:T(8,128)S(1)}, u32[]{:S(2)}, u32[]{:S(2)}) %collective-permute-start.13) | collective-permute-done | bytes 49184 | tf_op jit(solution)/shard_map/ppermute | solution.py:17
  135.2 3.7 %collective-permute-done.15 = f32[34,1,256]{2,1,0:T(1,128)S(1)} collective-permute-done((f32[34,1,256]{2,1,0:T(1,128)S(1)}, f32[34,1,256]{2,1,0:T(1,128)S(1)}, u32[]{:S(2)}, u32[]{:S(2)}) %collective-permute-start.15) | collective-permute-done | bytes 34848 | tf_op jit(solution)/shard_map/ppermute | solution.py:17
  138.8 2.3 %select_maximum_fusion.3 = (f32[34,50,256]{2,1,0:T(8,128)}, f32[34,50,256]{2,1,0:T(8,128)S(1)}, f32[34,50,256]{2,1,0:T(8,128)}) fusion(f32[34,1,256]{2,1,0:T(1,128)S(1)} %collective-permute-done.15, f32[1,48,256]{2,1,0:T(8,128)S(1)} %collective-permute-done.13, f32[32,48,256]{2,1,0:T(8,128)S(1)} %multiply_add_fusion.1, ...), kind=kLoop, calls=%fused_computation.6 | loop fusion | flops 8704000 | bytes 6963200 | tf_op jit(solution)/shard_map/concatenate | solution.py:18
  141.1 1.7 fusion.72
  143.0 2.6 %fusion.73 = (f32[34,50,255]{2,1,0:T(8,128)}, f32[34,50,255]{2,1,0:T(8,128)}) fusion(f32[34,50,256]{2,1,0:T(8,128)S(1)} %get-tuple-element.48), kind=kLoop, calls=%fused_computation.164 | loop fusion | bytes 6936000 | tf_op jit(solution)/shard_map/slice | solution.py:24
  146.4 4.0 %pad_multiply_fusion.3 = (f32[34,50,256]{2,1,0:T(8,128)}, f32[34,50,256]{2,1,0:T(8,128)S(1)}, f32[34,50,256]{2,1,0:T(8,128)}) fusion(f32[33,50,256]{2,1,0:T(8,128)S(1)} %get-tuple-element.35, f32[34,50,256]{2,1,0:T(8,128)S(1)} %copy-done.6, f32[33,50,256]{2,1,0:T(8,128)S(1)} %copy-done.26, f32[4,34,50,256]{3,2,1,0:T(8,128)} %copy-done.3), kind=kLoop, calls=%fused_computation.50 | loop fusion | flops 2176000 | bytes 12083200 | tf_op jit(solution)/shard_map/mul | solution.py:52
  150.6 1.7 pad_add_fusion.1
  152.5 21.1 %fusion.63 = (f32[1,32,48,256]{3,2,1,0:T(8,128)}, f32[32,48,256]{2,1,0:T(8,128)}, f32[32,48,256]{2,1,0:T(8,128)}, f32[32,48,256]{2,1,0:T(8,128)}) fusion(f32[32,48,256]{2,1,0:T(8,128)} %copy-done.15, f32[2,32,48,256]{3,2,1,0:T(8,128)} %param.11, f32[2,32,48,256]{3,2,1,0:T(8,128)} %param.12, f32[34,50,255]{2,1,0:T(8,128)} %get-tuple-element.38, ...), kind=kLoop, calls=%fused_computation.128 | loop fusion | flops 16515072 | bytes 50019776 | tf_op jit(solution)/shard_map/stack | solution.py:162
  173.6 4.2 %fusion.57 = f32[1,32,48,256]{3,2,1,0:T(8,128)S(1)} fusion(f32[32,48,256]{2,1,0:T(8,128)} %get-tuple-element.12, f32[32,48,256]{2,1,0:T(8,128)} %get-tuple-element.11, f32[32,48,256]{2,1,0:T(8,128)} %get-tuple-element.10, f32[2,32,48,256]{3,2,1,0:T(8,128)} %param.12, f32[2,32,48,256]{3,2,1,0:T(8,128)} %param.11), kind=kLoop, calls=%fused_computation.116 | loop fusion | flops 1572864 | bytes 9437184 | tf_op jit(solution)/shard_map/stack | solution.py:162
  177.8 1.9 %pad_maximum_fusion.1 = f32[2,32,48,256]{3,2,1,0:T(8,128)} fusion(f32[1,32,48,256]{3,2,1,0:T(8,128)S(1)} %fusion.57, f32[1,32,48,256]{3,2,1,0:T(8,128)S(1)} %copy-done.27), kind=kLoop, calls=%fused_computation.1 | loop fusion | flops 786432 | bytes 6291456 | tf_op jit(solution)/shard_map/stack | solution.py:162
  (117 shorter events, 39.5 us)
Async XLA Ops:
  0.0 119.7 %copy-start = (f32[1,192,192]{2,1,0:T(8,128)S(1)}, f32[1,192,192]{2,1,0:T(8,128)}, u32[]{:S(2)}) copy-start(f32[1,192,192]{2,1,0:T(8,128)} %param.19) | copy-start | bytes 442372
  2.4 14.1 %copy-start.25 = (f32[32,48,256]{2,1,0:T(8,128)S(1)}, f32[32,48,256]{2,1,0:T(8,128)}, u32[]{:S(2)}) copy-start(f32[32,48,256]{2,1,0:T(8,128)} %param.14) | copy-start | bytes 4718596
  3.4 9.1 %collective-permute-start = (f32[4,1,48,256]{3,2,1,0:T(8,128)S(1)}, f32[4,1,48,256]{3,2,1,0:T(8,128)S(1)}, u32[]{:S(2)}, u32[]{:S(2)}) collective-permute-start(f32[4,1,48,256]{3,2,1,0:T(8,128)S(1)} %get-tuple-element.32), channel_id=1, source_target_pairs={{0,4},{4,8},{8,12},{12,16},{16,20},{20,24},{24,28},{1,5},{5,9},{9,... | collective-permute-start | bytes 589832 | tf_op jit(solution)/shard_map/ppermute | solution.py:16
  8.2 8.3 %collective-permute-start.1 = (f32[4,1,48,256]{3,2,1,0:T(8,128)S(1)}, f32[4,1,48,256]{3,2,1,0:T(8,128)S(1)}, u32[]{:S(2)}, u32[]{:S(2)}) collective-permute-start(f32[4,1,48,256]{3,2,1,0:T(8,128)S(1)} %get-tuple-element.33), channel_id=1, source_target_pairs={{4,0},{8,4},{12,8},{16,12},{20,16},{24,20},{28,24},{5,1},{9,5},{13... | collective-permute-start | bytes 589832 | tf_op jit(solution)/shard_map/ppermute | solution.py:17
  16.7 2.6 %collective-permute-start.2 = (f32[4,34,1,256]{3,2,1,0:T(1,128)S(1)}, f32[4,34,1,256]{3,2,1,0:T(1,128)S(1)}, u32[]{:S(2)}, u32[]{:S(2)}) collective-permute-start(f32[4,34,1,256]{3,2,1,0:T(1,128)S(1)} %get-tuple-element.30), channel_id=1, source_target_pairs={{0,1},{1,2},{2,3},{4,5},{5,6},{6,7},{8,9},{9,10},{10,11},{12,13},{... | collective-permute-start | bytes 417800 | tf_op jit(solution)/shard_map/ppermute | solution.py:16
  18.0 5.0 %collective-permute-start.3 = (f32[4,34,1,256]{3,2,1,0:T(1,128)S(1)}, f32[4,34,1,256]{3,2,1,0:T(1,128)S(1)}, u32[]{:S(2)}, u32[]{:S(2)}) collective-permute-start(f32[4,34,1,256]{3,2,1,0:T(1,128)S(1)} %get-tuple-element.31), channel_id=1, source_target_pairs={{1,0},{2,1},{3,2},{5,4},{6,5},{7,6},{9,8},{10,9},{11,10},{13,12},{... | collective-permute-start | bytes 417800 | tf_op jit(solution)/shard_map/ppermute | solution.py:17
  26.2 3.7 %copy-start.3 = (f32[4,34,50,256]{3,2,1,0:T(8,128)}, f32[4,34,50,256]{3,2,1,0:T(8,128)S(1)}, u32[]{:S(2)}) copy-start(f32[4,34,50,256]{3,2,1,0:T(8,128)S(1)} %pad_maximum_fusion) | copy-start | bytes 20889604
  33.8 32.1 %copy-start.4 = (f32[34,50,256]{2,1,0:T(8,128)}, f32[34,50,256]{2,1,0:T(8,128)S(1)}, u32[]{:S(2)}) copy-start(f32[34,50,256]{2,1,0:T(8,128)S(1)} %get-tuple-element.25) | copy-start | bytes 5222404
  33.8 33.6 %copy-start.1 = (f32[34,50,256]{2,1,0:T(8,128)}, f32[34,50,256]{2,1,0:T(8,128)S(1)}, u32[]{:S(2)}) copy-start(f32[34,50,256]{2,1,0:T(8,128)S(1)} %get-tuple-element.27) | copy-start | bytes 5222404
  33.9 33.5 %copy-start.8 = (f32[33,50,256]{2,1,0:T(8,128)}, f32[33,50,256]{2,1,0:T(8,128)S(1)}, u32[]{:S(2)}) copy-start(f32[33,50,256]{2,1,0:T(8,128)S(1)} %slice.280) | copy-start | bytes 5068804
  33.9 3.8 %copy-start.16 = (f32[2,32,48,256]{3,2,1,0:T(8,128)S(1)}, f32[2,32,48,256]{3,2,1,0:T(8,128)}, u32[]{:S(2)}) copy-start(f32[2,32,48,256]{3,2,1,0:T(8,128)} %param.12) | copy-start | bytes 9437188
  33.9 4.8 %copy-start.17 = (f32[2,32,48,256]{3,2,1,0:T(8,128)S(1)}, f32[2,32,48,256]{3,2,1,0:T(8,128)}, u32[]{:S(2)}) copy-start(f32[2,32,48,256]{3,2,1,0:T(8,128)} %param.11) | copy-start | bytes 9437188
  38.7 28.7 %copy-start.13 = (f32[34,50,256]{2,1,0:T(8,128)}, f32[34,50,256]{2,1,0:T(8,128)S(1)}, u32[]{:S(2)}) copy-start(f32[34,50,256]{2,1,0:T(8,128)S(1)} %pad_add_fusion) | copy-start | bytes 5222404
  43.3 24.1 %copy-start.19 = (f32[32,48,256]{2,1,0:T(8,128)}, f32[32,48,256]{2,1,0:T(8,128)S(1)}, u32[]{:S(2)}) copy-start(f32[32,48,256]{2,1,0:T(8,128)S(1)} %get-tuple-element.20) | copy-start | bytes 4718596
  43.3 24.1 %copy-start.21 = (f32[32,48,256]{2,1,0:T(8,128)}, f32[32,48,256]{2,1,0:T(8,128)S(1)}, u32[]{:S(2)}) copy-start(f32[32,48,256]{2,1,0:T(8,128)S(1)} %get-tuple-element.21) | copy-start | bytes 4718596
  43.3 6.2 %collective-permute-start.4 = (f32[1,48,256]{2,1,0:T(8,128)S(1)}, f32[1,48,256]{2,1,0:T(8,128)S(1)}, u32[]{:S(2)}, u32[]{:S(2)}) collective-permute-start(f32[1,48,256]{2,1,0:T(8,128)S(1)} %get-tuple-element.66), channel_id=1, source_target_pairs={{0,4},{4,8},{8,12},{12,16},{16,20},{20,24},{24,28},{1,5},{5,9},{9,... | collective-permute-start | bytes 147464 | tf_op jit(solution)/shard_map/ppermute | solution.py:16
  47.8 6.4 %collective-permute-start.5 = (f32[1,48,256]{2,1,0:T(8,128)S(1)}, f32[1,48,256]{2,1,0:T(8,128)S(1)}, u32[]{:S(2)}, u32[]{:S(2)}) collective-permute-start(f32[1,48,256]{2,1,0:T(8,128)S(1)} %get-tuple-element.67), channel_id=1, source_target_pairs={{4,0},{8,4},{12,8},{16,12},{20,16},{24,20},{28,24},{5,1},{9,5},{13... | collective-permute-start | bytes 147464 | tf_op jit(solution)/shard_map/ppermute | solution.py:17
  54.3 5.7 %collective-permute-start.6 = (f32[34,1,256]{2,1,0:T(1,128)S(1)}, f32[34,1,256]{2,1,0:T(1,128)S(1)}, u32[]{:S(2)}, u32[]{:S(2)}) collective-permute-start(f32[34,1,256]{2,1,0:T(1,128)S(1)} %get-tuple-element.60), channel_id=1, source_target_pairs={{0,1},{1,2},{2,3},{4,5},{5,6},{6,7},{8,9},{9,10},{10,11},{12,13},{... | collective-permute-start | bytes 104456 | tf_op jit(solution)/shard_map/ppermute | solution.py:16
  58.6 3.6 %collective-permute-start.7 = (f32[34,1,256]{2,1,0:T(1,128)S(1)}, f32[34,1,256]{2,1,0:T(1,128)S(1)}, u32[]{:S(2)}, u32[]{:S(2)}) collective-permute-start(f32[34,1,256]{2,1,0:T(1,128)S(1)} %get-tuple-element.61), channel_id=1, source_target_pairs={{1,0},{2,1},{3,2},{5,4},{6,5},{7,6},{9,8},{10,9},{11,10},{13,12},{... | collective-permute-start | bytes 104456 | tf_op jit(solution)/shard_map/ppermute | solution.py:17
  74.3 11.0 %copy-start.10 = (f32[32,48,256]{2,1,0:T(8,128)}, f32[32,48,256]{2,1,0:T(8,128)S(1)}, u32[]{:S(2)}) copy-start(f32[32,48,256]{2,1,0:T(8,128)S(1)} %fusion.29) | copy-start | bytes 4718596
  74.3 15.7 %copy-start.30 = (u32[32]{0:T(128)S(1)}, u32[32]{0:T(128)}, u32[]{:S(2)}) copy-start(u32[32]{0:T(128)} %constant.91) | copy-start | bytes 388
  74.4 6.7 %collective-permute-start.8 = (f32[1,48,256]{2,1,0:T(8,128)S(1)}, f32[1,48,256]{2,1,0:T(8,128)S(1)}, u32[]{:S(2)}, u32[]{:S(2)}) collective-permute-start(f32[1,48,256]{2,1,0:T(8,128)S(1)} %get-tuple-element.64), channel_id=1, source_target_pairs={{0,4},{4,8},{8,12},{12,16},{16,20},{20,24},{24,28},{1,5},{5,9},{9,... | collective-permute-start | bytes 147464 | tf_op jit(solution)/shard_map/ppermute | solution.py:16
  79.3 6.0 %collective-permute-start.9 = (f32[1,48,256]{2,1,0:T(8,128)S(1)}, f32[1,48,256]{2,1,0:T(8,128)S(1)}, u32[]{:S(2)}, u32[]{:S(2)}) collective-permute-start(f32[1,48,256]{2,1,0:T(8,128)S(1)} %get-tuple-element.65), channel_id=1, source_target_pairs={{4,0},{8,4},{12,8},{16,12},{20,16},{24,20},{28,24},{5,1},{9,5},{13... | collective-permute-start | bytes 147464 | tf_op jit(solution)/shard_map/ppermute | solution.py:17
  85.4 6.0 %collective-permute-start.10 = (f32[34,1,256]{2,1,0:T(1,128)S(1)}, f32[34,1,256]{2,1,0:T(1,128)S(1)}, u32[]{:S(2)}, u32[]{:S(2)}) collective-permute-start(f32[34,1,256]{2,1,0:T(1,128)S(1)} %get-tuple-element.57), channel_id=1, source_target_pairs={{0,1},{1,2},{2,3},{4,5},{5,6},{6,7},{8,9},{9,10},{10,11},{12,13},{... | collective-permute-start | bytes 104456 | tf_op jit(solution)/shard_map/ppermute | solution.py:16
  88.5 4.0 %collective-permute-start.11 = (f32[34,1,256]{2,1,0:T(1,128)S(1)}, f32[34,1,256]{2,1,0:T(1,128)S(1)}, u32[]{:S(2)}, u32[]{:S(2)}) collective-permute-start(f32[34,1,256]{2,1,0:T(1,128)S(1)} %get-tuple-element.58), channel_id=1, source_target_pairs={{1,0},{2,1},{3,2},{5,4},{6,5},{7,6},{9,8},{10,9},{11,10},{13,12},{... | collective-permute-start | bytes 104456 | tf_op jit(solution)/shard_map/ppermute | solution.py:17
  102.2 8.6 %copy-start.29 = (s32[4,6]{1,0:T(4,128)S(1)}, s32[4,6]{1,0:T(4,128)}, u32[]{:S(2)}) copy-start(s32[4,6]{1,0:T(4,128)} %param.18) | copy-start | bytes 292
  123.5 17.6 %copy-start.15 = (f32[32,48,256]{2,1,0:T(8,128)}, f32[32,48,256]{2,1,0:T(8,128)S(1)}, u32[]{:S(2)}) copy-start(f32[32,48,256]{2,1,0:T(8,128)S(1)} %multiply_add_fusion.1) | copy-start | bytes 4718596
  123.6 4.7 %collective-permute-start.12 = (f32[1,48,256]{2,1,0:T(8,128)S(1)}, f32[1,48,256]{2,1,0:T(8,128)S(1)}, u32[]{:S(2)}, u32[]{:S(2)}) collective-permute-start(f32[1,48,256]{2,1,0:T(8,128)S(1)} %get-tuple-element.62), channel_id=1, source_target_pairs={{0,4},{4,8},{8,12},{12,16},{16,20},{20,24},{24,28},{1,5},{5,9},{9,... | collective-permute-start | bytes 147464 | tf_op jit(solution)/shard_map/ppermute | solution.py:16
  126.5 6.0 %collective-permute-start.13 = (f32[1,48,256]{2,1,0:T(8,128)S(1)}, f32[1,48,256]{2,1,0:T(8,128)S(1)}, u32[]{:S(2)}, u32[]{:S(2)}) collective-permute-start(f32[1,48,256]{2,1,0:T(8,128)S(1)} %get-tuple-element.63), channel_id=1, source_target_pairs={{4,0},{8,4},{12,8},{16,12},{20,16},{24,20},{28,24},{5,1},{9,5},{13... | collective-permute-start | bytes 147464 | tf_op jit(solution)/shard_map/ppermute | solution.py:17
  132.5 2.6 %collective-permute-start.14 = (f32[34,1,256]{2,1,0:T(1,128)S(1)}, f32[34,1,256]{2,1,0:T(1,128)S(1)}, u32[]{:S(2)}, u32[]{:S(2)}) collective-permute-start(f32[34,1,256]{2,1,0:T(1,128)S(1)} %get-tuple-element.54), channel_id=1, source_target_pairs={{0,1},{1,2},{2,3},{4,5},{5,6},{6,7},{8,9},{9,10},{10,11},{12,13},{... | collective-permute-start | bytes 104456 | tf_op jit(solution)/shard_map/ppermute | solution.py:16
  133.8 5.0 %collective-permute-start.15 = (f32[34,1,256]{2,1,0:T(1,128)S(1)}, f32[34,1,256]{2,1,0:T(1,128)S(1)}, u32[]{:S(2)}, u32[]{:S(2)}) collective-permute-start(f32[34,1,256]{2,1,0:T(1,128)S(1)} %get-tuple-element.55), channel_id=1, source_target_pairs={{1,0},{2,1},{3,2},{5,4},{6,5},{7,6},{9,8},{10,9},{11,10},{13,12},{... | collective-permute-start | bytes 104456 | tf_op jit(solution)/shard_map/ppermute | solution.py:17
  173.6 4.2 %copy-start.27 = (f32[1,32,48,256]{3,2,1,0:T(8,128)S(1)}, f32[1,32,48,256]{3,2,1,0:T(8,128)}, u32[]{:S(2)}) copy-start(f32[1,32,48,256]{3,2,1,0:T(8,128)} %get-tuple-element.9) | copy-start | bytes 4718596
  (15 other events, 35.8 us)
where the time goes:
time: 183 us; the launch traced here: 180 us
  other arithmetic  77.3 us (42%)
  starting transfers between devices  37.8 us (21%)
  waiting for transfers between devices  32.3 us (18%)
  local copies, waits for them, and re-layouts  22.6 us (12%)
  blocking collectives  8.27 us (5%)
    ppermute x8, waiting for transfers between devices, extended(): after = lax.ppermute(leading, axis, down)  28.1 us
    ppermute x8, starting transfers between devices, extended(): before = lax.ppermute(last, axis, up)  27.3 us
    another operation x3, other arithmetic, shards(): return jnp.stack([out_p, out_s])  27.1 us
    concatenate x4, other arithmetic, extended(): array = jnp.concatenate([before, array, after], axis=dim)  12.7 us
    unnamed x65, local copies, waits for them, and re-layouts  12.3 us
    ppermute x8, starting transfers between devices, extended(): after = lax.ppermute(leading, axis, down)  10.5 us
    slice x11, local copies, waits for them, and re-layouts, forward(): moved = lax.slice_in_dim(field, 1, size, axis=along)  8.98 us
    unnamed x1, blocking collectives  8.27 us
  transfers between devices with their start and end apart: 16, of which 12 were waited for; matrix products, arithmetic and copies ran while one was open for 0% of the time, Pallas kernels for 0%

commit v1 on v0

v1 whole, which is shorter than its diff:
```python
import functools

import jax
import jax.numpy as jnp
from jax import lax
from jax.experimental import pallas as pl
from jax.experimental.pallas import tpu as pltpu
from jax.sharding import PartitionSpec as P

relaxation = 2.0 / 3.0
F32 = jnp.float32
WHOLE = pl.BlockSpec(memory_space=pltpu.VMEM)
SCALARS = pl.BlockSpec(memory_space=pltpu.SMEM)
G = 8
EDGE_FIELDS = 4
PLANES = 3


def params(mib):
    return pltpu.CompilerParams(vmem_limit_bytes=mib << 20)


def cost(flops, size):
    return pl.CostEstimate(flops=flops, bytes_accessed=size, transcendentals=0)


def y_next(v):
    return pltpu.roll(v, v.shape[0] - 1, 0)


def y_prev(v):
    return pltpu.roll(v, 1, 0)


def z_next(v):
    return pltpu.roll(v, v.shape[1] - 1, 1)


def z_prev(v):
    return pltpu.roll(v, 1, 1)


def quasi_impes(active, rp, rs, dpp, dss, dps, dsp):
    weight = dps / dss
    return active * (rp - weight * rs), active * (dpp - weight * dsp) + (1.0 - active)


def swap_pairs(axis, size):
    near = [(i, i ^ 1) for i in range(size) if i ^ 1 < size]
    far = [(i, ((i + 1) ^ 1) - 1) for i in range(size) if 0 <= ((i + 1) ^ 1) - 1 < size]
    return near, far


def swap(message, axis, size):
    near, far = swap_pairs(axis, size)
    return lax.ppermute(message[0], axis, near), lax.ppermute(message[1], axis, far)


def y_message_kernel(split_ref, *refs):
    low, high = refs[:8], refs[8:16]
    near_ref, far_ref = refs[16:]
    even = lax.rem(lax.axis_index("gy"), 2) == 0
    step = pl.program_id(0)

    def fields(group):
        res, diag, crs, mask, tx, ty, tz, ff = group
        active = mask[...].astype(F32)
        b, c = quasi_impes(active, res[0], res[1], diag[0], diag[1], crs[0], crs[1])
        return active, b, c, tx[...], ty[...], tz[...], ff[...]

    shape = low[3].shape
    s = lax.broadcasted_iota(jnp.int32, shape, 1)
    lane = lax.broadcasted_iota(jnp.int32, shape, 2)

    def turn(v, k):
        return jnp.stack([pltpu.roll(v[i], k, 0) for i in range(v.shape[0])])

    a, b, c, tx, ty, tz, ff = fields(high)
    lower = (lane < split_ref[step, split_ref.shape[1] - 1]).astype(F32)
    up = (
        jnp.where(s >= 5, a, jnp.where(s >= 2, turn(ty, 5), turn(tx, 2))),
        jnp.where(
            s >= 6,
            b,
            jnp.where(
                s >= 4,
                turn(c, 6),
                jnp.where(s >= 2, turn(tz, 4), jnp.where(s == 1, turn(ff, 2), lower)),
            ),
        ),
    )
    a, b, c, tx, ty, tz, ff = fields(low)
    lower = (lane < split_ref[step, 0]).astype(F32)
    down = (
        jnp.where(s < 3, a, jnp.where(s < 6, turn(ty, 3), turn(tx, 6))),
        jnp.where(
            s < 2,
            b,
            jnp.where(
                s < 4,
                turn(c, 2),
                jnp.where(s < 6, turn(tz, 4), jnp.where(s == 6, turn(ff, 6), lower)),
            ),
        ),
    )
    for k in range(2):
        near_ref[:, 8 * k : 8 * k + 8, :] = jnp.where(even, up[k], down[k])
        far_ref[:, 8 * k : 8 * k + 8, :] = jnp.where(even, down[k], up[k])


class Ghosts:
    def __init__(self, near_ref, far_ref):
        self.refs = near_ref, far_ref
        self.even = lax.rem(lax.axis_index("gy"), 2) == 0

    def tiles(self, x, k):
        near, far = (ref[x, 8 * k : 8 * k + 8, :] for ref in self.refs)
        return jnp.where(self.even, near, far), jnp.where(self.even, far, near)

    def pick(self, tiles, high_turn, low_turn, rings):
        high, low = tiles
        s = lax.broadcasted_iota(jnp.int32, high.shape, 0)
        high = pltpu.roll(high, high_turn, 0) if high_turn else high
        low = pltpu.roll(low, low_turn, 0) if low_turn else low
        return jnp.where(s < rings, high, jnp.where(s >= G - rings, low, 0.0))

    def first(self, x):
        t = self.tiles(x, 0)
        return self.pick(t, 0, 0, 3), self.pick(t, 2, 6, 2), self.pick(t, 5, 3, 3)

    def second(self, x):
        t = self.tiles(x, 1)
        c = jnp.maximum(self.pick(t, 6, 2, 2), 1.0)
        return self.pick(t, 0, 0, 2), c, self.pick(t, 4, 4, 2)

    def active(self, x):
        return self.pick(self.tiles(x, 0), 0, 0, 3)

    def frac_and_lower(self, x):
        t = self.tiles(x, 1)
        return self.pick(t, 2, 6, 1), self.pick(t, 1, 7, 1)


def join(own, ghost):
    return jnp.concatenate([own, ghost], axis=0)


class Rows:
    def __init__(self, res, diag, crs, mask, tx, ty, tz, ghosts):
        self.res, self.diag, self.crs, self.mask = res, diag, crs, mask
        self.tx, self.ty, self.tz, self.ghosts = tx, ty, tz, ghosts

    def active(self, x):
        return join(self.mask[x].astype(F32), self.ghosts.active(x))

    def trans_x(self, x):
        return join(self.tx[x], self.ghosts.first(x)[1])

    def all(self, x):
        ga, gtx, gty = self.ghosts.first(x)
        gb, gc, gtz = self.ghosts.second(x)
        own = self.mask[x].astype(F32)
        b, c = quasi_impes(
            own, self.res[0, x], self.res[1, x], self.diag[0, x], self.diag[1, x],
            self.crs[0, x], self.crs[1, x],
        )
        a = join(own, ga)
        lane = lax.broadcasted_iota(jnp.int32, a.shape, 1)
        ey = join(self.ty[x], gty) * a * y_next(a)
        ez = jnp.where(lane < a.shape[1] - 1, join(self.tz[x], gtz) * a * z_next(a), 0.0)
        return a, join(b, gb), join(c, gc), join(self.tx[x], gtx) * a, ey, ez


def in_plane_total(ey, ez):
    return ey + y_prev(ey) + ez + z_prev(ez)


def in_plane_sum(ey, ez, p):
    return ey * y_next(p) + y_prev(ey * p) + ez * z_next(p) + z_prev(ez * p)


def x_message_kernel(split_ref, res, diag, crs, mask, tx, ty, tz, ff, ynear, yfar, inv, near_ref, far_ref):
    even = lax.rem(lax.axis_index("gx"), 2) == 0
    j = lax.axis_index("gy")
    rows = Rows(res, diag, crs, mask, tx, ty, tz, Ghosts(ynear, yfar))
    last = mask.shape[0] - 1
    own = mask.shape[1]
    ext = own + G
    per_tile = 2 * split_ref.shape[0] * split_ref.shape[1]
    a1, b1, c1, t1, ey1, ez1 = rows.all(last - 1)
    a0, b0, c0, t0, ey0, ez0 = rows.all(last)
    inner = t1 * a0
    beyond = rows.active(last - 2) * rows.trans_x(last - 2) * a1
    first = relaxation * b1 / (c1 + inner + beyond + in_plane_total(ey1, ez1))
    up = (b0, c0 + inner + in_plane_total(ey0, ez0), t0, ey0, ez0, inner * first, ff[last])
    a0, b0, c0, t0, ey0, ez0 = rows.all(0)
    a1, b1, c1, t1, ey1, ez1 = rows.all(1)
    inner = t0 * a1
    beyond = t1 * rows.active(2)
    first = relaxation * b1 / (c1 + inner + beyond + in_plane_total(ey1, ez1))
    down = (b0, c0 + inner + in_plane_total(ey0, ez0), a0, ey0, ez0, inner * first, ff[0])
    at = 0
    for k in range(EDGE_FIELDS + PLANES):
        n = ext if k < EDGE_FIELDS else own
        near_ref[at : at + n, :] = jnp.where(even, up[k][:n], down[k][:n])
        far_ref[at : at + n, :] = jnp.where(even, down[k][:n], up[k][:n])
        at += n
    wide = near_ref.shape[1]
    unknowns = inv.shape[2]
    top = inv[0, pl.ds(pl.multiple_of(j * per_tile + per_tile - 16, 8), 16), :]
    bottom = inv[0, pl.ds(pl.multiple_of(j * per_tile, 8), 16), :]
    for k in range(0, unknowns, wide):
        n = min(wide, unknowns - k)
        if n < wide:
            near_ref[at : at + 16, :] = jnp.zeros((16, wide), F32)
            far_ref[at : at + 16, :] = jnp.zeros((16, wide), F32)
        near_ref[at : at + 16, :n] = jnp.where(even, top[:, k : k + n], bottom[:, k : k + n])
        far_ref[at : at + 16, :n] = jnp.where(even, bottom[:, k : k + n], top[:, k : k + n])
        at += 16
    lane = lax.broadcasted_iota(jnp.int32, (1, wide), 1)
    zero = jnp.zeros((8, wide), F32)
    near_ref[at : at + 8, :] = zero
    far_ref[at : at + 8, :] = zero
    for q in range(split_ref.shape[1]):
        top = (lane < split_ref[split_ref.shape[0] - 1, q]).astype(F32)
        bottom = (lane < split_ref[0, q]).astype(F32)
        near_ref[at + q : at + q + 1, :] = jnp.where(even, top, bottom)
        far_ref[at + q : at + q + 1, :] = jnp.where(even, bottom, top)


def x_message_rows(own, unknowns, wide):
    return EDGE_FIELDS * (own + G) + PLANES * own + 16 * pl.cdiv(unknowns, wide) + 8


class Planes:
    def __init__(self, near_ref, far_ref, own):
        self.refs, self.own = (near_ref, far_ref), own
        self.even = lax.rem(lax.axis_index("gx"), 2) == 0

    def rows(self, at, n, side):
        near, far = (ref[at : at + n, :] for ref in self.refs)
        return jnp.where(self.even, near, far) if side else jnp.where(self.even, far, near)

    def field(self, k, side):
        ext = self.own + G
        if k < EDGE_FIELDS:
            return self.rows(k * ext, ext, side)
        at = EDGE_FIELDS * ext + (k - EDGE_FIELDS) * self.own
        return self.rows(at, self.own, side)

    def extra(self, at, n, side):
        return self.rows(EDGE_FIELDS * (self.own + G) + PLANES * self.own + at, n, side)


def interior_kernel(res, diag, crs, mask, tx, ty, tz, ynear, yfar,
                    act, rhs, tot, gain, fx, fy, fz, one, two, acc):
    rows = Rows(res, diag, crs, mask, tx, ty, tz, Ghosts(ynear, yfar))
    n = mask.shape[0]
    own = mask.shape[1]

    act[0] = rows.active(0)

    def faces(x, before):
        a, b, c, t, ey, ez = rows.all(x)

        @pl.when(x < n - 1)
        def _():
            act[x + 1] = rows.active(x + 1)

        here = t * act[jnp.minimum(x + 1, n - 1)]
        ex = jnp.where(x < n - 1, here, 0.0)
        total = c + ex + before + in_plane_total(ey, ez)
        g = relaxation / total
        rhs[x] = b
        tot[x] = total
        gain[x] = g
        fx[x] = jnp.where(x < n - 1, here, t)
        fy[x] = ey
        fz[x] = ez
        one[x] = g * b
        return ex

    lax.fori_loop(0, n, faces, jnp.zeros(act.shape[1:], F32))

    def second(x, carry):
        p = one[x]
        s = fx[x] * one[x + 1] + fx[x - 1] * one[x - 1] + in_plane_sum(fy[x], fz[x], p)
        two[x] = gain[x] * ((2.0 - relaxation) * rhs[x] + s)
        return carry

    lax.fori_loop(2, n - 2, second, 0)

    def rest(x):
        p = two[x]
        s = fx[x] * two[x + 1] + fx[x - 1] * two[x - 1] + in_plane_sum(fy[x], fz[x], p)
        return (rhs[x] - tot[x] * p + s)[:own]

    for q in range(n // 8):
        acc[q] = lax.fori_loop(
            max(8 * q, 3), min(8 * q + 8, n - 3), lambda x, v: v + rest(x), jnp.zeros((own, mask.shape[2]), F32)
        )


def edge_kernel(split_ref, xnear, xfar, act, rhs, tot, fx, fy, fz, one, two, acc, sent, edge_two, edge_fx):
    n, ext = act.shape[0], act.shape[1]
    own = ext - G
    wide = act.shape[2]
    planes = Planes(xnear, xfar, own)
    none = jnp.zeros((G, wide), F32)

    class Far:
        def __init__(self, side):
            self.b = planes.field(0, side)
            self.total = jnp.maximum(planes.field(1, side), 1.0)
            self.key = planes.field(2, side)
            self.ey = planes.field(3, side)
            self.ez = join(planes.field(4, side), none)
            self.beyond = join(planes.field(5, side), none)

    low, high = Far(0), Far(1)
    ex = {-1: low.key * act[0], n - 1: fx[n - 1] * high.key}
    edge_fx[0] = ex[-1]
    edge_fx[1] = ex[n - 1]
    total = {
        -1: low.total + ex[-1],
        0: tot[0] + ex[-1],
        n - 1: tot[n - 1] + ex[n - 1],
        n: high.total + ex[n - 1],
    }
    b_of = lambda x: low.b if x == -1 else high.b if x == n else rhs[x]
    ey_of = lambda x: low.ey if x == -1 else high.ey if x == n else fy[x]
    ez_of = lambda x: low.ez if x == -1 else high.ez if x == n else fz[x]
    ex_of = lambda x: ex[x] if x in ex else fx[x]
    total_of = lambda x: total[x] if x in total else tot[x]
    gain = {x: relaxation / total[x] for x in total}
    first = {x: gain[x] * b_of(x) for x in total}
    first_of = lambda x: first[x] if x in first else one[x]

    def beside(x, field_of):
        s = in_plane_sum(ey_of(x), ez_of(x), field_of(x))
        s = s + (low.beyond if x == -1 else ex_of(x - 1) * field_of(x - 1))
        return s + (high.beyond if x == n else ex_of(x) * field_of(x + 1))

    second = {}
    for slot, x in enumerate((-1, 0, 1, n - 2, n - 1, n)):
        g = gain[x] if x in gain else relaxation / tot[x]
        second[x] = g * ((2.0 - relaxation) * b_of(x) + beside(x, first_of))
        edge_two[slot] = second[x]
    second_of = lambda x: second[x] if x in second else two[x]

    def rest(x):
        return (b_of(x) - total_of(x) * second_of(x) + beside(x, second_of))[:own]

    rows_b, cols_b = split_ref.shape
    lane = lax.broadcasted_iota(jnp.int32, (1, wide), 1)
    lower, upper = [], []
    for q in range(rows_b):
        field = acc[q]
        for x in (0, 1, 2, n - 3, n - 2, n - 1):
            if x // 8 == q:
                field = field + rest(x)
        for r in range(cols_b):
            column = jnp.sum(field[8 * r : 8 * r + 8], axis=0, keepdims=True)
            below = lane < split_ref[q, r]
            lower.append(jnp.where(below, column, 0.0))
            upper.append(jnp.where(below, 0.0, column))
    count = rows_b * cols_b
    low_sum = jnp.sum(jnp.concatenate(lower, axis=0), axis=1, keepdims=True)
    high_sum = jnp.sum(jnp.concatenate(upper, axis=0), axis=1, keepdims=True)
    span = sent.shape[1]
    place = lax.broadcasted_iota(jnp.int32, (count, span), 1) - 2 * count * lax.axis_index("gy")
    which = 2 * lax.broadcasted_iota(jnp.int32, (count, span), 0)
    laid = jnp.where(place == which, low_sum, jnp.where(place == which + 1, high_sum, 0.0))
    sent[...] = jnp.broadcast_to(jnp.sum(laid, axis=0, keepdims=True), sent.shape)


def final_kernel(tiles_y, split_ref, res, diag, crs, frac, inv, ynear, yfar, xnear, xfar,
                 act, fx, fy, fz, two, edge_two, edge_fx, got, out, coarse, three, held, sems):
    i, j = lax.axis_index("gx"), lax.axis_index("gy")
    n, ext = act.shape[0], act.shape[1]
    own = ext - G
    wide = act.shape[2]
    unknowns = inv.shape[2]
    rows_b, cols_b = split_ref.shape
    per_tile = 2 * rows_b * cols_b
    ghosts = Ghosts(ynear, yfar)
    planes = Planes(xnear, xfar, own)

    all_got = got[...]
    owner = lax.broadcasted_iota(jnp.int32, all_got.shape, 0)

    def row_of(tile_row):
        mine = (owner >= tile_row * tiles_y) & (owner < (tile_row + 1) * tiles_y)
        return jnp.sum(jnp.where(mine, all_got, 0.0), axis=0, keepdims=True)

    coarse_res = row_of(i)

    def solve(tile):
        start = pl.multiple_of(jnp.clip(tile, 0, tiles_y - 1) * per_tile, 8)
        block = inv[0, pl.ds(start, per_tile), :]
        e = jnp.sum(block * coarse_res[:, :unknowns], axis=1, keepdims=True)
        return jnp.broadcast_to(e, (per_tile, wide))

    lane = lax.broadcasted_iota(jnp.int32, (1, wide), 1)
    s = lax.broadcasted_iota(jnp.int32, (G, wide), 0)
    mine, before, after = solve(j), solve(j - 1), solve(j + 1)

    def one_of(e, k):
        return jnp.broadcast_to(e[k : k + 1], (8, wide))

    for q in range(rows_b):
        for r in range(cols_b):
            k = 2 * (q * cols_b + r)
            coarse[q + 1, 8 * r : 8 * r + 8, :] = jnp.where(
                lane < split_ref[q, r], one_of(mine, k), one_of(mine, k + 1)
            )
        below = ghosts.frac_and_lower(8 * q)[1] > 0.5
        k_high, k_low = 2 * q * cols_b, 2 * (q * cols_b + cols_b - 1)
        coarse[q + 1, own:ext, :] = jnp.where(
            s == 0,
            jnp.where(below, one_of(after, k_high), one_of(after, k_high + 1)),
            jnp.where(below, one_of(before, k_low), one_of(before, k_low + 1)),
        )
    blocks = pl.cdiv(unknowns, wide)
    for side, tile_row in ((0, i - 1), (1, i + 1)):
        other = row_of(tile_row)
        e = jnp.zeros((16, 1), F32)
        for k in range(blocks):
            w = min(wide, unknowns - k * wide)
            part = planes.extra(16 * k, 16, side)[:, :w] * other[:, k * wide : k * wide + w]
            e = e + jnp.sum(part, axis=1, keepdims=True)
        e = jnp.broadcast_to(e, (16, wide))
        below = planes.extra(16 * blocks, 8, side)
        skip = 16 - 2 * cols_b if side == 0 else 0
        at = 0 if side == 0 else rows_b + 1
        for r in range(cols_b):
            k = skip + 2 * r
            coarse[at, 8 * r : 8 * r + 8, :] = jnp.where(
                one_of(below, r) > 0.5, one_of(e, k), one_of(e, k + 1)
            )
        coarse[at, own:ext, :] = jnp.zeros((G, wide), F32)

    three[0] = edge_two[0] + coarse[0]
    three[1] = edge_two[1] + act[0] * coarse[1]
    three[2] = edge_two[2] + act[1] * coarse[1]
    three[n - 1] = edge_two[3] + act[n - 2] * coarse[rows_b]
    three[n] = edge_two[4] + act[n - 1] * coarse[rows_b]
    three[n + 1] = edge_two[5] + coarse[rows_b + 1]

    def correct(x, carry):
        three[x + 1] = two[x] + act[x] * coarse[x // 8 + 1]
        return carry

    lax.fori_loop(2, n - 2, correct, 0)

    def row(x, ex, ff_after, qx_before, sx_before):
        p = three[x + 1]
        f = frac[x]
        fe = join(f, ghosts.frac_and_lower(x)[0])
        ey, ez = fy[x], fz[x][:own]
        po = p[:own]
        qx = ex[:own] * (three[x + 2][:own] - po)
        qy = ey * (y_next(p) - p)
        qz = ez * (z_next(po) - po)
        sx = qx * (0.5 * (f + ff_after))
        sy = qy * (0.5 * (fe + y_next(fe)))
        sz = qz * (0.5 * (f + z_next(f)))
        flux_p = (qx_before - qx) + (y_prev(qy) - qy)[:own] + (z_prev(qz) - qz)
        flux_s = (sx_before - sx) + (y_prev(sy) - sy)[:own] + (z_prev(sz) - sz)
        dpp, dss, dps, dsp = diag[0, x], diag[1, x], crs[0, x], crs[1, x]
        up = res[0, x] - (dpp * po + flux_p)
        us = res[1, x] - (dsp * po + flux_s)
        inverse = 1.0 / (dpp * dss - dps * dsp)
        held[0, x] = po + (dss * up - dps * us) * inverse
        held[1, x] = (dpp * us - dsp * up) * inverse
        return qx, sx

    def copies(q):
        return [
            pltpu.make_async_copy(
                held.at[k, pl.ds(8 * q, 8)], out.at[k, pl.ds(8 * q, 8)], sems.at[k, q]
            )
            for k in range(2)
        ]

    qx = edge_fx[0][:own] * (three[1][:own] - three[0][:own])
    sx = qx * (0.5 * (planes.field(6, 0) + frac[0]))
    carry = qx, sx
    for q in range(n // 8):
        stop = min(8 * q + 8, n - 1)
        carry = lax.fori_loop(8 * q, stop, lambda x, v: row(x, fx[x], frac[x + 1], *v), carry)
        if stop == n - 1:
            row(n - 1, edge_fx[1], planes.field(6, 1), *carry)
        for copy in copies(q):
            copy.start()
    for q in range(n // 8):
        for copy in copies(q):
            copy.wait()


def shards(tiles_x, tiles_y, residual, accum_diag, accum_cross, mask, trans_x, trans_y, trans_z,
           frac_flow, split_layer, coarse_inverse):
    n, own, wide = mask.shape
    ext = own + G
    unknowns = coarse_inverse.shape[2]
    raw = (residual, accum_diag, accum_cross, mask, trans_x, trans_y, trans_z)
    columns = (*raw, frac_flow)
    groups = own // 8

    def group_spec(array, group):
        lead = array.shape[:-3]
        zero = (0,) * len(lead)
        return pl.BlockSpec((*lead, 8, 8, wide), lambda x: (*zero, x, group, 0))

    message = jax.ShapeDtypeStruct((n, 16, wide), F32)
    message_spec = pl.BlockSpec((8, 16, wide), lambda x: (x, 0, 0))
    y_messages = pl.pallas_call(
        y_message_kernel,
        grid=(n // 8,),
        in_specs=[SCALARS]
        + [group_spec(v, 0) for v in columns]
        + [group_spec(v, groups - 1) for v in columns],
        out_specs=[message_spec] * 2,
        out_shape=[message] * 2,
        compiler_params=params(16),
        name="y_messages",
    )(split_layer, *columns, *columns)
    ynear, yfar = swap(y_messages, "gy", tiles_y)

    x_message = jax.ShapeDtypeStruct((x_message_rows(own, unknowns, wide), wide), F32)
    x_messages = pl.pallas_call(
        x_message_kernel,
        in_specs=[SCALARS] + [WHOLE] * 11,
        out_specs=[WHOLE] * 2,
        out_shape=[x_message] * 2,
        compiler_params=params(16),
        name="x_messages",
    )(split_layer, *columns, ynear, yfar, coarse_inverse)
    xnear, xfar = swap(x_messages, "gx", tiles_x)

    field = jax.ShapeDtypeStruct((n, ext, wide), F32)
    act, rhs, tot, gain, fx, fy, fz, one, two, acc = pl.pallas_call(
        interior_kernel,
        in_specs=[WHOLE] * 9,
        out_specs=[WHOLE] * 10,
        out_shape=[field] * 9 + [jax.ShapeDtypeStruct((n // 8, own, wide), F32)],
        compiler_params=params(16),
        cost_estimate=cost(60_000_000, 30_000_000),
        name="interior",
    )(*raw, ynear, yfar)

    devices = tiles_x * tiles_y
    span = pl.cdiv(unknowns, 128) * 128
    sent, edge_two, edge_fx = pl.pallas_call(
        edge_kernel,
        in_specs=[SCALARS] + [WHOLE] * 11,
        out_specs=[WHOLE] * 3,
        out_shape=[
            jax.ShapeDtypeStruct((devices, span), F32),
            jax.ShapeDtypeStruct((6, ext, wide), F32),
            jax.ShapeDtypeStruct((2, ext, wide), F32),
        ],
        compiler_params=params(16),
        name="edges",
    )(split_layer, xnear, xfar, act, rhs, tot, fx, fy, fz, one, two, acc)
    got = lax.all_to_all(sent, ("gx", "gy"), 0, 0, tiled=True)

    return pl.pallas_call(
        functools.partial(final_kernel, tiles_y),
        in_specs=[SCALARS] + [WHOLE] * 17,
        out_specs=pl.BlockSpec(memory_space=pl.ANY),
        out_shape=jax.ShapeDtypeStruct((2, n, own, wide), F32),
        scratch_shapes=[
            pltpu.VMEM((n // 8 + 2, ext, wide), F32),
            pltpu.VMEM((n + 2, ext, wide), F32),
            pltpu.VMEM((2, n, own, wide), F32),
            pltpu.SemaphoreType.DMA((2, n // 8)),
        ],
        compiler_params=params(16),
        name="final",
    )(split_layer, residual, accum_diag, accum_cross, frac_flow, coarse_inverse, ynear, yfar, xnear, xfar,
      act, fx, fy, fz, two, edge_two, edge_fx, got)


def solution(mesh):
    placed = (
        P(None, "gx", "gy", None),
        P(None, "gx", "gy", None),
        P(None, "gx", "gy", None),
        P("gx", "gy", None),
        P("gx", "gy", None),
        P("gx", "gy", None),
        P("gx", "gy", None),
        P("gx", "gy", None),
        P("gx", "gy"),
        P("gx", None, None),
    )
    return jax.shard_map(
        functools.partial(shards, mesh.shape["gx"], mesh.shape["gy"]),
        mesh=mesh,
        in_specs=placed,
        out_specs=P(None, "gx", "gy", None),
        check_vma=False,
    )
```

time: 183 us -> 68.9 us (0.38); the launches traced: 180 us -> 68.5 us
  other arithmetic: 77.3 us -> 0 us
  starting transfers between devices: 37.8 us -> 4.95 us
  waiting for transfers between devices: 32.3 us -> 0.7 us
  Pallas kernels: 0 us -> 25.6 us
  blocking collectives: 8.27 us -> 23.7 us
  local copies, waits for them, and re-layouts: 22.6 us -> 13.5 us
    ppermute x16 -> x4, starting transfers between devices: 37.8 us -> 4.95 us  [the longest x2 3.45 us: swap(): lax.ppermute(message[0], axis, near)]
    ppermute x16 -> x4, waiting for transfers between devices: 32.3 us -> 0.7 us  [the longest x2 0.69 us: swap(): lax.ppermute(message[0], axis, near)]
    another operation x5 -> x0, other arithmetic: 28.8 us -> none  [the longest x3 27.1 us: shards(): return jnp.stack([out_p, out_s])]
    pallas_call x0 -> x5, Pallas kernels: none -> 25.6 us  [the longest x1 13.2 us: shards(): pl.pallas_call(interior_kernel, in_specs=[WHOLE] * 9, out_specs=[WHOLE] *...]
    all_to_all x0 -> x1, blocking collectives: none -> 23.7 us  [shards(): got = lax.all_to_all(sent, ('gx', 'gy'), 0, 0, tiled=True)]
    concatenate x4 -> x0, other arithmetic: 12.7 us -> none  [extended(): array = jnp.concatenate([before, array, after], axis=dim)]
    add x5 -> x0, other arithmetic: 12 us -> none  [the longest x1 6.91 us: shards(): sweep_one + relaxation * (pressure_rhs - schur_diag * sweep_one - inner(n...]
    slice x17 -> x0, local copies, waits for them, and re-layouts: 9.4 us -> none  [the longest x11 8.98 us: forward(): moved = lax.slice_in_dim(field, 1, size, axis=along)]
  transfers between devices with their start and end apart: 16 -> 4, of which waited for: 12 -> 1; matrix products, arithmetic and copies ran while one was open for 0% -> 0% of each run, Pallas kernels for 0% -> 19%
where the time goes in v1:
time: 68.9 us; the launch traced here: 68.5 us
  Pallas kernels  25.6 us (37%)
  blocking collectives  23.7 us (34%)
  local copies, waits for them, and re-layouts  13.5 us (20%)
  starting transfers between devices  4.95 us (7%)
  waiting for transfers between devices  0.7 us (1%)
    all_to_all x1, blocking collectives, shards(): got = lax.all_to_all(sent, ('gx', 'gy'), 0, 0, tiled=True)  23.7 us
    unnamed x37, local copies, waits for them, and re-layouts  13.4 us
    pallas_call x1, Pallas kernels, shards(): pl.pallas_call(interior_kernel, in_specs=[WHOLE] * 9, out_specs=[WHOLE] *...  13.2 us
    pallas_call x1, Pallas kernels, shards(): pl.pallas_call(functools.partial(final_kernel, tiles_y), in_specs=[SCALAR...  8.43 us
    ppermute x2, starting transfers between devices, swap(): lax.ppermute(message[0], axis, near)  3.45 us
    pallas_call x1, Pallas kernels, shards(): pl.pallas_call(y_message_kernel, grid=(n // 8,), in_specs=[SCALARS] + [gr...  1.62 us
    ppermute x2, starting transfers between devices, swap(): lax.ppermute(message[1], axis, far)  1.5 us
    pallas_call x1, Pallas kernels, shards(): pl.pallas_call(edge_kernel, in_specs=[SCALARS] + [WHOLE] * 11, out_specs=...  1.45 us
  transfers between devices with their start and end apart: 4, of which 1 were waited for; matrix products, arithmetic and copies ran while one was open for 0% of the time, Pallas kernels for 19%

profile of v1, /device:TPU:0, one launch (start us, length us, event | category | flops | bytes accessed | tf_op | source)
XLA Modules:
  0.0 68.5 jit_solution(17111097779888764199)
XLA Ops:
  0.0 1.9 %copy-done = f32[2,32,48,256]{3,2,1,0:T(8,128)S(1)} copy-done((f32[2,32,48,256]{3,2,1,0:T(8,128)S(1)}, f32[2,32,48,256]{3,2,1,0:T(8,128)}, u32[]{:S(2)}) %copy-start) | copy-done | bytes 3145752
  1.9 1.9 %copy-done.2 = f32[2,32,48,256]{3,2,1,0:T(8,128)S(1)} copy-done((f32[2,32,48,256]{3,2,1,0:T(8,128)S(1)}, f32[2,32,48,256]{3,2,1,0:T(8,128)}, u32[]{:S(2)}) %copy-start.2) | copy-done | bytes 3145752
  3.8 1.9 %copy-done.4 = f32[2,32,48,256]{3,2,1,0:T(8,128)S(1)} copy-done((f32[2,32,48,256]{3,2,1,0:T(8,128)S(1)}, f32[2,32,48,256]{3,2,1,0:T(8,128)}, u32[]{:S(2)}) %copy-start.4) | copy-done | bytes 3145752
  5.7 1.4 %copy-done.6 = s32[32,48,256]{2,1,0:T(8,128)S(1)} copy-done((s32[32,48,256]{2,1,0:T(8,128)S(1)}, s32[32,48,256]{2,1,0:T(8,128)}, u32[]{:S(2)}) %copy-start.6) | copy-done | bytes 1572888
  7.1 1.4 %copy-done.8 = f32[32,48,256]{2,1,0:T(8,128)S(1)} copy-done((f32[32,48,256]{2,1,0:T(8,128)S(1)}, f32[32,48,256]{2,1,0:T(8,128)}, u32[]{:S(2)}) %copy-start.8) | copy-done | bytes 1572888
  8.5 1.4 %copy-done.10 = f32[32,48,256]{2,1,0:T(8,128)S(1)} copy-done((f32[32,48,256]{2,1,0:T(8,128)S(1)}, f32[32,48,256]{2,1,0:T(8,128)}, u32[]{:S(2)}) %copy-start.10) | copy-done | bytes 1572888
  9.9 1.4 %copy-done.12 = f32[32,48,256]{2,1,0:T(8,128)S(1)} copy-done((f32[32,48,256]{2,1,0:T(8,128)S(1)}, f32[32,48,256]{2,1,0:T(8,128)}, u32[]{:S(2)}) %copy-start.12) | copy-done | bytes 1572888
  11.3 1.4 %copy-done.14 = f32[32,48,256]{2,1,0:T(8,128)S(1)} copy-done((f32[32,48,256]{2,1,0:T(8,128)S(1)}, f32[32,48,256]{2,1,0:T(8,128)}, u32[]{:S(2)}) %copy-start.14) | copy-done | bytes 1572888
  12.7 0.7 copy-done.17
  13.4 1.6 %y_messages.1 = (f32[32,16,256]{2,1,0:T(8,128)S(1)}, f32[32,16,256]{2,1,0:T(8,128)S(1)}) custom-call(s32[4,6]{1,0:T(4,128)S(1)} %copy-done.17, f32[2,32,48,256]{3,2,1,0:T(8,128)S(1)} %copy-done, f32[2,32,48,256]{3,2,1,0:T(8,128)S(1)} %copy-done.2, f32[2,32,48,256]{3,2,1,0:T(8,128)S(1)} %copy-done.4, s32[32,48,256]{2,1,0:T(8,128)S(1)} %copy-done.6, ...), custom_call_target="tpu_custom_call" | custom-call | tf_op jit(solution)/shard_map/y_messages/pallas_call | solution.py:517
  15.0 0.5 collective-permute-start
  15.6 0.8 %collective-permute-start.1 = (f32[32,16,256]{2,1,0:T(8,128)S(1)}, f32[32,16,256]{2,1,0:T(8,128)S(1)}, u32[]{:S(2)}, u32[]{:S(2)}) collective-permute-start(f32[32,16,256]{2,1,0:T(8,128)S(1)} %get-tuple-element.22), channel_id=1, source_target_pairs={{1,2},{2,1},{5,6},{6,5},{9,10},{10,9},{13,14},{14,13},{17,18},{18,... | collective-permute-start | bytes 1572872 | tf_op jit(solution)/shard_map/ppermute | solution.py:56
  16.4 0.7 %collective-permute-done.ynear = f32[32,16,256]{2,1,0:T(8,128)S(1)} collective-permute-done((f32[32,16,256]{2,1,0:T(8,128)S(1)}, f32[32,16,256]{2,1,0:T(8,128)S(1)}, u32[]{:S(2)}, u32[]{:S(2)}) %collective-permute-start) | collective-permute-done | bytes 524320 | tf_op jit(solution)/shard_map/ppermute | solution.py:56
  17.1 0.0 collective-permute-done.1.yfar
  17.1 0.0 copy-done.16
  17.1 0.0 copy-start.5
  17.1 0.9 %x_messages.1 = (f32[392,256]{1,0:T(8,128)S(1)}, f32[392,256]{1,0:T(8,128)S(1)}) custom-call(s32[4,6]{1,0:T(4,128)S(1)} %copy-done.17, f32[2,32,48,256]{3,2,1,0:T(8,128)S(1)} %copy-done, f32[2,32,48,256]{3,2,1,0:T(8,128)S(1)} %copy-done.2, f32[2,32,48,256]{3,2,1,0:T(8,128)S(1)} %copy-done.4, s32[32,48,256]{2,1,0:T(8,128)S(1)} %copy-done.6, ...), custom_call_target="tpu_custom_call" | custom-call | tf_op jit(solution)/shard_map/x_messages/pallas_call | solution.py:531
  18.0 2.9 %collective-permute-start.2 = (f32[392,256]{1,0:T(8,128)S(1)}, f32[392,256]{1,0:T(8,128)S(1)}, u32[]{:S(2)}, u32[]{:S(2)}) collective-permute-start(f32[392,256]{1,0:T(8,128)S(1)} %get-tuple-element.23), channel_id=1, source_target_pairs={{0,4},{4,0},{8,12},{12,8},{16,20},{20,16},{24,28},{28,24},{1,5},{5... | collective-permute-start | bytes 1204232 | tf_op jit(solution)/shard_map/ppermute | solution.py:56
  21.0 0.7 collective-permute-start.3
  21.6 0.0 copy-done.7
  21.6 0.0 copy-done.9
  21.7 0.0 copy-done.11
  21.7 0.0 copy-done.13
  21.7 0.0 copy-done.1
  21.7 0.0 copy-done.3
  21.7 0.0 copy-done.5
  21.7 13.2 %interior.1 = (f32[32,56,256]{2,1,0:T(8,128)S(1)}, f32[32,56,256]{2,1,0:T(8,128)S(1)}, f32[32,56,256]{2,1,0:T(8,128)S(1)}, f32[32,56,256]{2,1,0:T(8,128)}, f32[3...) custom-call(f32[2,32,48,256]{3,2,1,0:T(8,128)S(1)} %copy-done.1, ...), custom_call_target="tpu_custom_call" | custom-call | flops 60000000 | bytes 30000000 | tf_op jit(solution)/shard_map/interior/pallas_call | solution.py:542
  34.9 0.0 collective-permute-done.2.xnear
  34.9 0.0 collective-permute-done.3.xfar
  34.9 1.4 %edges.1 = (f32[32,256]{1,0:T(8,128)S(1)}, f32[6,56,256]{2,1,0:T(8,128)S(1)}, f32[2,56,256]{2,1,0:T(8,128)S(1)}) custom-call(s32[4,6]{1,0:T(4,128)S(1)} %copy-done.17, f32[392,256]{1,0:T(8,128)S(1)} %collective-permute-done.2.xnear, f32[392,256]{1,0:T(8,128)S(1)} %collective-permute-done.3.xfar, f32[32,56,256]{2,1,0:T(8,128)S(1)} %get-tuple-element.25.act, ...), custom_call_target="tpu_custom_call" | custom-call | tf_op jit(solution)/shard_map/edges/pallas_call | solution.py:554
  36.4 23.7 %all_to_all.11 = f32[32,1,256]{2,1,0:T(1,128)S(1)} all-to-all(f32[32,1,256]{2,1,0:T(1,128)S(1)} %copy.11), channel_id=1, replica_groups=mesh['gx'=8,'gy'=4] {'gx','gy'}, dimensions={0} | all-to-all | bytes 65536 | tf_op jit(solution)/shard_map/all_to_all | solution.py:566
  60.1 8.4 %final.1 = f32[2,32,48,256]{3,2,1,0:T(8,128)} custom-call(s32[4,6]{1,0:T(4,128)S(1)} %copy-done.17, f32[2,32,48,256]{3,2,1,0:T(8,128)S(1)} %copy-done.1, f32[2,32,48,256]{3,2,1,0:T(8,128)S(1)} %copy-done.3, f32[2,32,48,256]{3,2,1,0:T(8,128)S(1)} %copy-done.5, f32[32,48,256]{2,1,0:T(8,128)S(1)} %copy-done.15, f32[1,192,192]{2,1,0:T(8,128)S(1)} %copy-done.16, ...), custom_call_target="tpu_custom_call" | custom-call | tf_op jit(solution)/shard_map/final/pallas_call | solution.py:568
  (20 shorter events, 0.1 us)
Async XLA Ops:
  0.0 1.9 %copy-start = (f32[2,32,48,256]{3,2,1,0:T(8,128)S(1)}, f32[2,32,48,256]{3,2,1,0:T(8,128)}, u32[]{:S(2)}) copy-start(f32[2,32,48,256]{3,2,1,0:T(8,128)} %res.5) | copy-start | bytes 9437188
  1.9 1.9 %copy-start.2 = (f32[2,32,48,256]{3,2,1,0:T(8,128)S(1)}, f32[2,32,48,256]{3,2,1,0:T(8,128)}, u32[]{:S(2)}) copy-start(f32[2,32,48,256]{3,2,1,0:T(8,128)} %diag.5) | copy-start | bytes 9437188
  3.8 1.9 %copy-start.4 = (f32[2,32,48,256]{3,2,1,0:T(8,128)S(1)}, f32[2,32,48,256]{3,2,1,0:T(8,128)}, u32[]{:S(2)}) copy-start(f32[2,32,48,256]{3,2,1,0:T(8,128)} %crs.5) | copy-start | bytes 9437188
  5.7 1.4 %copy-start.6 = (s32[32,48,256]{2,1,0:T(8,128)S(1)}, s32[32,48,256]{2,1,0:T(8,128)}, u32[]{:S(2)}) copy-start(s32[32,48,256]{2,1,0:T(8,128)} %mask.3) | copy-start | bytes 4718596
  7.1 1.4 %copy-start.8 = (f32[32,48,256]{2,1,0:T(8,128)S(1)}, f32[32,48,256]{2,1,0:T(8,128)}, u32[]{:S(2)}) copy-start(f32[32,48,256]{2,1,0:T(8,128)} %tx.3) | copy-start | bytes 4718596
  8.5 1.4 %copy-start.10 = (f32[32,48,256]{2,1,0:T(8,128)S(1)}, f32[32,48,256]{2,1,0:T(8,128)}, u32[]{:S(2)}) copy-start(f32[32,48,256]{2,1,0:T(8,128)} %ty.3) | copy-start | bytes 4718596
  9.9 1.4 %copy-start.12 = (f32[32,48,256]{2,1,0:T(8,128)S(1)}, f32[32,48,256]{2,1,0:T(8,128)}, u32[]{:S(2)}) copy-start(f32[32,48,256]{2,1,0:T(8,128)} %tz.3) | copy-start | bytes 4718596
  11.3 1.4 %copy-start.14 = (f32[32,48,256]{2,1,0:T(8,128)S(1)}, f32[32,48,256]{2,1,0:T(8,128)}, u32[]{:S(2)}) copy-start(f32[32,48,256]{2,1,0:T(8,128)} %frac.1) | copy-start | bytes 4718596
  12.7 0.7 copy-start.17
  13.4 3.7 %copy-start.16 = (f32[1,192,192]{2,1,0:T(8,128)S(1)}, f32[1,192,192]{2,1,0:T(8,128)}, u32[]{:S(2)}) copy-start(f32[1,192,192]{2,1,0:T(8,128)} %inv.3) | copy-start | bytes 442372
  15.0 2.1 %collective-permute-start = (f32[32,16,256]{2,1,0:T(8,128)S(1)}, f32[32,16,256]{2,1,0:T(8,128)S(1)}, u32[]{:S(2)}, u32[]{:S(2)}) collective-permute-start(f32[32,16,256]{2,1,0:T(8,128)S(1)} %get-tuple-element.21), channel_id=1, source_target_pairs={{0,1},{1,0},{2,3},{3,2},{4,5},{5,4},{6,7},{7,6},{8,9},{9,8},{10,11... | collective-permute-start | bytes 1572872 | tf_op jit(solution)/shard_map/ppermute | solution.py:56
  15.5 6.1 %copy-start.7 = (s32[32,48,256]{2,1,0:T(8,128)S(1)}, s32[32,48,256]{2,1,0:T(8,128)}, u32[]{:S(2)}) copy-start(s32[32,48,256]{2,1,0:T(8,128)} %mask.3) | copy-start | bytes 4718596
  15.5 6.1 %copy-start.9 = (f32[32,48,256]{2,1,0:T(8,128)S(1)}, f32[32,48,256]{2,1,0:T(8,128)}, u32[]{:S(2)}) copy-start(f32[32,48,256]{2,1,0:T(8,128)} %tx.3) | copy-start | bytes 4718596
  15.5 6.1 %copy-start.11 = (f32[32,48,256]{2,1,0:T(8,128)S(1)}, f32[32,48,256]{2,1,0:T(8,128)}, u32[]{:S(2)}) copy-start(f32[32,48,256]{2,1,0:T(8,128)} %ty.3) | copy-start | bytes 4718596
  15.6 6.1 %copy-start.13 = (f32[32,48,256]{2,1,0:T(8,128)S(1)}, f32[32,48,256]{2,1,0:T(8,128)}, u32[]{:S(2)}) copy-start(f32[32,48,256]{2,1,0:T(8,128)} %tz.3) | copy-start | bytes 4718596
  15.6 1.5 %collective-permute-start.1 = (f32[32,16,256]{2,1,0:T(8,128)S(1)}, f32[32,16,256]{2,1,0:T(8,128)S(1)}, u32[]{:S(2)}, u32[]{:S(2)}) collective-permute-start(f32[32,16,256]{2,1,0:T(8,128)S(1)} %get-tuple-element.22), channel_id=1, source_target_pairs={{1,2},{2,1},{5,6},{6,5},{9,10},{10,9},{13,14},{14,13},{17,18},{18,... | collective-permute-start | bytes 1572872 | tf_op jit(solution)/shard_map/ppermute | solution.py:56
  17.1 4.6 %copy-start.1 = (f32[2,32,48,256]{3,2,1,0:T(8,128)S(1)}, f32[2,32,48,256]{3,2,1,0:T(8,128)}, u32[]{:S(2)}) copy-start(f32[2,32,48,256]{3,2,1,0:T(8,128)} %res.5) | copy-start | bytes 9437188
  17.1 4.6 %copy-start.3 = (f32[2,32,48,256]{3,2,1,0:T(8,128)S(1)}, f32[2,32,48,256]{3,2,1,0:T(8,128)}, u32[]{:S(2)}) copy-start(f32[2,32,48,256]{3,2,1,0:T(8,128)} %diag.5) | copy-start | bytes 9437188
  17.1 4.6 %copy-start.5 = (f32[2,32,48,256]{3,2,1,0:T(8,128)S(1)}, f32[2,32,48,256]{3,2,1,0:T(8,128)}, u32[]{:S(2)}) copy-start(f32[2,32,48,256]{3,2,1,0:T(8,128)} %crs.5) | copy-start | bytes 9437188
  18.0 16.9 %collective-permute-start.2 = (f32[392,256]{1,0:T(8,128)S(1)}, f32[392,256]{1,0:T(8,128)S(1)}, u32[]{:S(2)}, u32[]{:S(2)}) collective-permute-start(f32[392,256]{1,0:T(8,128)S(1)} %get-tuple-element.23), channel_id=1, source_target_pairs={{0,4},{4,0},{8,12},{12,8},{16,20},{20,16},{24,28},{28,24},{1,5},{5... | collective-permute-start | bytes 1204232 | tf_op jit(solution)/shard_map/ppermute | solution.py:56
  21.0 13.9 %collective-permute-start.3 = (f32[392,256]{1,0:T(8,128)S(1)}, f32[392,256]{1,0:T(8,128)S(1)}, u32[]{:S(2)}, u32[]{:S(2)}) collective-permute-start(f32[392,256]{1,0:T(8,128)S(1)} %get-tuple-element.24), channel_id=1, source_target_pairs={{4,8},{8,4},{12,16},{16,12},{20,24},{24,20},{5,9},{9,5},{13,17},{1... | collective-permute-start | bytes 1204232 | tf_op jit(solution)/shard_map/ppermute | solution.py:56
  34.9 25.2 %copy-start.15 = (f32[32,48,256]{2,1,0:T(8,128)S(1)}, f32[32,48,256]{2,1,0:T(8,128)}, u32[]{:S(2)}) copy-start(f32[32,48,256]{2,1,0:T(8,128)} %frac.1) | copy-start | bytes 4718596

commit v2 on v1

--- a/solution.py
+++ b/solution.py
@@ -512,6 +512,7 @@
         zero = (0,) * len(lead)
         return pl.BlockSpec((*lead, 8, 8, wide), lambda x: (*zero, x, group, 0))
 
+    far_columns = [pltpu.with_memory_space_constraint(v, pltpu.HBM) for v in columns]
     message = jax.ShapeDtypeStruct((n, 16, wide), F32)
     message_spec = pl.BlockSpec((8, 16, wide), lambda x: (x, 0, 0))
     y_messages = pl.pallas_call(
@@ -524,7 +525,7 @@
         out_shape=[message] * 2,
         compiler_params=params(16),
         name="y_messages",
-    )(split_layer, *columns, *columns)
+    )(split_layer, *far_columns, *far_columns)
     ynear, yfar = swap(y_messages, "gy", tiles_y)
 
     x_message = jax.ShapeDtypeStruct((x_message_rows(own, unknowns, wide), wide), F32)

time: 68.9 us -> 59.2 us (0.86)
  local copies, waits for them, and re-layouts: 13.5 us -> 1.34 us
  Pallas kernels: 25.6 us -> 28.8 us
  blocking collectives: 23.7 us -> 23 us
    unnamed x37 -> x21, local copies, waits for them, and re-layouts: 13.4 us -> 1.31 us
    pallas_call x1, Pallas kernels: 1.62 us -> 4.64 us  [shards(): pl.pallas_call(y_message_kernel, grid=(n // 8,), in_specs=[SCALARS] + [gr...]
  transfers between devices with their start and end apart: 4 -> 4, of which waited for: 1 -> 1; matrix products, arithmetic and copies ran while one was open for 0% -> 0% of each run, Pallas kernels for 19% -> 23%
where the time goes in v2:
time: 59.2 us; the launch traced here: 59 us
  Pallas kernels  28.8 us (49%)
  blocking collectives  23 us (39%)
  starting transfers between devices  5.04 us (9%)
  local copies, waits for them, and re-layouts  1.34 us (2%)
  waiting for transfers between devices  0.72 us (1%)
    all_to_all x1, blocking collectives, shards(): got = lax.all_to_all(sent, ('gx', 'gy'), 0, 0, tiled=True)  23 us
    pallas_call x1, Pallas kernels, shards(): pl.pallas_call(interior_kernel, in_specs=[WHOLE] * 9, out_specs=[WHOLE] *...  13.4 us
    pallas_call x1, Pallas kernels, shards(): pl.pallas_call(functools.partial(final_kernel, tiles_y), in_specs=[SCALAR...  8.43 us
    pallas_call x1, Pallas kernels, shards(): pl.pallas_call(y_message_kernel, grid=(n // 8,), in_specs=[SCALARS] + [gr...  4.64 us
    ppermute x2, starting transfers between devices, swap(): lax.ppermute(message[0], axis, near)  3.55 us
    ppermute x2, starting transfers between devices, swap(): lax.ppermute(message[1], axis, far)  1.49 us
    pallas_call x1, Pallas kernels, shards(): pl.pallas_call(edge_kernel, in_specs=[SCALARS] + [WHOLE] * 11, out_specs=...  1.45 us
    unnamed x21, local copies, waits for them, and re-layouts  1.31 us
  transfers between devices with their start and end apart: 4, of which 1 were waited for; matrix products, arithmetic and copies ran while one was open for 0% of the time, Pallas kernels for 23%

profile of v2, /device:TPU:0, one launch (start us, length us, event | category | flops | bytes accessed | tf_op | source)
XLA Modules:
  0.0 59.0 jit_solution(16208027114424780389)
XLA Ops:
  0.0 0.0 copy-start.3
  0.0 0.0 copy-start.4
  0.0 0.0 copy-start.5
  0.0 0.0 copy-start.6
  0.0 0.0 copy-start.7
  0.0 0.0 copy-start.9
  0.0 0.8 %copy-done.9 = s32[4,6]{1,0:T(4,128)S(1)} copy-done((s32[4,6]{1,0:T(4,128)S(1)}, s32[4,6]{1,0:T(4,128)}, u32[]{:S(2)}) %copy-start.9) | copy-done | bytes 120
  0.8 0.0 copy-start
  0.9 0.0 copy-start.2
  0.9 4.6 %y_messages.1 = (f32[32,16,256]{2,1,0:T(8,128)S(1)}, f32[32,16,256]{2,1,0:T(8,128)S(1)}) custom-call(s32[4,6]{1,0:T(4,128)S(1)} %copy-done.9, f32[2,32,48,256]{3,2,1,0:T(8,128)} %res.5, f32[2,32,48,256]{3,2,1,0:T(8,128)} %diag.5, f32[2,32,48,256]{3,2,1,0:T(8,128)} %crs.5, s32[32,48,256]{2,1,0:T(8,128)} %mask.3, f32[32,48,256]{2,1,0:T(8,128)} %tx.3, ...), custom_call_target="tpu_custom_call" | custom-call | tf_op jit(solution)/shard_map/y_messages/pallas_call | solution.py:518
  5.5 0.5 collective-permute-start
  6.1 0.8 %collective-permute-start.1 = (f32[32,16,256]{2,1,0:T(8,128)S(1)}, f32[32,16,256]{2,1,0:T(8,128)S(1)}, u32[]{:S(2)}, u32[]{:S(2)}) collective-permute-start(f32[32,16,256]{2,1,0:T(8,128)S(1)} %get-tuple-element.22), channel_id=1, source_target_pairs={{1,2},{2,1},{5,6},{6,5},{9,10},{10,9},{13,14},{14,13},{17,18},{18,... | collective-permute-start | bytes 1572872 | tf_op jit(solution)/shard_map/ppermute | solution.py:56
  6.9 0.7 %collective-permute-done.ynear = f32[32,16,256]{2,1,0:T(8,128)S(1)} collective-permute-done((f32[32,16,256]{2,1,0:T(8,128)S(1)}, f32[32,16,256]{2,1,0:T(8,128)S(1)}, u32[]{:S(2)}, u32[]{:S(2)}) %collective-permute-start) | collective-permute-done | bytes 524320 | tf_op jit(solution)/shard_map/ppermute | solution.py:56
  7.6 0.0 collective-permute-done.1.yfar
  7.6 0.0 copy-done.3
  7.6 0.0 copy-done.4
  7.6 0.0 copy-done.5
  7.6 0.0 copy-done.6
  7.6 0.0 copy-done.7
  7.6 0.0 copy-done
  7.6 0.0 copy-done.1
  7.6 0.4 copy-done.2
  8.1 0.0 copy-done.8
  8.1 0.9 %x_messages.1 = (f32[392,256]{1,0:T(8,128)S(1)}, f32[392,256]{1,0:T(8,128)S(1)}) custom-call(s32[4,6]{1,0:T(4,128)S(1)} %copy-done.9, f32[2,32,48,256]{3,2,1,0:T(8,128)S(1)} %copy-done, f32[2,32,48,256]{3,2,1,0:T(8,128)S(1)} %copy-done.1, f32[2,32,48,256]{3,2,1,0:T(8,128)S(1)} %copy-done.2, s32[32,48,256]{2,1,0:T(8,128)S(1)} %copy-done.3, ...), custom_call_target="tpu_custom_call" | custom-call | tf_op jit(solution)/shard_map/x_messages/pallas_call | solution.py:532
  9.0 3.0 %collective-permute-start.2 = (f32[392,256]{1,0:T(8,128)S(1)}, f32[392,256]{1,0:T(8,128)S(1)}, u32[]{:S(2)}, u32[]{:S(2)}) collective-permute-start(f32[392,256]{1,0:T(8,128)S(1)} %get-tuple-element.23), channel_id=1, source_target_pairs={{0,4},{4,0},{8,12},{12,8},{16,20},{20,16},{24,28},{28,24},{1,5},{5... | collective-permute-start | bytes 1204232 | tf_op jit(solution)/shard_map/ppermute | solution.py:56
  12.0 0.7 %collective-permute-start.3 = (f32[392,256]{1,0:T(8,128)S(1)}, f32[392,256]{1,0:T(8,128)S(1)}, u32[]{:S(2)}, u32[]{:S(2)}) collective-permute-start(f32[392,256]{1,0:T(8,128)S(1)} %get-tuple-element.24), channel_id=1, source_target_pairs={{4,8},{8,4},{12,16},{16,12},{20,24},{24,20},{5,9},{9,5},{13,17},{1... | collective-permute-start | bytes 1204232 | tf_op jit(solution)/shard_map/ppermute | solution.py:56
  12.7 13.4 %interior.1 = (f32[32,56,256]{2,1,0:T(8,128)S(1)}, f32[32,56,256]{2,1,0:T(8,128)S(1)}, f32[32,56,256]{2,1,0:T(8,128)S(1)}, f32[32,56,256]{2,1,0:T(8,128)}, f32[3...) custom-call(f32[2,32,48,256]{3,2,1,0:T(8,128)S(1)} %copy-done, ...), custom_call_target="tpu_custom_call" | custom-call | flops 60000000 | bytes 30000000 | tf_op jit(solution)/shard_map/interior/pallas_call | solution.py:543
  26.0 0.0 collective-permute-done.2.xnear
  26.0 0.0 collective-permute-done.3.xfar
  26.0 1.5 %edges.1 = (f32[32,256]{1,0:T(8,128)S(1)}, f32[6,56,256]{2,1,0:T(8,128)S(1)}, f32[2,56,256]{2,1,0:T(8,128)S(1)}) custom-call(s32[4,6]{1,0:T(4,128)S(1)} %copy-done.9, f32[392,256]{1,0:T(8,128)S(1)} %collective-permute-done.2.xnear, f32[392,256]{1,0:T(8,128)S(1)} %collective-permute-done.3.xfar, f32[32,56,256]{2,1,0:T(8,128)S(1)} %get-tuple-element.25.act, ...), custom_call_target="tpu_custom_call" | custom-call | tf_op jit(solution)/shard_map/edges/pallas_call | solution.py:555
  27.5 23.0 %all_to_all.11 = f32[32,1,256]{2,1,0:T(1,128)S(1)} all-to-all(f32[32,1,256]{2,1,0:T(1,128)S(1)} %copy.11), channel_id=1, replica_groups=mesh['gx'=8,'gy'=4] {'gx','gy'}, dimensions={0} | all-to-all | bytes 65536 | tf_op jit(solution)/shard_map/all_to_all | solution.py:567
  50.6 8.4 %final.1 = f32[2,32,48,256]{3,2,1,0:T(8,128)} custom-call(s32[4,6]{1,0:T(4,128)S(1)} %copy-done.9, f32[2,32,48,256]{3,2,1,0:T(8,128)S(1)} %copy-done, f32[2,32,48,256]{3,2,1,0:T(8,128)S(1)} %copy-done.1, f32[2,32,48,256]{3,2,1,0:T(8,128)S(1)} %copy-done.2, f32[32,48,256]{2,1,0:T(8,128)S(1)} %copy-done.7, f32[1,192,192]{2,1,0:T(8,128)S(1)} %copy-done.8, ...), custom_call_target="tpu_custom_call" | custom-call | tf_op jit(solution)/shard_map/final/pallas_call | solution.py:569
  (4 shorter events, 0.0 us)
Async XLA Ops:
  0.0 7.6 %copy-start.3 = (s32[32,48,256]{2,1,0:T(8,128)S(1)}, s32[32,48,256]{2,1,0:T(8,128)}, u32[]{:S(2)}) copy-start(s32[32,48,256]{2,1,0:T(8,128)} %mask.3) | copy-start | bytes 4718596
  0.0 7.6 %copy-start.4 = (f32[32,48,256]{2,1,0:T(8,128)S(1)}, f32[32,48,256]{2,1,0:T(8,128)}, u32[]{:S(2)}) copy-start(f32[32,48,256]{2,1,0:T(8,128)} %tx.3) | copy-start | bytes 4718596
  0.0 7.6 %copy-start.5 = (f32[32,48,256]{2,1,0:T(8,128)S(1)}, f32[32,48,256]{2,1,0:T(8,128)}, u32[]{:S(2)}) copy-start(f32[32,48,256]{2,1,0:T(8,128)} %ty.3) | copy-start | bytes 4718596
  0.0 7.6 %copy-start.6 = (f32[32,48,256]{2,1,0:T(8,128)S(1)}, f32[32,48,256]{2,1,0:T(8,128)}, u32[]{:S(2)}) copy-start(f32[32,48,256]{2,1,0:T(8,128)} %tz.3) | copy-start | bytes 4718596
  0.0 7.6 %copy-start.7 = (f32[32,48,256]{2,1,0:T(8,128)S(1)}, f32[32,48,256]{2,1,0:T(8,128)}, u32[]{:S(2)}) copy-start(f32[32,48,256]{2,1,0:T(8,128)} %frac.1) | copy-start | bytes 4718596
  0.0 0.8 %copy-start.9 = (s32[4,6]{1,0:T(4,128)S(1)}, s32[4,6]{1,0:T(4,128)}, u32[]{:S(2)}) copy-start(s32[4,6]{1,0:T(4,128)} %split_ref.7) | copy-start | bytes 292
  0.8 6.8 %copy-start = (f32[2,32,48,256]{3,2,1,0:T(8,128)S(1)}, f32[2,32,48,256]{3,2,1,0:T(8,128)}, u32[]{:S(2)}) copy-start(f32[2,32,48,256]{3,2,1,0:T(8,128)} %res.5) | copy-start | bytes 9437188
  0.8 6.8 %copy-start.1 = (f32[2,32,48,256]{3,2,1,0:T(8,128)S(1)}, f32[2,32,48,256]{3,2,1,0:T(8,128)}, u32[]{:S(2)}) copy-start(f32[2,32,48,256]{3,2,1,0:T(8,128)} %diag.5) | copy-start | bytes 9437188
  0.9 7.2 %copy-start.2 = (f32[2,32,48,256]{3,2,1,0:T(8,128)S(1)}, f32[2,32,48,256]{3,2,1,0:T(8,128)}, u32[]{:S(2)}) copy-start(f32[2,32,48,256]{3,2,1,0:T(8,128)} %crs.5) | copy-start | bytes 9437188
  0.9 7.2 %copy-start.8 = (f32[1,192,192]{2,1,0:T(8,128)S(1)}, f32[1,192,192]{2,1,0:T(8,128)}, u32[]{:S(2)}) copy-start(f32[1,192,192]{2,1,0:T(8,128)} %inv.3) | copy-start | bytes 442372
  5.5 2.1 %collective-permute-start = (f32[32,16,256]{2,1,0:T(8,128)S(1)}, f32[32,16,256]{2,1,0:T(8,128)S(1)}, u32[]{:S(2)}, u32[]{:S(2)}) collective-permute-start(f32[32,16,256]{2,1,0:T(8,128)S(1)} %get-tuple-element.21), channel_id=1, source_target_pairs={{0,1},{1,0},{2,3},{3,2},{4,5},{5,4},{6,7},{7,6},{8,9},{9,8},{10,11... | collective-permute-start | bytes 1572872 | tf_op jit(solution)/shard_map/ppermute | solution.py:56
  6.1 1.5 %collective-permute-start.1 = (f32[32,16,256]{2,1,0:T(8,128)S(1)}, f32[32,16,256]{2,1,0:T(8,128)S(1)}, u32[]{:S(2)}, u32[]{:S(2)}) collective-permute-start(f32[32,16,256]{2,1,0:T(8,128)S(1)} %get-tuple-element.22), channel_id=1, source_target_pairs={{1,2},{2,1},{5,6},{6,5},{9,10},{10,9},{13,14},{14,13},{17,18},{18,... | collective-permute-start | bytes 1572872 | tf_op jit(solution)/shard_map/ppermute | solution.py:56
  9.0 17.1 %collective-permute-start.2 = (f32[392,256]{1,0:T(8,128)S(1)}, f32[392,256]{1,0:T(8,128)S(1)}, u32[]{:S(2)}, u32[]{:S(2)}) collective-permute-start(f32[392,256]{1,0:T(8,128)S(1)} %get-tuple-element.23), channel_id=1, source_target_pairs={{0,4},{4,0},{8,12},{12,8},{16,20},{20,16},{24,28},{28,24},{1,5},{5... | collective-permute-start | bytes 1204232 | tf_op jit(solution)/shard_map/ppermute | solution.py:56
  12.0 14.0 %collective-permute-start.3 = (f32[392,256]{1,0:T(8,128)S(1)}, f32[392,256]{1,0:T(8,128)S(1)}, u32[]{:S(2)}, u32[]{:S(2)}) collective-permute-start(f32[392,256]{1,0:T(8,128)S(1)} %get-tuple-element.24), channel_id=1, source_target_pairs={{4,8},{8,4},{12,16},{16,12},{20,24},{24,20},{5,9},{9,5},{13,17},{1... | collective-permute-start | bytes 1204232 | tf_op jit(solution)/shard_map/ppermute | solution.py:56

commit v3 on v2

v3 whole, which is shorter than its diff:
```python
import functools

import jax
import jax.numpy as jnp
from jax import lax
from jax.experimental import pallas as pl
from jax.experimental.pallas import tpu as pltpu
from jax.sharding import PartitionSpec as P

relaxation = 2.0 / 3.0
F32 = jnp.float32
WHOLE = pl.BlockSpec(memory_space=pltpu.VMEM)
SCALARS = pl.BlockSpec(memory_space=pltpu.SMEM)
G = 8
EDGE_FIELDS = 4
PLANES = 3


def params(mib):
    return pltpu.CompilerParams(vmem_limit_bytes=mib << 20)


def cost(flops, size):
    return pl.CostEstimate(flops=flops, bytes_accessed=size, transcendentals=0)


def z_next(v):
    return pltpu.roll(v, v.shape[1] - 1, 1)


def z_prev(v):
    return pltpu.roll(v, 1, 1)


def quasi_impes(active, rp, rs, dpp, dss, dps, dsp):
    weight = dps / dss
    return active * (rp - weight * rs), active * (dpp - weight * dsp) + (1.0 - active)


def swap_pairs(axis, size):
    near = [(i, i ^ 1) for i in range(size) if i ^ 1 < size]
    far = [(i, ((i + 1) ^ 1) - 1) for i in range(size) if 0 <= ((i + 1) ^ 1) - 1 < size]
    return near, far


def swap(message, axis, size):
    near, far = swap_pairs(axis, size)
    return lax.ppermute(message[0], axis, near), lax.ppermute(message[1], axis, far)


def y_message_kernel(split_ref, *refs):
    low, high = refs[:8], refs[8:16]
    near_ref, far_ref = refs[16:]
    even = lax.rem(lax.axis_index("gy"), 2) == 0
    step = pl.program_id(0)

    def fields(group):
        res, diag, crs, mask, tx, ty, tz, ff = group
        active = mask[...].astype(F32)
        b, c = quasi_impes(active, res[0], res[1], diag[0], diag[1], crs[0], crs[1])
        return active, b, c, tx[...], ty[...], tz[...], ff[...]

    shape = low[3].shape
    s = lax.broadcasted_iota(jnp.int32, shape, 1)
    lane = lax.broadcasted_iota(jnp.int32, shape, 2)

    def turn(v, k):
        return jnp.stack([pltpu.roll(v[i], k, 0) for i in range(v.shape[0])])

    a, b, c, tx, ty, tz, ff = fields(high)
    lower = (lane < split_ref[step, split_ref.shape[1] - 1]).astype(F32)
    up = (
        jnp.where(s >= 5, a, jnp.where(s >= 2, turn(ty, 5), turn(tx, 2))),
        jnp.where(
            s >= 6,
            b,
            jnp.where(
                s >= 4,
                turn(c, 6),
                jnp.where(s >= 2, turn(tz, 4), jnp.where(s == 1, turn(ff, 2), lower)),
            ),
        ),
    )
    a, b, c, tx, ty, tz, ff = fields(low)
    lower = (lane < split_ref[step, 0]).astype(F32)
    down = (
        jnp.where(s < 3, a, jnp.where(s < 6, turn(ty, 3), turn(tx, 6))),
        jnp.where(
            s < 2,
            b,
            jnp.where(
                s < 4,
                turn(c, 2),
                jnp.where(s < 6, turn(tz, 4), jnp.where(s == 6, turn(ff, 6), lower)),
            ),
        ),
    )
    for k in range(2):
        near_ref[:, 8 * k : 8 * k + 8, :] = jnp.where(even, up[k], down[k])
        far_ref[:, 8 * k : 8 * k + 8, :] = jnp.where(even, down[k], up[k])


class Ghosts:
    def __init__(self, near_ref, far_ref):
        self.refs = near_ref, far_ref
        self.even = lax.rem(lax.axis_index("gy"), 2) == 0

    def tiles(self, x, k):
        near, far = (ref[x, 8 * k : 8 * k + 8, :] for ref in self.refs)
        return jnp.where(self.even, near, far), jnp.where(self.even, far, near)

    def pick(self, tiles, high_turn, low_turn, rings):
        high, low = tiles
        s = lax.broadcasted_iota(jnp.int32, high.shape, 0)
        high = pltpu.roll(high, high_turn, 0) if high_turn else high
        low = pltpu.roll(low, low_turn, 0) if low_turn else low
        return jnp.where(s < rings, high, jnp.where(s >= G - rings, low, 0.0))

    def first(self, x):
        t = self.tiles(x, 0)
        return self.pick(t, 0, 0, 3), self.pick(t, 2, 6, 2), self.pick(t, 5, 3, 3)

    def second(self, x):
        t = self.tiles(x, 1)
        c = jnp.maximum(self.pick(t, 6, 2, 2), 1.0)
        return self.pick(t, 0, 0, 2), c, self.pick(t, 4, 4, 2)

    def active(self, x):
        return self.pick(self.tiles(x, 0), 0, 0, 3)

    def frac_and_lower(self, x):
        t = self.tiles(x, 1)
        return self.pick(t, 2, 6, 1), self.pick(t, 1, 7, 1)


def group(k):
    return slice(8 * k, 8 * k + 8)


def turned_next(mine, after, s):
    return jnp.where(s == G - 1, after, mine)


def turned_prev(mine, before, s):
    return jnp.where(s == 0, before, mine)


def turn_next(v):
    return pltpu.roll(v, G - 1, 0)


def turn_prev(v):
    return pltpu.roll(v, 1, 0)


def places(wide):
    shape = (G, wide)
    return lax.broadcasted_iota(jnp.int32, shape, 0), lax.broadcasted_iota(jnp.int32, shape, 1)


def along_z(tz, a, lane):
    return jnp.where(lane < a.shape[1] - 1, tz * a * z_next(a), 0.0)


def prep_kernel(res_hbm, diag_hbm, crs_hbm, mask_hbm, tx_hbm, ty_hbm, tz_hbm,
                rhs, own_diag, tot, gain, one, fx, fy, fz, al0, al1, be0, be1,
                res, diag, crs, mask, tx, ty, tz, sems):
    n, own, wide = mask.shape
    groups = own // 8
    chunk = 4
    s, lane = places(wide)

    def copies(q):
        at = pl.ds(chunk * q, chunk)
        pairs = (
            (res_hbm.at[:, at], res.at[:, at]),
            (diag_hbm.at[:, at], diag.at[:, at]),
            (crs_hbm.at[:, at], crs.at[:, at]),
            (tx_hbm.at[at], tx.at[at]),
            (ty_hbm.at[at], ty.at[at]),
            (tz_hbm.at[at], tz.at[at]),
        )
        return [pltpu.make_async_copy(a, b, sems.at[k + 1, q]) for k, (a, b) in enumerate(pairs)]

    def masks(q):
        at = pl.ds(chunk * q, chunk)
        return pltpu.make_async_copy(mask_hbm.at[at], mask.at[at], sems.at[0, q])

    for q in range(n // chunk):
        for copy in (masks(q), *copies(q)):
            copy.start()
    masks(0).wait()

    def row(x, carry):
        first, last = x == 0, x == n - 1
        after = jnp.minimum(x + 1, n - 1)
        before = jnp.maximum(x - 1, 0)
        a_after = mask[x, group(0), :].astype(F32)
        turned_after = turn_next(a_after)
        ey_before = jnp.zeros((G, wide), F32)
        for k in range(groups):
            here = group(k)
            a, turned = a_after, turned_after
            rp, rs = res[0, x, here, :], res[1, x, here, :]
            dpp, dss = diag[0, x, here, :], diag[1, x, here, :]
            dps, dsp = crs[0, x, here, :], crs[1, x, here, :]
            det = dpp * dss - dps * dsp
            both = 1.0 / (dss * det)
            inverse = both * dss
            weight = dps * (both * det)
            b = a * (rp - weight * rs)
            c = a * (dpp - weight * dsp) + (1.0 - a)
            rhs[x, here, :] = b
            own_diag[x, here, :] = c
            al0[x, here, :] = dss * inverse
            al1[x, here, :] = dps * inverse
            be0[x, here, :] = dpp * inverse
            be1[x, here, :] = dsp * inverse
            t = tx[x, here, :] * a
            ex = t * mask[after, here, :].astype(F32)
            fx[x, here, :] = jnp.where(last, t, ex)
            total = c + jnp.where(last, 0.0, ex)
            total = total + jnp.where(first, 0.0, fx[before, here, :])
            ez = along_z(tz[x, here, :], a, lane)
            fz[x, here, :] = ez
            total = total + ez + z_prev(ez)
            ey = ty[x, here, :] * a
            if k < groups - 1:
                a_after = mask[x, group(k + 1), :].astype(F32)
                turned_after = turn_next(a_after)
                ey = ey * turned_next(turned, turned_after, s)
                inside = ey
            else:
                ey = jnp.where(s == G - 1, ey, ey * turned)
                inside = jnp.where(s == G - 1, 0.0, ey)
            fy[x, here, :] = ey
            ey_turned = turn_prev(inside)
            total = total + inside + turned_prev(ey_turned, ey_before, s)
            ey_before = ey_turned
            tot[x, here, :] = total
            if 0 < k < groups - 1:
                g = relaxation / total
                gain[x, here, :] = g
                one[x, here, :] = g * b
        return carry

    def part(q, carry):
        @pl.when(q < n // chunk - 1)
        def _():
            masks(q + 1).wait()

        for copy in copies(q):
            copy.wait()
        return lax.fori_loop(chunk * q, chunk * q + chunk, row, carry)

    lax.fori_loop(0, n // chunk, part, 0)


class Finished:
    def __init__(self, x, n, ghosts, mask, rhs, tot, fx, fy, s, lane):
        groups = mask.shape[1] // 8
        first, last = x == 0, x == n - 1
        ga, gtx, gty = ghosts.first(x)
        gb, gc, gtz = ghosts.second(x)
        before, after = jnp.maximum(x - 1, 0), jnp.minimum(x + 1, n - 1)
        a_before, tx_before, _ = ghosts.first(before)
        a_after = ghosts.active(after)
        turned = turn_next(ga)
        end = fy[x, group(groups - 1), :]
        end = jnp.where(s == G - 1, end * turned, end)
        a_first = mask[x, group(0), :].astype(F32)
        ey = gty * ga * turned_next(turned, turn_next(a_first), s)
        ey_turned = turn_prev(ey)
        ez = along_z(gtz, ga, lane)
        t = gtx * ga
        ex = t * a_after
        total = gc + ez + z_prev(ez) + ey + turned_prev(ey_turned, turn_prev(end), s)
        total = total + jnp.where(last, 0.0, ex) + jnp.where(first, 0.0, tx_before * a_before * ga)
        self.end = end
        self.fx, self.fy, self.fz = jnp.where(last, t, ex), ey, ez
        self.rhs = gb
        self.total = (
            tot[x, group(0), :] + jnp.where(s == 0, ey_turned, 0.0),
            tot[x, group(groups - 1), :] + jnp.where(s == G - 1, end, 0.0),
            total,
        )
        self.all_rhs = (rhs[x, group(0), :], rhs[x, group(groups - 1), :], gb)


def slot_of(k, groups):
    return {0: 0, groups - 1: 1, groups: 2}[k]


def x_message_kernel(split_ref, mask, ff, rhs, tot, gain, one, fx, fy, fz, ynear, yfar, inv, near_ref, far_ref):
    even = lax.rem(lax.axis_index("gx"), 2) == 0
    j = lax.axis_index("gy")
    n, own, wide = mask.shape
    groups = own // 8
    s, lane = places(wide)
    ghosts = Ghosts(ynear, yfar)
    per_tile = 2 * split_ref.shape[0] * split_ref.shape[1]
    finished = {x: Finished(x, n, ghosts, mask, rhs, tot, fx, fy, s, lane) for x in (0, 1, n - 2, n - 1)}
    at = 0
    for k in range(groups + 1):
        here = group(k)
        touched = k in (0, groups - 1, groups)

        def first_of(x):
            done = finished[x]
            if not touched:
                return one[x, here, :]
            slot = slot_of(k, groups)
            return relaxation * done.all_rhs[slot] / done.total[slot]

        def of(x, key):
            done = finished[x]
            total = done.total[slot_of(k, groups)] if touched else tot[x, here, :]
            if k == groups:
                return done.rhs, total, key, done.fy
            return rhs[x, here, :], total, key, done.end if k == groups - 1 else fy[x, here, :]

        if k == groups:
            up = of(n - 1, finished[n - 1].fx)
            down = of(0, ghosts.active(0))
        else:
            up = of(n - 1, fx[n - 1, here, :])
            down = of(0, mask[0, here, :].astype(F32))
            up += (fz[n - 1, here, :], fx[n - 2, here, :] * first_of(n - 2), ff[n - 1, here, :])
            down += (fz[0, here, :], fx[0, here, :] * first_of(1), ff[0, here, :])
        for f in range(len(up)):
            ext = own + G
            start = f * ext if f < EDGE_FIELDS else EDGE_FIELDS * ext + (f - EDGE_FIELDS) * own
            start += 8 * k
            near_ref[start : start + 8, :] = jnp.where(even, up[f], down[f])
            far_ref[start : start + 8, :] = jnp.where(even, down[f], up[f])
    at = EDGE_FIELDS * (own + G) + PLANES * own
    unknowns = inv.shape[2]
    top = inv[0, pl.ds(pl.multiple_of(j * per_tile + per_tile - 16, 8), 16), :]
    bottom = inv[0, pl.ds(pl.multiple_of(j * per_tile, 8), 16), :]
    for k in range(0, unknowns, wide):
        w = min(wide, unknowns - k)
        if w < wide:
            near_ref[at : at + 16, :] = jnp.zeros((16, wide), F32)
            far_ref[at : at + 16, :] = jnp.zeros((16, wide), F32)
        near_ref[at : at + 16, :w] = jnp.where(even, top[:, k : k + w], bottom[:, k : k + w])
        far_ref[at : at + 16, :w] = jnp.where(even, bottom[:, k : k + w], top[:, k : k + w])
        at += 16
    lane = lax.broadcasted_iota(jnp.int32, (1, wide), 1)
    zero = jnp.zeros((8, wide), F32)
    near_ref[at : at + 8, :] = zero
    far_ref[at : at + 8, :] = zero
    for q in range(split_ref.shape[1]):
        top = (lane < split_ref[split_ref.shape[0] - 1, q]).astype(F32)
        bottom = (lane < split_ref[0, q]).astype(F32)
        near_ref[at + q : at + q + 1, :] = jnp.where(even, top, bottom)
        far_ref[at + q : at + q + 1, :] = jnp.where(even, bottom, top)


def x_message_rows(own, unknowns, wide):
    return EDGE_FIELDS * (own + G) + PLANES * own + 16 * pl.cdiv(unknowns, wide) + 8


class Planes:
    def __init__(self, near_ref, far_ref, own):
        self.refs, self.own = (near_ref, far_ref), own
        self.even = lax.rem(lax.axis_index("gx"), 2) == 0

    def rows(self, at, n, side):
        near, far = (ref[at : at + n, :] for ref in self.refs)
        return jnp.where(self.even, near, far) if side else jnp.where(self.even, far, near)

    def field(self, f, k, side):
        ext = self.own + G
        if f < EDGE_FIELDS:
            return self.rows(f * ext + 8 * k, 8, side)
        at = EDGE_FIELDS * ext + (f - EDGE_FIELDS) * self.own
        if 8 * k == self.own:
            return jnp.zeros((8, self.refs[0].shape[1]), F32)
        return self.rows(at + 8 * k, 8, side)

    def extra(self, at, n, side):
        return self.rows(EDGE_FIELDS * (self.own + G) + PLANES * self.own + at, n, side)


class Inside:
    def __init__(self, groups, ff, rhs, gain, one, fx, fy, fz, gain3, one3, six, end):
        self.groups, self.own_ff, self.own_rhs = groups, ff, rhs
        self.own_gain, self.own_one, self.own_fx, self.own_fy, self.own_fz = gain, one, fx, fy, fz
        self.gain3, self.one3, self.six, self.end = gain3, one3, six, end

    def pick(self, own, which, x, k):
        return self.six[which, x] if k == self.groups else own[x, group(k), :]

    def three(self, own, other, x, k):
        if 0 < k < self.groups - 1:
            return own[x, group(k), :]
        return other[x, group(slot_of(k, self.groups)), :]

    def rhs(self, x, k):
        return self.pick(self.own_rhs, 0, x, k)

    def fx(self, x, k):
        return self.pick(self.own_fx, 1, x, k)

    def fy(self, x, k):
        if k == self.groups - 1:
            return self.end[x]
        return self.pick(self.own_fy, 2, x, k)

    def fz(self, x, k):
        return self.pick(self.own_fz, 3, x, k)

    def ff(self, x, k):
        return self.pick(self.own_ff, 4, x, k)

    def gain(self, x, k):
        return self.three(self.own_gain, self.gain3, x, k)

    def one(self, x, k):
        return self.three(self.own_one, self.one3, x, k)

    def before(self, x, k):
        return self.fx(x - 1, k) * self.one(x - 1, k)

    def after(self, x, k):
        return self.fx(x, k) * self.one(x + 1, k)


def second_row(o, x, s, put):
    total = o.groups + 1
    p = o.one(x, 0)
    p_turned = turn_next(p)
    w_turned = turn_prev(o.fy(x, total - 1) * o.one(x, total - 1))
    for k in range(total):
        p_after = o.one(x, (k + 1) % total)
        after_turned = turn_next(p_after)
        ey, ez = o.fy(x, k), o.fz(x, k)
        mine = turn_prev(ey * p)
        beside = ey * turned_next(p_turned, after_turned, s) + turned_prev(mine, w_turned, s)
        beside = beside + ez * z_next(p) + z_prev(ez * p)
        beside = beside + o.after(x, k) + o.before(x, k)
        put(k, o.gain(x, k) * ((2.0 - relaxation) * o.rhs(x, k) + beside))
        p, p_turned, w_turned = p_after, after_turned, mine


def x_flux(o, x, k, two):
    step = two(x + 1, k) - two(x, k)
    ex = o.fx(x, k)
    return ex * step, ex * (o.ff(x, k) + o.ff(x + 1, k)) * step


def flux_row(o, x, s, lane, two, res, own_diag, split, carried, put):
    groups = o.groups

    def faces_y(k, p, p_turned, p_after, f, f_turned, f_after):
        ey = o.fy(x, k)
        weighted = ey * (f + turned_next(f_turned, f_after, s))
        return ey, weighted, turned_next(p_turned, p_after, s) - p

    p0, f0 = two(x, 0), o.ff(x, 0)
    p0_turned, f0_turned = turn_next(p0), turn_next(f0)
    p, f = two(x, groups), o.ff(x, groups)
    ghost = faces_y(groups, p, turn_next(p), p0_turned, f, turn_next(f), f0_turned)
    turned = [turn_prev(v) for v in ghost]
    p, f, p_turned, f_turned = p0, f0, p0_turned, f0_turned
    for k in range(groups):
        here = group(k)
        p_after, f_after = two(x, k + 1), o.ff(x, k + 1)
        p_after_turned, f_after_turned = turn_next(p_after), turn_next(f_after)
        mine = faces_y(k, p, p_turned, p_after_turned, f, f_turned, f_after_turned)
        mine_turned = [turn_prev(v) for v in mine]
        ey, wy, dy = mine
        ey_before, wy_before, dy_before = (
            turned_prev(a, b, s) for a, b in zip(mine_turned, turned, strict=True)
        )
        ez = o.fz(x, k)
        wz = ez * (f + z_next(f))
        dz = z_next(p) - p
        ez_before, wz_before, dz_before = z_prev(ez), z_prev(wz), z_prev(dz)
        qx, sx = x_flux(o, x, k, two)
        gained = (qx - carried[0, here, :]) + (ey * dy - ey_before * dy_before)
        gained = gained + (ez * dz - ez_before * dz_before)
        weighed = (sx - carried[1, here, :]) + (wy * dy - wy_before * dy_before)
        weighed = weighed + (wz * dz - wz_before * dz_before)
        carried[0, here, :] = qx
        carried[1, here, :] = sx
        rest = o.rhs(x, k) - own_diag[x, here, :] * p + gained
        below = lane < split(k)
        put(
            k,
            rest,
            res[0, x, here, :] + gained,
            res[1, x, here, :] + 0.5 * weighed,
            jnp.where(s == 0, ey_before, ey),
            jnp.where(s == 0, wy_before, wy),
            jnp.where(below, ez, ez_before),
            jnp.where(below, wz, wz_before),
        )
        turned = mine_turned
        p, f, p_turned, f_turned = p_after, f_after, p_after_turned, f_after_turned


FLUXES = 6


def interior_kernel(split_ref, res, mask, ff, rhs, own_diag, tot, gain, one, fx, fy, fz, ynear, yfar,
                    tot3, gain3, one3, six, end, two, acc, *flux_and_carried):
    flux, carried = flux_and_carried[:FLUXES], flux_and_carried[FLUXES]
    n, own, wide = mask.shape
    groups = own // 8
    s, lane = places(wide)
    ghosts = Ghosts(ynear, yfar)

    def finish(x, carry):
        done = Finished(x, n, ghosts, mask, rhs, tot, fx, fy, s, lane)
        for slot in range(3):
            g = relaxation / done.total[slot]
            tot3[x, group(slot), :] = done.total[slot]
            gain3[x, group(slot), :] = g
            one3[x, group(slot), :] = g * done.all_rhs[slot]
        end[x] = done.end
        for k, v in enumerate((done.rhs, done.fx, done.fy, done.fz, ghosts.frac_and_lower(x)[0])):
            six[k, x] = v
        return carry

    lax.fori_loop(0, n, finish, 0)
    o = Inside(groups, ff, rhs, gain, one, fx, fy, fz, gain3, one3, six, end)

    def second(x, carry):
        def put(k, v):
            two[x, group(k), :] = v

        second_row(o, x, s, put)
        return carry

    lax.fori_loop(2, n - 2, second, 0)

    def two_of(x, k):
        return two[x, group(k), :]

    for k in range(groups):
        carried[0, group(k), :], carried[1, group(k), :] = x_flux(o, 2, k, two_of)
    acc[...] = jnp.zeros_like(acc)

    def row(x, carry):
        def put(k, rest, *values):
            acc[x // 8, group(k), :] += rest
            for f, v in enumerate(values):
                flux[f][x, group(k), :] = v

        flux_row(o, x, s, lane, two_of, res, own_diag, lambda k: split_ref[x // 8, k], carried, put)
        return carry

    lax.fori_loop(3, n - 3, row, 0)


class Edges(Inside):
    def beyond(self, n, planes, act, tot, tot3, one_edge, gain_edge, edge_fx):
        self.n, self.planes = n, planes
        self.slots = {-1: 0, 0: 1, n - 1: 2, n: 3}
        self.one_edge, self.gain_edge, self.edge_fx = one_edge, gain_edge, edge_fx
        self.far = {-1: 0, n: 1}
        for k in range(self.groups + 1):
            here = group(k)
            low = planes.field(2, k, 0) * act(k)
            high = super().fx(n - 1, k) * planes.field(2, k, 1)
            edge_fx[0, here, :] = low
            edge_fx[1, here, :] = high
            for x, slot in self.slots.items():
                face = low if x <= 0 else high
                if x in self.far:
                    total = jnp.maximum(planes.field(1, k, self.far[x]), 1.0) + face
                else:
                    total = self.three(tot, tot3, x, k) + face
                g = relaxation / total
                gain_edge[slot, here, :] = g
                one_edge[slot, here, :] = g * self.rhs(x, k)

    def rhs(self, x, k):
        return self.planes.field(0, k, self.far[x]) if x in self.far else super().rhs(x, k)

    def fx(self, x, k):
        if x in (-1, self.n - 1):
            return self.edge_fx[0 if x == -1 else 1, group(k), :]
        return super().fx(x, k)

    def fy(self, x, k):
        return self.planes.field(3, k, self.far[x]) if x in self.far else super().fy(x, k)

    def fz(self, x, k):
        return self.planes.field(4, k, self.far[x]) if x in self.far else super().fz(x, k)

    def ff(self, x, k):
        return self.planes.field(6, k, self.far[x]) if x in self.far else super().ff(x, k)

    def gain(self, x, k):
        return self.gain_edge[self.slots[x], group(k), :] if x in self.slots else super().gain(x, k)

    def one(self, x, k):
        return self.one_edge[self.slots[x], group(k), :] if x in self.slots else super().one(x, k)

    def before(self, x, k):
        return self.planes.field(5, k, 0) if x == -1 else super().before(x, k)

    def after(self, x, k):
        return self.planes.field(5, k, 1) if x == self.n else super().after(x, k)


def edge_kernel(split_ref, res, mask, ff, rhs, own_diag, tot, gain, one, fx, fy, fz, ynear, yfar, xnear, xfar,
                tot3, gain3, one3, six, end, two, acc,
                sent, edge_flux, edge_fx, one_edge, gain_edge, two_edge, carried, total_acc):
    n, own, wide = mask.shape
    groups = own // 8
    s, lane = places(wide)
    planes = Planes(xnear, xfar, own)
    ghosts = Ghosts(ynear, yfar)
    o = Edges(groups, ff, rhs, gain, one, fx, fy, fz, gain3, one3, six, end)

    def act(k):
        return ghosts.active(0) if k == groups else mask[0, group(k), :].astype(F32)

    o.beyond(n, planes, act, tot, tot3, one_edge, gain_edge, edge_fx)
    slots = {x: slot for slot, x in enumerate((-1, 0, 1, n - 2, n - 1, n))}
    for x, slot in slots.items():

        def put_two(k, v, slot=slot):
            two_edge[slot, group(k), :] = v

        second_row(o, x, s, put_two)

    def two_of(x, k):
        return two_edge[slots[x], group(k), :] if x in slots else two[x, group(k), :]

    total_acc[...] = acc[...]
    for slot, x in enumerate((0, 1, 2, n - 3, n - 2, n - 1)):
        if slot % 3 == 0:
            for k in range(groups):
                carried[0, group(k), :], carried[1, group(k), :] = x_flux(o, x - 1, k, two_of)

        def put(k, rest, *values, x=x, slot=slot):
            total_acc[x // 8, group(k), :] += rest
            for f, v in enumerate(values):
                edge_flux[f, slot, group(k), :] = v

        flux_row(o, x, s, lane, two_of, res, own_diag, lambda k, x=x: split_ref[x // 8, k], carried, put)

    rows_b, cols_b = split_ref.shape
    lane = lax.broadcasted_iota(jnp.int32, (1, wide), 1)
    lower, upper = [], []
    for q in range(rows_b):
        for r in range(cols_b):
            column = jnp.sum(total_acc[q, group(r), :], axis=0, keepdims=True)
            below = lane < split_ref[q, r]
            lower.append(jnp.where(below, column, 0.0))
            upper.append(jnp.where(below, 0.0, column))
    count = rows_b * cols_b
    low_sum = jnp.sum(jnp.concatenate(lower, axis=0), axis=1, keepdims=True)
    high_sum = jnp.sum(jnp.concatenate(upper, axis=0), axis=1, keepdims=True)
    span = sent.shape[1]
    place = lax.broadcasted_iota(jnp.int32, (count, span), 1) - 2 * count * lax.axis_index("gy")
    which = 2 * lax.broadcasted_iota(jnp.int32, (count, span), 0)
    laid = jnp.where(place == which, low_sum, jnp.where(place == which + 1, high_sum, 0.0))
    sent[...] = jnp.broadcast_to(jnp.sum(laid, axis=0, keepdims=True), sent.shape)


def final_kernel(tiles_y, split_ref, frac, inv, ynear, yfar, xnear, xfar, fx, edge_flux, edge_fx,
                 al0, al1, be0, be1, got, *rest):
    flux = rest[:FLUXES]
    out, coarse, step_y, step_z, held, sems = rest[FLUXES:]
    i, j = lax.axis_index("gx"), lax.axis_index("gy")
    n, own, wide = frac.shape
    ext = own + G
    unknowns = inv.shape[2]
    rows_b, cols_b = split_ref.shape
    per_tile = 2 * rows_b * cols_b
    ghosts = Ghosts(ynear, yfar)
    planes = Planes(xnear, xfar, own)
    s8, lane8 = places(wide)

    all_got = got[...]
    owner = lax.broadcasted_iota(jnp.int32, all_got.shape, 0)

    def row_of(tile_row):
        mine = (owner >= tile_row * tiles_y) & (owner < (tile_row + 1) * tiles_y)
        return jnp.sum(jnp.where(mine, all_got, 0.0), axis=0, keepdims=True)

    coarse_res = row_of(i)

    def solve(tile):
        start = pl.multiple_of(jnp.clip(tile, 0, tiles_y - 1) * per_tile, 8)
        block = inv[0, pl.ds(start, per_tile), :]
        e = jnp.sum(block * coarse_res[:, :unknowns], axis=1, keepdims=True)
        return jnp.broadcast_to(e, (per_tile, wide))

    mine, before, after = solve(j), solve(j - 1), solve(j + 1)

    def one_of(e, k):
        return jnp.broadcast_to(e[k : k + 1], (8, wide))

    for q in range(rows_b):
        for r in range(cols_b):
            k = 2 * (q * cols_b + r)
            low, high = one_of(mine, k), one_of(mine, k + 1)
            split = split_ref[q, r]
            coarse[q + 1, group(r), :] = jnp.where(lane8 < split, low, high)
            jump = high - low
            step_z[q, group(r), :] = jnp.where(
                lane8 == split - 1, jump, jnp.where(lane8 == split, -jump, 0.0)
            )
        below = ghosts.frac_and_lower(8 * q)[1] > 0.5
        k_high, k_low = 2 * q * cols_b, 2 * (q * cols_b + cols_b - 1)
        coarse[q + 1, own:ext, :] = jnp.where(
            s8 == 0,
            jnp.where(below, one_of(after, k_high), one_of(after, k_high + 1)),
            jnp.where(below, one_of(before, k_low), one_of(before, k_low + 1)),
        )
        for r in range(cols_b):
            here = coarse[q + 1, group(r), :]
            ahead = turn_next(coarse[q + 1, group(r + 1), :])
            behind = turn_prev(coarse[q + 1, group(r - 1 if r else cols_b), :])
            step_y[q, group(r), :] = jnp.where(
                s8 == G - 1, ahead - here, jnp.where(s8 == 0, behind - here, 0.0)
            )
    blocks = pl.cdiv(unknowns, wide)
    for side, tile_row in ((0, i - 1), (1, i + 1)):
        other = row_of(tile_row)
        e = jnp.zeros((16, 1), F32)
        for k in range(blocks):
            w = min(wide, unknowns - k * wide)
            part = planes.extra(16 * k, 16, side)[:, :w] * other[:, k * wide : k * wide + w]
            e = e + jnp.sum(part, axis=1, keepdims=True)
        e = jnp.broadcast_to(e, (16, wide))
        below = planes.extra(16 * blocks, 8, side)
        skip = 16 - 2 * cols_b if side == 0 else 0
        at = 0 if side == 0 else rows_b + 1
        for r in range(cols_b):
            k = skip + 2 * r
            coarse[at, group(r), :] = jnp.where(one_of(below, r) > 0.5, one_of(e, k), one_of(e, k + 1))

    def solved(x, q, values, beside):
        for r in range(cols_b):
            here = group(r)
            u, v, wy, sy, wz, sz = (value(r) for value in values)
            along_y, along_z = step_y[q, here, :], step_z[q, here, :]
            u = u + (wy * along_y + wz * along_z)
            weighed = sy * along_y + sz * along_z
            if beside is not None:
                ex, sx, step = beside(r)
                u = u + ex * step
                weighed = weighed + sx * step
            v = v + 0.5 * weighed
            held[0, x, here, :] = al0[x, here, :] * u - al1[x, here, :] * v
            held[1, x, here, :] = be0[x, here, :] * v - be1[x, here, :] * u

    def copies(q):
        return [
            pltpu.make_async_copy(
                held.at[k, pl.ds(8 * q, 8)], out.at[k, pl.ds(8 * q, 8)], sems.at[k, q]
            )
            for k in range(2)
        ]

    def frac_of(x, r):
        if x in (-1, n):
            return planes.field(6, r, 0 if x == -1 else 1)
        return frac[x, group(r), :]

    def face(x, r):
        if x in (-1, n - 1):
            ex = edge_fx[0 if x == -1 else 1, group(r), :]
        else:
            ex = fx[x, group(r), :]
        return ex, ex * (frac_of(x, r) + frac_of(x + 1, r))

    outer = {x: slot for slot, x in enumerate((0, 1, 2, n - 3, n - 2, n - 1))}

    def values_of(x):
        if isinstance(x, int) and x in outer:
            return [lambda r, f=f: edge_flux[f, outer[x], group(r), :] for f in range(FLUXES)]
        return [lambda r, f=f: flux[f][x, group(r), :] for f in range(FLUXES)]

    for q in range(rows_b):
        first, last = 8 * q, 8 * q + 7

        def ahead(r, q=q, last=last):
            return *face(last, r), coarse[q + 2, group(r), :] - coarse[q + 1, group(r), :]

        def behind(r, q=q, first=first):
            return *face(first - 1, r), coarse[q, group(r), :] - coarse[q + 1, group(r), :]

        solved(first, q, values_of(first), behind)
        start, stop = first + 1, last
        while start in outer:
            solved(start, q, values_of(start), None)
            start += 1
        while stop - 1 in outer:
            stop -= 1
            solved(stop, q, values_of(stop), None)

        def row(x, carry, q=q):
            solved(x, q, values_of(x), None)
            return carry

        lax.fori_loop(start, stop, row, 0)
        solved(last, q, values_of(last), ahead)
        for copy in copies(q):
            copy.start()
    for q in range(rows_b):
        for copy in copies(q):
            copy.wait()


def shards(tiles_x, tiles_y, residual, accum_diag, accum_cross, mask, trans_x, trans_y, trans_z,
           frac_flow, split_layer, coarse_inverse):
    n, own, wide = mask.shape
    ext = own + G
    unknowns = coarse_inverse.shape[2]
    columns = (residual, accum_diag, accum_cross, mask, trans_x, trans_y, trans_z, frac_flow)
    far_columns = [pltpu.with_memory_space_constraint(v, pltpu.HBM) for v in columns]
    groups = own // 8

    def group_spec(array, k):
        lead = array.shape[:-3]
        zero = (0,) * len(lead)
        return pl.BlockSpec((*lead, 8, 8, wide), lambda x: (*zero, x, k, 0))

    def array(*shape):
        return jax.ShapeDtypeStruct(shape, F32)

    y_messages = pl.pallas_call(
        y_message_kernel,
        grid=(n // 8,),
        in_specs=[SCALARS]
        + [group_spec(v, 0) for v in columns]
        + [group_spec(v, groups - 1) for v in columns],
        out_specs=[pl.BlockSpec((8, 16, wide), lambda x: (x, 0, 0))] * 2,
        out_shape=[array(n, 16, wide)] * 2,
        compiler_params=params(16),
        name="y_messages",
    )(split_layer, *far_columns, *far_columns)
    ynear, yfar = swap(y_messages, "gy", tiles_y)

    rhs, own_diag, tot, gain, one, fx, fy, fz, al0, al1, be0, be1 = pl.pallas_call(
        prep_kernel,
        in_specs=[pl.BlockSpec(memory_space=pltpu.HBM)] * 7,
        out_specs=[WHOLE] * 12,
        out_shape=[array(n, own, wide)] * 12,
        scratch_shapes=[pltpu.VMEM(v.shape, v.dtype) for v in columns[:7]]
        + [pltpu.SemaphoreType.DMA((7, n // 4))],
        compiler_params=params(18),
        cost_estimate=cost(60_000_000, 30_000_000),
        name="prep",
    )(*far_columns[:7])
    shared = (rhs, tot, gain, one, fx, fy, fz)

    x_messages = pl.pallas_call(
        x_message_kernel,
        in_specs=[SCALARS] + [WHOLE] * 12,
        out_specs=[WHOLE] * 2,
        out_shape=[array(x_message_rows(own, unknowns, wide), wide)] * 2,
        compiler_params=params(8),
        name="x_messages",
    )(split_layer, mask, frac_flow, *shared, ynear, yfar, coarse_inverse)
    xnear, xfar = swap(x_messages, "gx", tiles_x)

    shared = (residual, mask, frac_flow, rhs, own_diag, tot, gain, one, fx, fy, fz, ynear, yfar)
    tot3, gain3, one3, six, end, two, acc, *flux = pl.pallas_call(
        interior_kernel,
        in_specs=[SCALARS] + [WHOLE] * 13,
        out_specs=[WHOLE] * (7 + FLUXES),
        out_shape=[array(n, 3 * G, wide)] * 3
        + [
            array(5, n, G, wide),
            array(n, G, wide),
            array(n, ext, wide),
            array(n // 8, own, wide),
        ]
        + [array(n, own, wide)] * FLUXES,
        scratch_shapes=[pltpu.VMEM((2, own, wide), F32)],
        compiler_params=params(8),
        cost_estimate=cost(60_000_000, 30_000_000),
        name="interior",
    )(split_layer, *shared)

    devices = tiles_x * tiles_y
    span = pl.cdiv(unknowns, 128) * 128
    sent, edge_flux, edge_fx = pl.pallas_call(
        edge_kernel,
        in_specs=[SCALARS] + [WHOLE] * 22,
        out_specs=[WHOLE] * 3,
        out_shape=[array(devices, span), array(FLUXES, 6, own, wide), array(2, ext, wide)],
        scratch_shapes=[
            pltpu.VMEM((4, ext, wide), F32),
            pltpu.VMEM((4, ext, wide), F32),
            pltpu.VMEM((6, ext, wide), F32),
            pltpu.VMEM((2, own, wide), F32),
            pltpu.VMEM((n // 8, own, wide), F32),
        ],
        compiler_params=params(8),
        name="edges",
    )(split_layer, *shared, xnear, xfar, tot3, gain3, one3, six, end, two, acc)
    got = lax.all_to_all(sent, ("gx", "gy"), 0, 0, tiled=True)

    return pl.pallas_call(
        functools.partial(final_kernel, tiles_y),
        in_specs=[SCALARS] + [WHOLE] * (14 + FLUXES),
        out_specs=pl.BlockSpec(memory_space=pl.ANY),
        out_shape=array(2, n, own, wide),
        scratch_shapes=[
            pltpu.VMEM((n // 8 + 2, ext, wide), F32),
            pltpu.VMEM((n // 8, own, wide), F32),
            pltpu.VMEM((n // 8, own, wide), F32),
            pltpu.VMEM((2, n, own, wide), F32),
            pltpu.SemaphoreType.DMA((2, n // 8)),
        ],
        compiler_params=params(12),
        name="final",
    )(split_layer, frac_flow, coarse_inverse, ynear, yfar, xnear, xfar, fx, edge_flux, edge_fx,
      al0, al1, be0, be1, got, *flux)


def solution(mesh):
    placed = (
        P(None, "gx", "gy", None),
        P(None, "gx", "gy", None),
        P(None, "gx", "gy", None),
        P("gx", "gy", None),
        P("gx", "gy", None),
        P("gx", "gy", None),
        P("gx", "gy", None),
        P("gx", "gy", None),
        P("gx", "gy"),
        P("gx", None, None),
    )
    return jax.shard_map(
        functools.partial(shards, mesh.shape["gx"], mesh.shape["gy"]),
        mesh=mesh,
        in_specs=placed,
        out_specs=P(None, "gx", "gy", None),
        check_vma=False,
    )
```

time: 59.2 us -> 54.6 us (0.922)
  blocking collectives: 23 us -> 15.5 us
  Pallas kernels: 28.8 us -> 31.7 us
  waiting for transfers between devices: 0.72 us -> 1.71 us
  local copies, waits for them, and re-layouts: 1.34 us -> 0.74 us
    pallas_call x3 -> x4, Pallas kernels: 15.7 us -> 25.2 us  [the longest x1 13.9 us: shards(): pl.pallas_call(interior_kernel, in_specs=[SCALARS] + [WHOLE] * 13, out_sp...]
    all_to_all x1, blocking collectives: 23 us -> 15.5 us  [shards(): got = lax.all_to_all(sent, ('gx', 'gy'), 0, 0, tiled=True)]
    pallas_call x1, Pallas kernels: 8.43 us -> 3.06 us  [shards(): pl.pallas_call(functools.partial(final_kernel, tiles_y), in_specs=[SCALAR...]
    pallas_call x1, Pallas kernels: 4.64 us -> 3.5 us  [shards(): pl.pallas_call(y_message_kernel, grid=(n // 8,), in_specs=[SCALARS] + [gr...]
    ppermute x2, waiting for transfers between devices: 0.72 us -> 1.71 us  [swap(): lax.ppermute(message[0], axis, near)]
    unnamed x21 -> x13, local copies, waits for them, and re-layouts: 1.31 us -> 0.71 us
  transfers between devices with their start and end apart: 4 -> 4, of which waited for: 1 -> 1; matrix products, arithmetic and copies ran while one was open for 0% -> 0% of each run, Pallas kernels for 23% -> 39%
where the time goes in v3:
time: 54.6 us; the launch traced here: 54.3 us
  Pallas kernels  31.7 us (58%)
  blocking collectives  15.5 us (28%)
  starting transfers between devices  4.59 us (8%)
  waiting for transfers between devices  1.71 us (3%)
  local copies, waits for them, and re-layouts  0.74 us (1%)
    all_to_all x1, blocking collectives, shards(): got = lax.all_to_all(sent, ('gx', 'gy'), 0, 0, tiled=True)  15.5 us
    pallas_call x1, Pallas kernels, shards(): pl.pallas_call(interior_kernel, in_specs=[SCALARS] + [WHOLE] * 13, out_sp...  13.9 us
    pallas_call x1, Pallas kernels, shards(): pl.pallas_call(prep_kernel, in_specs=[pl.BlockSpec(memory_space=pltpu.HBM...  7.45 us
    pallas_call x1, Pallas kernels, shards(): pl.pallas_call(y_message_kernel, grid=(n // 8,), in_specs=[SCALARS] + [gr...  3.5 us
    pallas_call x1, Pallas kernels, shards(): pl.pallas_call(edge_kernel, in_specs=[SCALARS] + [WHOLE] * 22, out_specs=...  3.11 us
    ppermute x2, starting transfers between devices, swap(): lax.ppermute(message[0], axis, near)  3.09 us
    pallas_call x1, Pallas kernels, shards(): pl.pallas_call(functools.partial(final_kernel, tiles_y), in_specs=[SCALAR...  3.06 us
    ppermute x2, waiting for transfers between devices, swap(): lax.ppermute(message[0], axis, near)  1.71 us
  transfers between devices with their start and end apart: 4, of which 1 were waited for; matrix products, arithmetic and copies ran while one was open for 0% of the time, Pallas kernels for 39%

profile of v3, /device:TPU:0, one launch (start us, length us, event | category | flops | bytes accessed | tf_op | source)
XLA Modules:
  0.0 54.3 jit_solution(7105803534763986877)
XLA Ops:
  0.0 0.0 copy-start.4
  0.0 0.7 %copy-done.4 = s32[4,6]{1,0:T(4,128)S(1)} copy-done((s32[4,6]{1,0:T(4,128)S(1)}, s32[4,6]{1,0:T(4,128)}, u32[]{:S(2)}) %copy-start.4) | copy-done | bytes 120
  0.7 3.5 %y_messages.1 = (f32[32,16,256]{2,1,0:T(8,128)S(1)}, f32[32,16,256]{2,1,0:T(8,128)S(1)}) custom-call(s32[4,6]{1,0:T(4,128)S(1)} %copy-done.4, f32[2,32,48,256]{3,2,1,0:T(8,128)} %res.3, f32[2,32,48,256]{3,2,1,0:T(8,128)} %diag_hbm.1, f32[2,32,48,256]{3,2,1,0:T(8,128)} %crs_hbm.1, s32[32,48,256]{2,1,0:T(8,128)} %mask.5, f32[32,48,256]{2,1,0:T(8,128)} %tx_hbm.1, ...), custom_call_target="tpu_custom_call" | custom-call | tf_op jit(solution)/shard_map/y_messages/pallas_call | solution.py:830
  4.2 0.5 collective-permute-start
  4.7 0.0 copy-start.1
  4.7 0.0 copy-start.2
  4.7 0.0 copy-start.3
  4.7 0.0 copy-start.5
  4.7 0.8 %collective-permute-start.1 = (f32[32,16,256]{2,1,0:T(8,128)S(1)}, f32[32,16,256]{2,1,0:T(8,128)S(1)}, u32[]{:S(2)}, u32[]{:S(2)}) collective-permute-start(f32[32,16,256]{2,1,0:T(8,128)S(1)} %get-tuple-element.38), channel_id=1, source_target_pairs={{1,2},{2,1},{5,6},{6,5},{9,10},{10,9},{13,14},{14,13},{17,18},{18,... | collective-permute-start | bytes 1572872 | tf_op jit(solution)/shard_map/ppermute | solution.py:48
  5.6 7.4 %prep.1 = (f32[32,48,256]{2,1,0:T(8,128)S(1)}, f32[32,48,256]{2,1,0:T(8,128)S(1)}, f32[32,48,256]{2,1,0:T(8,128)S(1)}, f32[32,48,256]{2,1,0:T(8,128)S(1)}, f32[3...) custom-call(f32[2,32,48,256]{3,2,1,0:T(8,128)} %res.3, ...), custom_call_target="tpu_custom_call" | custom-call | flops 60000000 | bytes 30000000 | tf_op jit(solution)/shard_map/prep/pallas_call | solution.py:843
  13.0 0.0 collective-permute-done.ynear
  13.0 0.0 collective-permute-done.1.yfar
  13.0 0.0 copy-done.1
  13.0 0.0 copy-done.2
  13.1 0.0 copy-done.3
  13.1 0.0 copy-done.5
  13.1 0.0 copy-start
  13.1 0.7 %x_messages.1 = (f32[392,256]{1,0:T(8,128)S(1)}, f32[392,256]{1,0:T(8,128)S(1)}) custom-call(s32[4,6]{1,0:T(4,128)S(1)} %copy-done.5, s32[32,48,256]{2,1,0:T(8,128)S(1)} %copy-done.2, f32[32,48,256]{2,1,0:T(8,128)S(1)} %copy-done.1, f32[32,48,256]{2,1,0:T(8,128)S(1)} %get-tuple-element.39.rhs, f32[32,48,256]{2,1,0:T(8,128)S(1)} %get-tuple-element.40.tot, ...), custom_call_target="tpu_custom_call" | custom-call | tf_op jit(solution)/shard_map/x_messages/pallas_call | solution.py:856
  13.8 2.6 %collective-permute-start.2 = (f32[392,256]{1,0:T(8,128)S(1)}, f32[392,256]{1,0:T(8,128)S(1)}, u32[]{:S(2)}, u32[]{:S(2)}) collective-permute-start(f32[392,256]{1,0:T(8,128)S(1)} %get-tuple-element.46), channel_id=1, source_target_pairs={{0,4},{4,0},{8,12},{12,8},{16,20},{20,16},{24,28},{28,24},{1,5},{5... | collective-permute-start | bytes 1204232 | tf_op jit(solution)/shard_map/ppermute | solution.py:48
  16.4 0.7 %collective-permute-start.3 = (f32[392,256]{1,0:T(8,128)S(1)}, f32[392,256]{1,0:T(8,128)S(1)}, u32[]{:S(2)}, u32[]{:S(2)}) collective-permute-start(f32[392,256]{1,0:T(8,128)S(1)} %get-tuple-element.47), channel_id=1, source_target_pairs={{4,8},{8,4},{12,16},{16,12},{20,24},{24,20},{5,9},{9,5},{13,17},{1... | collective-permute-start | bytes 1204232 | tf_op jit(solution)/shard_map/ppermute | solution.py:48
  17.1 0.0 copy-done
  17.1 13.9 %interior.1 = (f32[32,24,256]{2,1,0:T(8,128)S(1)}, f32[32,24,256]{2,1,0:T(8,128)S(1)}, f32[32,24,256]{2,1,0:T(8,128)S(1)}, f32[5,32,8,256]{3,2,1,0:T(8,128)S(1)}...) custom-call(s32[4,6]{1,0:T(4,128)S(1)} %copy-done.5, ...), custom_call_target="tpu_custom_call" | custom-call | flops 60000000 | bytes 30000000 | tf_op jit(solution)/shard_map/interior/pallas_call | solution.py:867
  31.0 1.7 %collective-permute-done.2.xnear = f32[392,256]{1,0:T(8,128)S(1)} collective-permute-done((f32[392,256]{1,0:T(8,128)S(1)}, f32[392,256]{1,0:T(8,128)S(1)}, u32[]{:S(2)}, u32[]{:S(2)}) %collective-permute-start.2) | collective-permute-done | bytes 401440 | tf_op jit(solution)/shard_map/ppermute | solution.py:48
  32.7 0.0 collective-permute-done.3.xfar
  32.7 3.1 %edges.1 = (f32[32,256]{1,0:T(8,128)S(1)}, f32[6,6,48,256]{3,2,1,0:T(8,128)S(1)}, f32[2,56,256]{2,1,0:T(8,128)S(1)}) custom-call(s32[4,6]{1,0:T(4,128)S(1)} %copy-done.5, f32[2,32,48,256]{3,2,1,0:T(8,128)S(1)} %copy-done, s32[32,48,256]{2,1,0:T(8,128)S(1)} %copy-done.2, f32[32,48,256]{2,1,0:T(8,128)S(1)} %copy-done.1, ...), custom_call_target="tpu_custom_call" | custom-call | tf_op jit(solution)/shard_map/edges/pallas_call | solution.py:887
  35.8 15.5 %all_to_all.11 = f32[32,1,256]{2,1,0:T(1,128)S(1)} all-to-all(f32[32,1,256]{2,1,0:T(1,128)S(1)} %copy.11), channel_id=1, replica_groups=mesh['gx'=8,'gy'=4] {'gx','gy'}, dimensions={0} | all-to-all | bytes 65536 | tf_op jit(solution)/shard_map/all_to_all | solution.py:902
  51.3 3.1 %final.1 = f32[2,32,48,256]{3,2,1,0:T(8,128)} custom-call(s32[4,6]{1,0:T(4,128)S(1)} %copy-done.5, f32[32,48,256]{2,1,0:T(8,128)S(1)} %copy-done.1, f32[1,192,192]{2,1,0:T(8,128)S(1)} %copy-done.3, f32[32,16,256]{2,1,0:T(8,128)S(1)} %collective-permute-done.ynear, f32[32,16,256]{2,1,0:T(8,128)S(1)} %collective-permute-done.1.yfar, ...), custom_call_target="tpu_custom_call" | custom-call | tf_op jit(solution)/shard_map/final/pallas_call | solution.py:904
  (2 shorter events, 0.0 us)
Async XLA Ops:
  0.0 0.7 %copy-start.4 = (s32[4,6]{1,0:T(4,128)S(1)}, s32[4,6]{1,0:T(4,128)}, u32[]{:S(2)}) copy-start(s32[4,6]{1,0:T(4,128)} %split_ref.9) | copy-start | bytes 292
  4.2 8.8 %collective-permute-start = (f32[32,16,256]{2,1,0:T(8,128)S(1)}, f32[32,16,256]{2,1,0:T(8,128)S(1)}, u32[]{:S(2)}, u32[]{:S(2)}) collective-permute-start(f32[32,16,256]{2,1,0:T(8,128)S(1)} %get-tuple-element.37), channel_id=1, source_target_pairs={{0,1},{1,0},{2,3},{3,2},{4,5},{5,4},{6,7},{7,6},{8,9},{9,8},{10,11... | collective-permute-start | bytes 1572872 | tf_op jit(solution)/shard_map/ppermute | solution.py:48
  4.7 8.3 %copy-start.1 = (f32[32,48,256]{2,1,0:T(8,128)S(1)}, f32[32,48,256]{2,1,0:T(8,128)}, u32[]{:S(2)}) copy-start(f32[32,48,256]{2,1,0:T(8,128)} %frac.1) | copy-start | bytes 4718596
  4.7 8.3 %copy-start.2 = (s32[32,48,256]{2,1,0:T(8,128)S(1)}, s32[32,48,256]{2,1,0:T(8,128)}, u32[]{:S(2)}) copy-start(s32[32,48,256]{2,1,0:T(8,128)} %mask.5) | copy-start | bytes 4718596
  4.7 8.3 %copy-start.3 = (f32[1,192,192]{2,1,0:T(8,128)S(1)}, f32[1,192,192]{2,1,0:T(8,128)}, u32[]{:S(2)}) copy-start(f32[1,192,192]{2,1,0:T(8,128)} %inv.3) | copy-start | bytes 442372
  4.7 8.3 %copy-start.5 = (s32[4,6]{1,0:T(4,128)S(1)}, s32[4,6]{1,0:T(4,128)}, u32[]{:S(2)}) copy-start(s32[4,6]{1,0:T(4,128)} %split_ref.9) | copy-start | bytes 292
  4.7 8.3 %collective-permute-start.1 = (f32[32,16,256]{2,1,0:T(8,128)S(1)}, f32[32,16,256]{2,1,0:T(8,128)S(1)}, u32[]{:S(2)}, u32[]{:S(2)}) collective-permute-start(f32[32,16,256]{2,1,0:T(8,128)S(1)} %get-tuple-element.38), channel_id=1, source_target_pairs={{1,2},{2,1},{5,6},{6,5},{9,10},{10,9},{13,14},{14,13},{17,18},{18,... | collective-permute-start | bytes 1572872 | tf_op jit(solution)/shard_map/ppermute | solution.py:48
  13.1 4.0 %copy-start = (f32[2,32,48,256]{3,2,1,0:T(8,128)S(1)}, f32[2,32,48,256]{3,2,1,0:T(8,128)}, u32[]{:S(2)}) copy-start(f32[2,32,48,256]{3,2,1,0:T(8,128)} %res.3) | copy-start | bytes 9437188
  13.8 18.8 %collective-permute-start.2 = (f32[392,256]{1,0:T(8,128)S(1)}, f32[392,256]{1,0:T(8,128)S(1)}, u32[]{:S(2)}, u32[]{:S(2)}) collective-permute-start(f32[392,256]{1,0:T(8,128)S(1)} %get-tuple-element.46), channel_id=1, source_target_pairs={{0,4},{4,0},{8,12},{12,8},{16,20},{20,16},{24,28},{28,24},{1,5},{5... | collective-permute-start | bytes 1204232 | tf_op jit(solution)/shard_map/ppermute | solution.py:48
  16.4 16.3 %collective-permute-start.3 = (f32[392,256]{1,0:T(8,128)S(1)}, f32[392,256]{1,0:T(8,128)S(1)}, u32[]{:S(2)}, u32[]{:S(2)}) collective-permute-start(f32[392,256]{1,0:T(8,128)S(1)} %get-tuple-element.47), channel_id=1, source_target_pairs={{4,8},{8,4},{12,16},{16,12},{20,24},{24,20},{5,9},{9,5},{13,17},{1... | collective-permute-start | bytes 1204232 | tf_op jit(solution)/shard_map/ppermute | solution.py:48

commit v4 on v3

--- a/solution.py
+++ b/solution.py
@@ -12,8 +12,7 @@
 WHOLE = pl.BlockSpec(memory_space=pltpu.VMEM)
 SCALARS = pl.BlockSpec(memory_space=pltpu.SMEM)
 G = 8
-EDGE_FIELDS = 4
-PLANES = 3
+PLANES = 6
 
 
 def params(mib):
@@ -68,7 +67,8 @@
         return jnp.stack([pltpu.roll(v[i], k, 0) for i in range(v.shape[0])])
 
     a, b, c, tx, ty, tz, ff = fields(high)
-    lower = (lane < split_ref[step, split_ref.shape[1] - 1]).astype(F32)
+    splits = split_ref[pl.ds(step, 1), :]
+    lower = (lane < splits[:, -1:].reshape(1, 1, 1)).astype(F32)
     up = (
         jnp.where(s >= 5, a, jnp.where(s >= 2, turn(ty, 5), turn(tx, 2))),
         jnp.where(
@@ -82,7 +82,7 @@
         ),
     )
     a, b, c, tx, ty, tz, ff = fields(low)
-    lower = (lane < split_ref[step, 0]).astype(F32)
+    lower = (lane < splits[:, :1].reshape(1, 1, 1)).astype(F32)
     down = (
         jnp.where(s < 3, a, jnp.where(s < 6, turn(ty, 3), turn(tx, 6))),
         jnp.where(
@@ -251,7 +251,7 @@
 
         for copy in copies(q):
             copy.wait()
-        return lax.fori_loop(chunk * q, chunk * q + chunk, row, carry)
+        return lax.fori_loop(0, chunk, lambda k, v: row(chunk * q + k, v), carry, unroll=2)
 
     lax.fori_loop(0, n // chunk, part, 0)
 
@@ -291,16 +291,13 @@
     return {0: 0, groups - 1: 1, groups: 2}[k]
 
 
-def x_message_kernel(split_ref, mask, ff, rhs, tot, gain, one, fx, fy, fz, ynear, yfar, inv, near_ref, far_ref):
+def x_message_kernel(mask, rhs, tot, gain, one, fx, fy, fz, ynear, yfar, near_ref, far_ref):
     even = lax.rem(lax.axis_index("gx"), 2) == 0
-    j = lax.axis_index("gy")
     n, own, wide = mask.shape
     groups = own // 8
     s, lane = places(wide)
     ghosts = Ghosts(ynear, yfar)
-    per_tile = 2 * split_ref.shape[0] * split_ref.shape[1]
     finished = {x: Finished(x, n, ghosts, mask, rhs, tot, fx, fy, s, lane) for x in (0, 1, n - 2, n - 1)}
-    at = 0
     for k in range(groups + 1):
         here = group(k)
         touched = k in (0, groups - 1, groups)
@@ -325,15 +322,33 @@
         else:
             up = of(n - 1, fx[n - 1, here, :])
             down = of(0, mask[0, here, :].astype(F32))
-            up += (fz[n - 1, here, :], fx[n - 2, here, :] * first_of(n - 2), ff[n - 1, here, :])
-            down += (fz[0, here, :], fx[0, here, :] * first_of(1), ff[0, here, :])
-        for f in range(len(up)):
-            ext = own + G
-            start = f * ext if f < EDGE_FIELDS else EDGE_FIELDS * ext + (f - EDGE_FIELDS) * own
-            start += 8 * k
-            near_ref[start : start + 8, :] = jnp.where(even, up[f], down[f])
-            far_ref[start : start + 8, :] = jnp.where(even, down[f], up[f])
-    at = EDGE_FIELDS * (own + G) + PLANES * own
+            up += (fz[n - 1, here, :], fx[n - 2, here, :] * first_of(n - 2))
+            down += (fz[0, here, :], fx[0, here, :] * first_of(1))
+        if k == groups:
+            b, total, key, ey = (jnp.where(even, p, q) for p, q in zip(up, down, strict=True))
+            ob, ototal, okey, oey = (jnp.where(even, q, p) for p, q in zip(up, down, strict=True))
+            for ref, (b, total, key, ey) in (
+                (near_ref, (b, total, key, ey)),
+                (far_ref, (ob, ototal, okey, oey)),
+            ):
+                at = PLANES * own
+                ref[at : at + G, :] = jnp.where((s == 0) | (s == G - 1), b, pltpu.roll(total, 4, 0))
+                ref[at + G : at + 2 * G, :] = jnp.where((s < 2) | (s >= G - 2), key, pltpu.roll(ey, 4, 0))
+        else:
+            for f in range(PLANES):
+                start = f * own + 8 * k
+                near_ref[start : start + 8, :] = jnp.where(even, up[f], down[f])
+                far_ref[start : start + 8, :] = jnp.where(even, down[f], up[f])
+
+
+def late_messages(split_ref, ff, inv, near_ref, far_ref):
+    even = lax.rem(lax.axis_index("gx"), 2) == 0
+    j = lax.axis_index("gy")
+    n, own, wide = ff.shape
+    per_tile = 2 * split_ref.shape[0] * split_ref.shape[1]
+    near_ref[0:own, :] = jnp.where(even, ff[n - 1], ff[0])
+    far_ref[0:own, :] = jnp.where(even, ff[0], ff[n - 1])
+    at = own
     unknowns = inv.shape[2]
     top = inv[0, pl.ds(pl.multiple_of(j * per_tile + per_tile - 16, 8), 16), :]
     bottom = inv[0, pl.ds(pl.multiple_of(j * per_tile, 8), 16), :]
@@ -356,8 +371,8 @@
         far_ref[at + q : at + q + 1, :] = jnp.where(even, bottom, top)
 
 
-def x_message_rows(own, unknowns, wide):
-    return EDGE_FIELDS * (own + G) + PLANES * own + 16 * pl.cdiv(unknowns, wide) + 8
+def late_rows(own, unknowns, wide):
+    return own + 16 * pl.cdiv(unknowns, wide) + 8
 
 
 class Planes:
@@ -370,16 +385,19 @@
         return jnp.where(self.even, near, far) if side else jnp.where(self.even, far, near)
 
     def field(self, f, k, side):
-        ext = self.own + G
-        if f < EDGE_FIELDS:
-            return self.rows(f * ext + 8 * k, 8, side)
-        at = EDGE_FIELDS * ext + (f - EDGE_FIELDS) * self.own
-        if 8 * k == self.own:
-            return jnp.zeros((8, self.refs[0].shape[1]), F32)
-        return self.rows(at + 8 * k, 8, side)
-
-    def extra(self, at, n, side):
-        return self.rows(EDGE_FIELDS * (self.own + G) + PLANES * self.own + at, n, side)
+        if 8 * k < self.own:
+            return self.rows(f * self.own + 8 * k, 8, side)
+        s, _ = places(self.refs[0].shape[1])
+        ends = (s == 0) | (s == G - 1)
+        if f < 2:
+            tile = self.rows(PLANES * self.own, G, side)
+            return jnp.where(ends, pltpu.roll(tile, 4, 0) if f else tile, 0.0)
+        if f < 4:
+            tile = self.rows(PLANES * self.own + G, G, side)
+            if f == 2:
+                return jnp.where((s < 2) | (s >= G - 2), tile, 0.0)
+            return jnp.where(s == G - 1, pltpu.roll(tile, 4, 0), 0.0)
+        return jnp.zeros_like(s, F32)
 
 
 class Inside:
@@ -424,6 +442,9 @@
 
     def after(self, x, k):
         return self.fx(x, k) * self.one(x + 1, k)
+
+    def outermost(self, x):
+        return False
 
 
 def second_row(o, x, s, put):
@@ -446,6 +467,8 @@
 def x_flux(o, x, k, two):
     step = two(x + 1, k) - two(x, k)
     ex = o.fx(x, k)
+    if o.outermost(x):
+        return ex * step, jnp.zeros_like(step)
     return ex * step, ex * (o.ff(x, k) + o.ff(x + 1, k)) * step
 
 
@@ -503,9 +526,10 @@
 FLUXES = 6
 
 
-def interior_kernel(split_ref, res, mask, ff, rhs, own_diag, tot, gain, one, fx, fy, fz, ynear, yfar,
-                    tot3, gain3, one3, six, end, two, acc, *flux_and_carried):
+def interior_kernel(split_ref, inv, res, mask, ff, rhs, own_diag, tot, gain, one, fx, fy, fz, ynear, yfar,
+                    late_near, late_far, tot3, gain3, one3, six, end, two, acc, *flux_and_carried):
     flux, carried = flux_and_carried[:FLUXES], flux_and_carried[FLUXES]
+    late_messages(split_ref, ff, inv, late_near, late_far)
     n, own, wide = mask.shape
     groups = own // 8
     s, lane = places(wide)
@@ -523,7 +547,7 @@
             six[k, x] = v
         return carry
 
-    lax.fori_loop(0, n, finish, 0)
+    lax.fori_loop(0, n, finish, 0, unroll=8)
     o = Inside(groups, ff, rhs, gain, one, fx, fy, fz, gain3, one3, six, end)
 
     def second(x, carry):
@@ -533,7 +557,7 @@
         second_row(o, x, s, put)
         return carry
 
-    lax.fori_loop(2, n - 2, second, 0)
+    lax.fori_loop(2, n - 2, second, 0, unroll=4)
 
     def two_of(x, k):
         return two[x, group(k), :]
@@ -551,7 +575,7 @@
         flux_row(o, x, s, lane, two_of, res, own_diag, lambda k: split_ref[x // 8, k], carried, put)
         return carry
 
-    lax.fori_loop(3, n - 3, row, 0)
+    lax.fori_loop(3, n - 3, row, 0, unroll=2)
 
 
 class Edges(Inside):
@@ -590,8 +614,8 @@
     def fz(self, x, k):
         return self.planes.field(4, k, self.far[x]) if x in self.far else super().fz(x, k)
 
-    def ff(self, x, k):
-        return self.planes.field(6, k, self.far[x]) if x in self.far else super().ff(x, k)
+    def outermost(self, x):
+        return x in (-1, self.n - 1)
 
     def gain(self, x, k):
         return self.gain_edge[self.slots[x], group(k), :] if x in self.slots else super().gain(x, k)
@@ -608,7 +632,7 @@
 
 def edge_kernel(split_ref, res, mask, ff, rhs, own_diag, tot, gain, one, fx, fy, fz, ynear, yfar, xnear, xfar,
                 tot3, gain3, one3, six, end, two, acc,
-                sent, edge_flux, edge_fx, one_edge, gain_edge, two_edge, carried, total_acc):
+                sent, edge_flux, edge_fx, edge_step, one_edge, gain_edge, two_edge, carried, total_acc):
     n, own, wide = mask.shape
     groups = own // 8
     s, lane = places(wide)
@@ -631,6 +655,9 @@
     def two_of(x, k):
         return two_edge[slots[x], group(k), :] if x in slots else two[x, group(k), :]
 
+    for k in range(groups):
+        edge_step[0, group(k), :] = two_of(0, k) - two_of(-1, k)
+        edge_step[1, group(k), :] = two_of(n, k) - two_of(n - 1, k)
     total_acc[...] = acc[...]
     for slot, x in enumerate((0, 1, 2, n - 3, n - 2, n - 1)):
         if slot % 3 == 0:
@@ -663,7 +690,7 @@
     sent[...] = jnp.broadcast_to(jnp.sum(laid, axis=0, keepdims=True), sent.shape)
 
 
-def final_kernel(tiles_y, split_ref, frac, inv, ynear, yfar, xnear, xfar, fx, edge_flux, edge_fx,
+def final_kernel(tiles_y, split_ref, frac, inv, ynear, yfar, xnear, xfar, fx, edge_flux, edge_fx, edge_step,
                  al0, al1, be0, be1, got, *rest):
     flux = rest[:FLUXES]
     out, coarse, step_y, step_z, held, sems = rest[FLUXES:]
@@ -727,10 +754,10 @@
         e = jnp.zeros((16, 1), F32)
         for k in range(blocks):
             w = min(wide, unknowns - k * wide)
-            part = planes.extra(16 * k, 16, side)[:, :w] * other[:, k * wide : k * wide + w]
+            part = planes.rows(own + 16 * k, 16, side)[:, :w] * other[:, k * wide : k * wide + w]
             e = e + jnp.sum(part, axis=1, keepdims=True)
         e = jnp.broadcast_to(e, (16, wide))
-        below = planes.extra(16 * blocks, 8, side)
+        below = planes.rows(own + 16 * blocks, 8, side)
         skip = 16 - 2 * cols_b if side == 0 else 0
         at = 0 if side == 0 else rows_b + 1
         for r in range(cols_b):
@@ -745,9 +772,9 @@
             u = u + (wy * along_y + wz * along_z)
             weighed = sy * along_y + sz * along_z
             if beside is not None:
-                ex, sx, step = beside(r)
+                ex, sx, step, sweep_step = beside(r)
                 u = u + ex * step
-                weighed = weighed + sx * step
+                weighed = weighed + sx * (step + sweep_step)
             v = v + 0.5 * weighed
             held[0, x, here, :] = al0[x, here, :] * u - al1[x, here, :] * v
             held[1, x, here, :] = be0[x, here, :] * v - be1[x, here, :] * u
@@ -762,7 +789,7 @@
 
     def frac_of(x, r):
         if x in (-1, n):
-            return planes.field(6, r, 0 if x == -1 else 1)
+            return planes.rows(8 * r, 8, 0 if x == -1 else 1)
         return frac[x, group(r), :]
 
     def face(x, r):
@@ -783,10 +810,12 @@
         first, last = 8 * q, 8 * q + 7
 
         def ahead(r, q=q, last=last):
-            return *face(last, r), coarse[q + 2, group(r), :] - coarse[q + 1, group(r), :]
+            more = edge_step[1, group(r), :] if last == n - 1 else 0.0
+            return *face(last, r), coarse[q + 2, group(r), :] - coarse[q + 1, group(r), :], more
 
         def behind(r, q=q, first=first):
-            return *face(first - 1, r), coarse[q, group(r), :] - coarse[q + 1, group(r), :]
+            more = -edge_step[0, group(r), :] if first == 0 else 0.0
+            return *face(first - 1, r), coarse[q, group(r), :] - coarse[q + 1, group(r), :], more
 
         solved(first, q, values_of(first), behind)
         start, stop = first + 1, last
@@ -801,7 +830,7 @@
             solved(x, q, values_of(x), None)
             return carry
 
-        lax.fori_loop(start, stop, row, 0)
+        lax.fori_loop(start, stop, row, 0, unroll=3 if (stop - start) % 3 == 0 else 1)
         solved(last, q, values_of(last), ahead)
         for copy in copies(q):
             copy.start()
@@ -830,14 +859,14 @@
     y_messages = pl.pallas_call(
         y_message_kernel,
         grid=(n // 8,),
-        in_specs=[SCALARS]
+        in_specs=[pl.BlockSpec(split_layer.shape, lambda x: (0, 0))]
         + [group_spec(v, 0) for v in columns]
         + [group_spec(v, groups - 1) for v in columns],
         out_specs=[pl.BlockSpec((8, 16, wide), lambda x: (x, 0, 0))] * 2,
         out_shape=[array(n, 16, wide)] * 2,
         compiler_params=params(16),
         name="y_messages",
-    )(split_layer, *far_columns, *far_columns)
+    )(pltpu.with_memory_space_constraint(split_layer, pltpu.HBM), *far_columns, *far_columns)
     ynear, yfar = swap(y_messages, "gy", tiles_y)
 
     rhs, own_diag, tot, gain, one, fx, fy, fz, al0, al1, be0, be1 = pl.pallas_call(
@@ -855,20 +884,21 @@
 
     x_messages = pl.pallas_call(
         x_message_kernel,
-        in_specs=[SCALARS] + [WHOLE] * 12,
+        in_specs=[WHOLE] * 10,
         out_specs=[WHOLE] * 2,
-        out_shape=[array(x_message_rows(own, unknowns, wide), wide)] * 2,
+        out_shape=[array(PLANES * own + 2 * G, wide)] * 2,
         compiler_params=params(8),
         name="x_messages",
-    )(split_layer, mask, frac_flow, *shared, ynear, yfar, coarse_inverse)
+    )(mask, *shared, ynear, yfar)
     xnear, xfar = swap(x_messages, "gx", tiles_x)
 
     shared = (residual, mask, frac_flow, rhs, own_diag, tot, gain, one, fx, fy, fz, ynear, yfar)
-    tot3, gain3, one3, six, end, two, acc, *flux = pl.pallas_call(
+    late_near, late_far, tot3, gain3, one3, six, end, two, acc, *flux = pl.pallas_call(
         interior_kernel,
-        in_specs=[SCALARS] + [WHOLE] * 13,
-        out_specs=[WHOLE] * (7 + FLUXES),
-        out_shape=[array(n, 3 * G, wide)] * 3
+        in_specs=[SCALARS] + [WHOLE] * 14,
+        out_specs=[WHOLE] * (9 + FLUXES),
+        out_shape=[array(late_rows(own, unknowns, wide), wide)] * 2
+        + [array(n, 3 * G, wide)] * 3
         + [
             array(5, n, G, wide),
             array(n, G, wide),
@@ -880,15 +910,21 @@
         compiler_params=params(8),
         cost_estimate=cost(60_000_000, 30_000_000),
         name="interior",
-    )(split_layer, *shared)
+    )(split_layer, coarse_inverse, *shared)
+    late_near, late_far = swap((late_near, late_far), "gx", tiles_x)
 
     devices = tiles_x * tiles_y
     span = pl.cdiv(unknowns, 128) * 128
-    sent, edge_flux, edge_fx = pl.pallas_call(
+    sent, edge_flux, edge_fx, edge_step = pl.pallas_call(
         edge_kernel,
         in_specs=[SCALARS] + [WHOLE] * 22,
-        out_specs=[WHOLE] * 3,
-        out_shape=[array(devices, span), array(FLUXES, 6, own, wide), array(2, ext, wide)],
+        out_specs=[WHOLE] * 4,
+        out_shape=[
+            array(devices, span),
+            array(FLUXES, 6, own, wide),
+            array(2, ext, wide),
+            array(2, own, wide),
+        ],
         scratch_shapes=[
             pltpu.VMEM((4, ext, wide), F32),
             pltpu.VMEM((4, ext, wide), F32),
@@ -903,7 +939,7 @@
 
     return pl.pallas_call(
         functools.partial(final_kernel, tiles_y),
-        in_specs=[SCALARS] + [WHOLE] * (14 + FLUXES),
+        in_specs=[SCALARS] + [WHOLE] * (15 + FLUXES),
         out_specs=pl.BlockSpec(memory_space=pl.ANY),
         out_shape=array(2, n, own, wide),
         scratch_shapes=[
@@ -915,8 +951,8 @@
         ],
         compiler_params=params(12),
         name="final",
-    )(split_layer, frac_flow, coarse_inverse, ynear, yfar, xnear, xfar, fx, edge_flux, edge_fx,
-      al0, al1, be0, be1, got, *flux)
+    )(split_layer, frac_flow, coarse_inverse, ynear, yfar, late_near, late_far, fx, edge_flux, edge_fx,
+      edge_step, al0, al1, be0, be1, got, *flux)
 
 
 def solution(mesh):

time: 54.6 us -> 50.7 us (0.929)
  Pallas kernels: 31.7 us -> 23.6 us
  starting transfers between devices: 4.59 us -> 9.56 us
  waiting for transfers between devices: 1.71 us -> 0.02 us
    pallas_call x3, Pallas kernels: 18.1 us -> 10.9 us  [the longest x1 7.2 us: shards(): pl.pallas_call(interior_kernel, in_specs=[SCALARS] + [WHOLE] * 14, out_sp...]
    ppermute x2 -> x3, starting transfers between devices: 3.09 us -> 7.43 us  [swap(): lax.ppermute(message[0], axis, near)]
    ppermute x2 -> x3, waiting for transfers between devices: 1.71 us -> 0.01 us  [swap(): lax.ppermute(message[0], axis, near)]
    pallas_call x1, Pallas kernels: 7.45 us -> 6.35 us  [shards(): pl.pallas_call(prep_kernel, in_specs=[pl.BlockSpec(memory_space=pltpu.HBM...]
    ppermute x2 -> x3, starting transfers between devices: 1.5 us -> 2.14 us  [swap(): lax.ppermute(message[1], axis, far)]
    unnamed x13 -> x15, local copies, waits for them, and re-layouts: 0.71 us -> 1.18 us
  transfers between devices with their start and end apart: 4 -> 6, of which waited for: 1 -> 0; matrix products, arithmetic and copies ran while one was open for 0% -> 0% of each run, Pallas kernels for 39% -> 33%
where the time goes in v4:
time: 50.7 us; the launch traced here: 50.5 us
  Pallas kernels  23.6 us (47%)
  blocking collectives  15.9 us (31%)
  starting transfers between devices  9.56 us (19%)
  local copies, waits for them, and re-layouts  1.21 us (2%)
    all_to_all x1, blocking collectives, shards(): got = lax.all_to_all(sent, ('gx', 'gy'), 0, 0, tiled=True)  15.9 us
    ppermute x3, starting transfers between devices, swap(): lax.ppermute(message[0], axis, near)  7.43 us
    pallas_call x1, Pallas kernels, shards(): pl.pallas_call(interior_kernel, in_specs=[SCALARS] + [WHOLE] * 14, out_sp...  7.2 us
    pallas_call x1, Pallas kernels, shards(): pl.pallas_call(prep_kernel, in_specs=[pl.BlockSpec(memory_space=pltpu.HBM...  6.35 us
    pallas_call x1, Pallas kernels, shards(): pl.pallas_call(y_message_kernel, grid=(n // 8,), in_specs=[pl.BlockSpec(s...  3.57 us
    pallas_call x1, Pallas kernels, shards(): pl.pallas_call(edge_kernel, in_specs=[SCALARS] + [WHOLE] * 22, out_specs=...  3.18 us
    pallas_call x1, Pallas kernels, shards(): pl.pallas_call(functools.partial(final_kernel, tiles_y), in_specs=[SCALAR...  3.09 us
    ppermute x3, starting transfers between devices, swap(): lax.ppermute(message[1], axis, far)  2.14 us
  transfers between devices with their start and end apart: 6, of which 0 were waited for; matrix products, arithmetic and copies ran while one was open for 0% of the time, Pallas kernels for 33%

profile of v4, /device:TPU:0, one launch (start us, length us, event | category | flops | bytes accessed | tf_op | source)
XLA Modules:
  0.0 50.5 jit_solution(15142808983456142627)
XLA Ops:
  0.0 3.6 %y_messages.1 = (f32[32,16,256]{2,1,0:T(8,128)S(1)}, f32[32,16,256]{2,1,0:T(8,128)S(1)}) custom-call(s32[4,6]{1,0:T(4,128)} %split_ref.7, f32[2,32,48,256]{3,2,1,0:T(8,128)} %res.3, f32[2,32,48,256]{3,2,1,0:T(8,128)} %diag_hbm.1, f32[2,32,48,256]{3,2,1,0:T(8,128)} %crs_hbm.1, s32[32,48,256]{2,1,0:T(8,128)} %mask.5, f32[32,48,256]{2,1,0:T(8,128)} %tx_hbm.1, ...), custom_call_target="tpu_custom_call" | custom-call | tf_op jit(solution)/shard_map/y_messages/pallas_call | solution.py:859
  3.6 0.5 %collective-permute-start = (f32[32,16,256]{2,1,0:T(8,128)S(1)}, f32[32,16,256]{2,1,0:T(8,128)S(1)}, u32[]{:S(2)}, u32[]{:S(2)}) collective-permute-start(f32[32,16,256]{2,1,0:T(8,128)S(1)} %get-tuple-element.40), channel_id=1, source_target_pairs={{0,1},{1,0},{2,3},{3,2},{4,5},{5,4},{6,7},{7,6},{8,9},{9,8},{10,11... | collective-permute-start | bytes 1572872 | tf_op jit(solution)/shard_map/ppermute | solution.py:47
  4.1 0.8 %collective-permute-start.1 = (f32[32,16,256]{2,1,0:T(8,128)S(1)}, f32[32,16,256]{2,1,0:T(8,128)S(1)}, u32[]{:S(2)}, u32[]{:S(2)}) collective-permute-start(f32[32,16,256]{2,1,0:T(8,128)S(1)} %get-tuple-element.41), channel_id=1, source_target_pairs={{1,2},{2,1},{5,6},{6,5},{9,10},{10,9},{13,14},{14,13},{17,18},{18,... | collective-permute-start | bytes 1572872 | tf_op jit(solution)/shard_map/ppermute | solution.py:47
  4.9 6.3 %prep.1 = (f32[32,48,256]{2,1,0:T(8,128)S(1)}, f32[32,48,256]{2,1,0:T(8,128)S(1)}, f32[32,48,256]{2,1,0:T(8,128)S(1)}, f32[32,48,256]{2,1,0:T(8,128)S(1)}, f32[3...) custom-call(f32[2,32,48,256]{3,2,1,0:T(8,128)} %res.3, ...), custom_call_target="tpu_custom_call" | custom-call | flops 60000000 | bytes 30000000 | tf_op jit(solution)/shard_map/prep/pallas_call | solution.py:872
  11.3 0.0 copy-start.3
  11.3 1.1 %copy-done.3 = f32[32,48,256]{2,1,0:T(8,128)} copy-done((f32[32,48,256]{2,1,0:T(8,128)}, f32[32,48,256]{2,1,0:T(8,128)S(1)}, u32[]{:S(2)}) %copy-start.3) | copy-done | bytes 1572888
  12.4 0.0 collective-permute-done.ynear
  12.4 0.0 collective-permute-done.1.yfar
  12.4 0.0 copy-done.1
  12.4 0.0 copy-start
  12.4 0.0 copy-start.2
  12.5 0.0 copy-start.5
  12.5 0.0 copy-start.6
  12.5 0.2 x_messages.1
  12.7 2.6 %collective-permute-start.4 = (f32[304,256]{1,0:T(8,128)S(1)}, f32[304,256]{1,0:T(8,128)S(1)}, u32[]{:S(2)}, u32[]{:S(2)}) collective-permute-start(f32[304,256]{1,0:T(8,128)S(1)} %get-tuple-element.52), channel_id=1, source_target_pairs={{0,4},{4,0},{8,12},{12,8},{16,20},{20,16},{24,28},{28,24},{1,5},{5... | collective-permute-start | bytes 933896 | tf_op jit(solution)/shard_map/ppermute | solution.py:47
  15.2 0.7 %collective-permute-start.5 = (f32[304,256]{1,0:T(8,128)S(1)}, f32[304,256]{1,0:T(8,128)S(1)}, u32[]{:S(2)}, u32[]{:S(2)}) collective-permute-start(f32[304,256]{1,0:T(8,128)S(1)} %get-tuple-element.53), channel_id=1, source_target_pairs={{4,8},{8,4},{12,16},{16,12},{20,24},{24,20},{5,9},{9,5},{13,17},{1... | collective-permute-start | bytes 933896 | tf_op jit(solution)/shard_map/ppermute | solution.py:47
  15.9 0.0 copy-done
  15.9 0.0 copy-done.2
  15.9 0.0 copy-done.5
  15.9 0.0 copy-done.6
  15.9 7.2 %interior.1 = (f32[72,256]{1,0:T(8,128)S(1)}, f32[72,256]{1,0:T(8,128)S(1)}, f32[32,24,256]{2,1,0:T(8,128)S(1)}, f32[32,24,256]{2,1,0:T(8,128)S(1)}, f32[32,24,2...) custom-call(s32[4,6]{1,0:T(4,128)S(1)} %copy-done.6, ...), custom_call_target="tpu_custom_call" | custom-call | flops 60000000 | bytes 30000000 | tf_op jit(solution)/shard_map/interior/pallas_call | solution.py:896
  23.2 4.3 %collective-permute-start.2 = (f32[72,256]{1,0:T(8,128)S(1)}, f32[72,256]{1,0:T(8,128)S(1)}, u32[]{:S(2)}, u32[]{:S(2)}) collective-permute-start(f32[72,256]{1,0:T(8,128)S(1)} %get-tuple-element.50), channel_id=1, source_target_pairs={{0,4},{4,0},{8,12},{12,8},{16,20},{20,16},{24,28},{28,24},{1,5},{5... | collective-permute-start | bytes 221192 | tf_op jit(solution)/shard_map/ppermute | solution.py:47
  27.5 0.7 %collective-permute-start.3 = (f32[72,256]{1,0:T(8,128)S(1)}, f32[72,256]{1,0:T(8,128)S(1)}, u32[]{:S(2)}, u32[]{:S(2)}) collective-permute-start(f32[72,256]{1,0:T(8,128)S(1)} %get-tuple-element.51), channel_id=1, source_target_pairs={{4,8},{8,4},{12,16},{16,12},{20,24},{24,20},{5,9},{9,5},{13,17},{1... | collective-permute-start | bytes 221192 | tf_op jit(solution)/shard_map/ppermute | solution.py:47
  28.2 0.0 collective-permute-done.4.xnear
  28.2 0.0 collective-permute-done.5.xfar
  28.2 0.0 copy-start.4
  28.2 3.2 %edges.1 = (f32[32,256]{1,0:T(8,128)S(1)}, f32[6,6,48,256]{3,2,1,0:T(8,128)S(1)}, f32[2,56,256]{2,1,0:T(8,128)S(1)}, f32[2,48,256]{2,1,0:T(8,128)S(1)}) custom-call(s32[4,6]{1,0:T(4,128)S(1)} %copy-done.6, f32[2,32,48,256]{3,2,1,0:T(8,128)S(1)} %copy-done, s32[32,48,256]{2,1,0:T(8,128)S(1)} %copy-done.1, f32[32,48,256]{2,1,0:T(8,128)S(1)} %copy-done.2, ...), custom_call_target="tpu_custom_call" | custom-call | tf_op jit(solution)/shard_map/edges/pallas_call | solution.py:918
  31.4 15.9 %all_to_all.11 = f32[32,1,256]{2,1,0:T(1,128)S(1)} all-to-all(f32[32,1,256]{2,1,0:T(1,128)S(1)} %copy.11), channel_id=1, replica_groups=mesh['gx'=8,'gy'=4] {'gx','gy'}, dimensions={0} | all-to-all | bytes 65536 | tf_op jit(solution)/shard_map/all_to_all | solution.py:938
  47.4 0.0 collective-permute-done.2.xnear
  47.4 0.0 collective-permute-done.3.xfar
  47.4 0.0 copy-done.4
  47.4 3.1 %final.1 = f32[2,32,48,256]{3,2,1,0:T(8,128)} custom-call(s32[4,6]{1,0:T(4,128)S(1)} %copy-done.6, f32[32,48,256]{2,1,0:T(8,128)S(1)} %copy-done.2, f32[1,192,192]{2,1,0:T(8,128)S(1)} %copy-done.5, f32[32,16,256]{2,1,0:T(8,128)S(1)} %collective-permute-done.ynear, f32[32,16,256]{2,1,0:T(8,128)S(1)} %collective-permute-done.1.yfar, ...), custom_call_target="tpu_custom_call" | custom-call | tf_op jit(solution)/shard_map/final/pallas_call | solution.py:940
  (3 shorter events, 0.0 us)
Async XLA Ops:
  3.6 8.8 %collective-permute-start = (f32[32,16,256]{2,1,0:T(8,128)S(1)}, f32[32,16,256]{2,1,0:T(8,128)S(1)}, u32[]{:S(2)}, u32[]{:S(2)}) collective-permute-start(f32[32,16,256]{2,1,0:T(8,128)S(1)} %get-tuple-element.40), channel_id=1, source_target_pairs={{0,1},{1,0},{2,3},{3,2},{4,5},{5,4},{6,7},{7,6},{8,9},{9,8},{10,11... | collective-permute-start | bytes 1572872 | tf_op jit(solution)/shard_map/ppermute | solution.py:47
  4.1 8.3 %copy-start.1 = (s32[32,48,256]{2,1,0:T(8,128)S(1)}, s32[32,48,256]{2,1,0:T(8,128)}, u32[]{:S(2)}) copy-start(s32[32,48,256]{2,1,0:T(8,128)} %mask.5) | copy-start | bytes 4718596
  4.1 8.3 %collective-permute-start.1 = (f32[32,16,256]{2,1,0:T(8,128)S(1)}, f32[32,16,256]{2,1,0:T(8,128)S(1)}, u32[]{:S(2)}, u32[]{:S(2)}) collective-permute-start(f32[32,16,256]{2,1,0:T(8,128)S(1)} %get-tuple-element.41), channel_id=1, source_target_pairs={{1,2},{2,1},{5,6},{6,5},{9,10},{10,9},{13,14},{14,13},{17,18},{18,... | collective-permute-start | bytes 1572872 | tf_op jit(solution)/shard_map/ppermute | solution.py:47
  11.3 1.1 %copy-start.3 = (f32[32,48,256]{2,1,0:T(8,128)}, f32[32,48,256]{2,1,0:T(8,128)S(1)}, u32[]{:S(2)}) copy-start(f32[32,48,256]{2,1,0:T(8,128)S(1)} %get-tuple-element.67.be1) | copy-start | bytes 4718596
  12.4 3.5 %copy-start = (f32[2,32,48,256]{3,2,1,0:T(8,128)S(1)}, f32[2,32,48,256]{3,2,1,0:T(8,128)}, u32[]{:S(2)}) copy-start(f32[2,32,48,256]{3,2,1,0:T(8,128)} %res.3) | copy-start | bytes 9437188
  12.4 3.5 %copy-start.2 = (f32[32,48,256]{2,1,0:T(8,128)S(1)}, f32[32,48,256]{2,1,0:T(8,128)}, u32[]{:S(2)}) copy-start(f32[32,48,256]{2,1,0:T(8,128)} %frac.1) | copy-start | bytes 4718596
  12.5 3.5 %copy-start.5 = (f32[1,192,192]{2,1,0:T(8,128)S(1)}, f32[1,192,192]{2,1,0:T(8,128)}, u32[]{:S(2)}) copy-start(f32[1,192,192]{2,1,0:T(8,128)} %inv.3) | copy-start | bytes 442372
  12.5 3.5 %copy-start.6 = (s32[4,6]{1,0:T(4,128)S(1)}, s32[4,6]{1,0:T(4,128)}, u32[]{:S(2)}) copy-start(s32[4,6]{1,0:T(4,128)} %split_ref.7) | copy-start | bytes 292
  12.7 15.5 %collective-permute-start.4 = (f32[304,256]{1,0:T(8,128)S(1)}, f32[304,256]{1,0:T(8,128)S(1)}, u32[]{:S(2)}, u32[]{:S(2)}) collective-permute-start(f32[304,256]{1,0:T(8,128)S(1)} %get-tuple-element.52), channel_id=1, source_target_pairs={{0,4},{4,0},{8,12},{12,8},{16,20},{20,16},{24,28},{28,24},{1,5},{5... | collective-permute-start | bytes 933896 | tf_op jit(solution)/shard_map/ppermute | solution.py:47
  15.2 12.9 %collective-permute-start.5 = (f32[304,256]{1,0:T(8,128)S(1)}, f32[304,256]{1,0:T(8,128)S(1)}, u32[]{:S(2)}, u32[]{:S(2)}) collective-permute-start(f32[304,256]{1,0:T(8,128)S(1)} %get-tuple-element.53), channel_id=1, source_target_pairs={{4,8},{8,4},{12,16},{16,12},{20,24},{24,20},{5,9},{9,5},{13,17},{1... | collective-permute-start | bytes 933896 | tf_op jit(solution)/shard_map/ppermute | solution.py:47
  23.2 24.2 %collective-permute-start.2 = (f32[72,256]{1,0:T(8,128)S(1)}, f32[72,256]{1,0:T(8,128)S(1)}, u32[]{:S(2)}, u32[]{:S(2)}) collective-permute-start(f32[72,256]{1,0:T(8,128)S(1)} %get-tuple-element.50), channel_id=1, source_target_pairs={{0,4},{4,0},{8,12},{12,8},{16,20},{20,16},{24,28},{28,24},{1,5},{5... | collective-permute-start | bytes 221192 | tf_op jit(solution)/shard_map/ppermute | solution.py:47
  27.5 19.9 %collective-permute-start.3 = (f32[72,256]{1,0:T(8,128)S(1)}, f32[72,256]{1,0:T(8,128)S(1)}, u32[]{:S(2)}, u32[]{:S(2)}) collective-permute-start(f32[72,256]{1,0:T(8,128)S(1)} %get-tuple-element.51), channel_id=1, source_target_pairs={{4,8},{8,4},{12,16},{16,12},{20,24},{24,20},{5,9},{9,5},{13,17},{1... | collective-permute-start | bytes 221192 | tf_op jit(solution)/shard_map/ppermute | solution.py:47
  28.2 19.2 %copy-start.4 = (f32[32,48,256]{2,1,0:T(8,128)S(1)}, f32[32,48,256]{2,1,0:T(8,128)}, u32[]{:S(2)}) copy-start(f32[32,48,256]{2,1,0:T(8,128)} %copy-done.3) | copy-start | bytes 4718596

commit v5 on v4

--- a/solution.py
+++ b/solution.py
@@ -443,8 +443,9 @@
     def after(self, x, k):
         return self.fx(x, k) * self.one(x + 1, k)
 
-    def outermost(self, x):
-        return False
+    def faces_x(self, x, k):
+        ex = self.fx(x, k)
+        return ex, ex * (self.ff(x, k) + self.ff(x + 1, k))
 
 
 def second_row(o, x, s, put):
@@ -466,10 +467,8 @@
 
 def x_flux(o, x, k, two):
     step = two(x + 1, k) - two(x, k)
-    ex = o.fx(x, k)
-    if o.outermost(x):
-        return ex * step, jnp.zeros_like(step)
-    return ex * step, ex * (o.ff(x, k) + o.ff(x + 1, k)) * step
+    ex, wx = o.faces_x(x, k)
+    return ex * step, wx * step
 
 
 def flux_row(o, x, s, lane, two, res, own_diag, split, carried, put):
@@ -501,12 +500,16 @@
         dz = z_next(p) - p
         ez_before, wz_before, dz_before = z_prev(ez), z_prev(wz), z_prev(dz)
         qx, sx = x_flux(o, x, k, two)
-        gained = (qx - carried[0, here, :]) + (ey * dy - ey_before * dy_before)
+        if carried is None:
+            qx_before, sx_before = x_flux(o, x - 1, k, two)
+        else:
+            qx_before, sx_before = carried[0, here, :], carried[1, here, :]
+            carried[0, here, :] = qx
+            carried[1, here, :] = sx
+        gained = (qx - qx_before) + (ey * dy - ey_before * dy_before)
         gained = gained + (ez * dz - ez_before * dz_before)
-        weighed = (sx - carried[1, here, :]) + (wy * dy - wy_before * dy_before)
+        weighed = (sx - sx_before) + (wy * dy - wy_before * dy_before)
         weighed = weighed + (wz * dz - wz_before * dz_before)
-        carried[0, here, :] = qx
-        carried[1, here, :] = sx
         rest = o.rhs(x, k) - own_diag[x, here, :] * p + gained
         below = lane < split(k)
         put(
@@ -614,9 +617,6 @@
     def fz(self, x, k):
         return self.planes.field(4, k, self.far[x]) if x in self.far else super().fz(x, k)
 
-    def outermost(self, x):
-        return x in (-1, self.n - 1)
-
     def gain(self, x, k):
         return self.gain_edge[self.slots[x], group(k), :] if x in self.slots else super().gain(x, k)
 
@@ -631,8 +631,9 @@
 
 
 def edge_kernel(split_ref, res, mask, ff, rhs, own_diag, tot, gain, one, fx, fy, fz, ynear, yfar, xnear, xfar,
-                tot3, gain3, one3, six, end, two, acc,
-                sent, edge_flux, edge_fx, edge_step, one_edge, gain_edge, two_edge, carried, total_acc):
+                tot3, gain3, one3, six, end, two, acc, *others):
+    flux = others[FLUXES : 2 * FLUXES]
+    sent, edge_fx, edge_step, one_edge, gain_edge, two_edge, near_fx, total_acc = others[2 * FLUXES :]
     n, own, wide = mask.shape
     groups = own // 8
     s, lane = places(wide)
@@ -644,32 +645,56 @@
         return ghosts.active(0) if k == groups else mask[0, group(k), :].astype(F32)
 
     o.beyond(n, planes, act, tot, tot3, one_edge, gain_edge, edge_fx)
-    slots = {x: slot for slot, x in enumerate((-1, 0, 1, n - 2, n - 1, n))}
-    for x, slot in slots.items():
-
-        def put_two(k, v, slot=slot):
-            two_edge[slot, group(k), :] = v
-
-        second_row(o, x, s, put_two)
-
-    def two_of(x, k):
-        return two_edge[slots[x], group(k), :] if x in slots else two[x, group(k), :]
-
+    depth = 5
+    bases = (-1, n - depth + 1)
+    for side, base in enumerate(bases):
+        for r in range(depth):
+            x, slot = base + r, depth * side + r
+            if x in (-1, 0, 1, n - 2, n - 1, n):
+
+                def put_two(k, v, slot=slot):
+                    two_edge[slot, group(k), :] = v
+
+                second_row(o, x, s, put_two)
+            else:
+                two_edge[slot] = two[x]
+            if x == n:
+                continue
+            for k in range(groups):
+                ex = o.fx(x, k)
+                near_fx[0, slot, group(k), :] = ex
+                if x in (-1, n - 1):
+                    near_fx[1, slot, group(k), :] = jnp.zeros_like(ex)
+                else:
+                    near_fx[1, slot, group(k), :] = ex * (o.ff(x, k) + o.ff(x + 1, k))
     for k in range(groups):
-        edge_step[0, group(k), :] = two_of(0, k) - two_of(-1, k)
-        edge_step[1, group(k), :] = two_of(n, k) - two_of(n - 1, k)
+        edge_step[0, group(k), :] = two_edge[1, group(k), :] - two_edge[0, group(k), :]
+        edge_step[1, group(k), :] = two_edge[2 * depth - 1, group(k), :] - two_edge[2 * depth - 2, group(k), :]
     total_acc[...] = acc[...]
-    for slot, x in enumerate((0, 1, 2, n - 3, n - 2, n - 1)):
-        if slot % 3 == 0:
-            for k in range(groups):
-                carried[0, group(k), :], carried[1, group(k), :] = x_flux(o, x - 1, k, two_of)
-
-        def put(k, rest, *values, x=x, slot=slot):
+    plain = Inside(groups, ff, rhs, gain, one, fx, fy, fz, gain3, one3, six, end)
+
+    def row(r, carry):
+        high = r >= depth - 2
+        x = jnp.where(high, n - 2 * (depth - 2) + r, r)
+        shift = jnp.where(high, depth - bases[1], -bases[0])
+
+        def two_of(x, k):
+            return two_edge[x + shift, group(k), :]
+
+        def faces_x(x, k):
+            return near_fx[0, x + shift, group(k), :], near_fx[1, x + shift, group(k), :]
+
+        plain.faces_x = faces_x
+
+        def put(k, rest, *values):
             total_acc[x // 8, group(k), :] += rest
             for f, v in enumerate(values):
-                edge_flux[f, slot, group(k), :] = v
-
-        flux_row(o, x, s, lane, two_of, res, own_diag, lambda k, x=x: split_ref[x // 8, k], carried, put)
+                flux[f][x, group(k), :] = v
+
+        flux_row(plain, x, s, lane, two_of, res, own_diag, lambda k: split_ref[x // 8, k], None, put)
+        return carry
+
+    lax.fori_loop(0, 2 * (depth - 2), row, 0, unroll=2)
 
     rows_b, cols_b = split_ref.shape
     lane = lax.broadcasted_iota(jnp.int32, (1, wide), 1)
@@ -690,10 +715,10 @@
     sent[...] = jnp.broadcast_to(jnp.sum(laid, axis=0, keepdims=True), sent.shape)
 
 
-def final_kernel(tiles_y, split_ref, frac, inv, ynear, yfar, xnear, xfar, fx, edge_flux, edge_fx, edge_step,
+def final_kernel(tiles_y, split_ref, frac, inv, ynear, yfar, xnear, xfar, fx, edge_fx, edge_step,
                  al0, al1, be0, be1, got, *rest):
     flux = rest[:FLUXES]
-    out, coarse, step_y, step_z, held, sems = rest[FLUXES:]
+    out, coarse, step_y, step_z, across, held, sems = rest[FLUXES:]
     i, j = lax.axis_index("gx"), lax.axis_index("gy")
     n, own, wide = frac.shape
     ext = own + G
@@ -764,77 +789,56 @@
             k = skip + 2 * r
             coarse[at, group(r), :] = jnp.where(one_of(below, r) > 0.5, one_of(e, k), one_of(e, k + 1))
 
-    def solved(x, q, values, beside):
+    for q in range(rows_b + 1):
+        x = 8 * q - 1
         for r in range(cols_b):
             here = group(r)
-            u, v, wy, sy, wz, sz = (value(r) for value in values)
+            ex = edge_fx[0, here, :] if q == 0 else edge_fx[1, here, :] if q == rows_b else fx[x, here, :]
+            f_before = planes.rows(8 * r, 8, 0) if q == 0 else frac[x, here, :]
+            f_after = planes.rows(8 * r, 8, 1) if q == rows_b else frac[x + 1, here, :]
+            step = coarse[q + 1, here, :] - coarse[q, here, :]
+            across[0, q, here, :] = ex * step
+            if q in (0, rows_b):
+                step = step + edge_step[0 if q == 0 else 1, here, :]
+            across[1, q, here, :] = ex * (0.5 * (f_before + f_after)) * step
+
+    def solved(x, q, beside=None, sign=None):
+        for r in range(cols_b):
+            here = group(r)
+            u, v, wy, sy, wz, sz = (ref[x, here, :] for ref in flux)
             along_y, along_z = step_y[q, here, :], step_z[q, here, :]
             u = u + (wy * along_y + wz * along_z)
-            weighed = sy * along_y + sz * along_z
+            v = v + 0.5 * (sy * along_y + sz * along_z)
             if beside is not None:
-                ex, sx, step, sweep_step = beside(r)
-                u = u + ex * step
-                weighed = weighed + sx * (step + sweep_step)
-            v = v + 0.5 * weighed
+                u = sign(u, across[0, beside, here, :])
+                v = sign(v, across[1, beside, here, :])
             held[0, x, here, :] = al0[x, here, :] * u - al1[x, here, :] * v
             held[1, x, here, :] = be0[x, here, :] * v - be1[x, here, :] * u
 
     def copies(q):
         return [
             pltpu.make_async_copy(
-                held.at[k, pl.ds(8 * q, 8)], out.at[k, pl.ds(8 * q, 8)], sems.at[k, q]
+                held.at[k, pl.ds(4 * q, 4)], out.at[k, pl.ds(4 * q, 4)], sems.at[k, q]
             )
             for k in range(2)
         ]
 
-    def frac_of(x, r):
-        if x in (-1, n):
-            return planes.rows(8 * r, 8, 0 if x == -1 else 1)
-        return frac[x, group(r), :]
-
-    def face(x, r):
-        if x in (-1, n - 1):
-            ex = edge_fx[0 if x == -1 else 1, group(r), :]
-        else:
-            ex = fx[x, group(r), :]
-        return ex, ex * (frac_of(x, r) + frac_of(x + 1, r))
-
-    outer = {x: slot for slot, x in enumerate((0, 1, 2, n - 3, n - 2, n - 1))}
-
-    def values_of(x):
-        if isinstance(x, int) and x in outer:
-            return [lambda r, f=f: edge_flux[f, outer[x], group(r), :] for f in range(FLUXES)]
-        return [lambda r, f=f: flux[f][x, group(r), :] for f in range(FLUXES)]
-
-    for q in range(rows_b):
-        first, last = 8 * q, 8 * q + 7
-
-        def ahead(r, q=q, last=last):
-            more = edge_step[1, group(r), :] if last == n - 1 else 0.0
-            return *face(last, r), coarse[q + 2, group(r), :] - coarse[q + 1, group(r), :], more
-
-        def behind(r, q=q, first=first):
-            more = -edge_step[0, group(r), :] if first == 0 else 0.0
-            return *face(first - 1, r), coarse[q, group(r), :] - coarse[q + 1, group(r), :], more
-
-        solved(first, q, values_of(first), behind)
-        start, stop = first + 1, last
-        while start in outer:
-            solved(start, q, values_of(start), None)
-            start += 1
-        while stop - 1 in outer:
-            stop -= 1
-            solved(stop, q, values_of(stop), None)
-
-        def row(x, carry, q=q):
-            solved(x, q, values_of(x), None)
-            return carry
-
-        lax.fori_loop(start, stop, row, 0, unroll=3 if (stop - start) % 3 == 0 else 1)
-        solved(last, q, values_of(last), ahead)
-        for copy in copies(q):
+    def block(q, carry):
+        x = 8 * q
+        solved(x, q, q, jnp.subtract)
+        for k in range(1, 4):
+            solved(x + k, q)
+        for copy in copies(2 * q):
             copy.start()
-    for q in range(rows_b):
+        for k in range(4, 7):
+            solved(x + k, q)
+        solved(x + 7, q, q + 1, jnp.add)
+        for copy in copies(2 * q + 1):
+            copy.start()
+        return carry
+
+    lax.fori_loop(0, rows_b, block, 0)
+    for q in range(2 * rows_b):
         for copy in copies(q):
             copy.wait()
 
@@ -915,43 +919,45 @@
 
     devices = tiles_x * tiles_y
     span = pl.cdiv(unknowns, 128) * 128
-    sent, edge_flux, edge_fx, edge_step = pl.pallas_call(
+    *flux, sent, edge_fx, edge_step = pl.pallas_call(
         edge_kernel,
-        in_specs=[SCALARS] + [WHOLE] * 22,
-        out_specs=[WHOLE] * 4,
-        out_shape=[
+        in_specs=[SCALARS] + [WHOLE] * (22 + FLUXES),
+        out_specs=[WHOLE] * (3 + FLUXES),
+        out_shape=[array(n, own, wide)] * FLUXES
+        + [
             array(devices, span),
-            array(FLUXES, 6, own, wide),
             array(2, ext, wide),
             array(2, own, wide),
         ],
         scratch_shapes=[
             pltpu.VMEM((4, ext, wide), F32),
             pltpu.VMEM((4, ext, wide), F32),
-            pltpu.VMEM((6, ext, wide), F32),
-            pltpu.VMEM((2, own, wide), F32),
+            pltpu.VMEM((10, ext, wide), F32),
+            pltpu.VMEM((2, 10, own, wide), F32),
             pltpu.VMEM((n // 8, own, wide), F32),
         ],
+        input_output_aliases={23 + f: f for f in range(FLUXES)},
         compiler_params=params(8),
         name="edges",
-    )(split_layer, *shared, xnear, xfar, tot3, gain3, one3, six, end, two, acc)
+    )(split_layer, *shared, xnear, xfar, tot3, gain3, one3, six, end, two, acc, *flux)
     got = lax.all_to_all(sent, ("gx", "gy"), 0, 0, tiled=True)
 
     return pl.pallas_call(
         functools.partial(final_kernel, tiles_y),
-        in_specs=[SCALARS] + [WHOLE] * (15 + FLUXES),
+        in_specs=[SCALARS] + [WHOLE] * (14 + FLUXES),
         out_specs=pl.BlockSpec(memory_space=pl.ANY),
         out_shape=array(2, n, own, wide),
         scratch_shapes=[
             pltpu.VMEM((n // 8 + 2, ext, wide), F32),
             pltpu.VMEM((n // 8, own, wide), F32),
             pltpu.VMEM((n // 8, own, wide), F32),
+            pltpu.VMEM((2, n // 8 + 1, own, wide), F32),
             pltpu.VMEM((2, n, own, wide), F32),
-            pltpu.SemaphoreType.DMA((2, n // 8)),
+            pltpu.SemaphoreType.DMA((2, n // 4)),
         ],
         compiler_params=params(12),
         name="final",
-    )(split_layer, frac_flow, coarse_inverse, ynear, yfar, late_near, late_far, fx, edge_flux, edge_fx,
+    )(split_layer, frac_flow, coarse_inverse, ynear, yfar, late_near, late_far, fx, edge_fx,
       edge_step, al0, al1, be0, be1, got, *flux)
 
 

time: 50.7 us -> 49.3 us (0.972)
  Pallas kernels: 23.6 us -> 22.2 us
  blocking collectives: 15.9 us -> 17.1 us
  local copies, waits for them, and re-layouts: 1.21 us -> 0.07 us
    unnamed x15 -> x11, local copies, waits for them, and re-layouts: 1.18 us -> 0.03 us
    all_to_all x1, blocking collectives: 15.9 us -> 17.1 us  [shards(): got = lax.all_to_all(sent, ('gx', 'gy'), 0, 0, tiled=True)]
    pallas_call x1, Pallas kernels: 3.18 us -> 2.13 us  [shards(): pl.pallas_call(edge_kernel, in_specs=[SCALARS] + [WHOLE] * (22 + FLUXES),...]
  transfers between devices with their start and end apart: 6 -> 6, of which waited for: 0 -> 0; matrix products, arithmetic and copies ran while one was open for 0% -> 0% of each run, Pallas kernels for 33% -> 32%
where the time goes in v5:
time: 49.3 us; the launch traced here: 49.1 us
  Pallas kernels  22.2 us (45%)
  blocking collectives  17.1 us (35%)
  starting transfers between devices  9.56 us (19%)
    all_to_all x1, blocking collectives, shards(): got = lax.all_to_all(sent, ('gx', 'gy'), 0, 0, tiled=True)  17.1 us
    ppermute x3, starting transfers between devices, swap(): lax.ppermute(message[0], axis, near)  7.43 us
    pallas_call x1, Pallas kernels, shards(): pl.pallas_call(interior_kernel, in_specs=[SCALARS] + [WHOLE] * 14, out_sp...  7.2 us
    pallas_call x1, Pallas kernels, shards(): pl.pallas_call(prep_kernel, in_specs=[pl.BlockSpec(memory_space=pltpu.HBM...  6.34 us
    pallas_call x1, Pallas kernels, shards(): pl.pallas_call(y_message_kernel, grid=(n // 8,), in_specs=[pl.BlockSpec(s...  3.57 us
    pallas_call x1, Pallas kernels, shards(): pl.pallas_call(functools.partial(final_kernel, tiles_y), in_specs=[SCALAR...  2.78 us
    ppermute x3, starting transfers between devices, swap(): lax.ppermute(message[1], axis, far)  2.14 us
    pallas_call x1, Pallas kernels, shards(): pl.pallas_call(edge_kernel, in_specs=[SCALARS] + [WHOLE] * (22 + FLUXES),...  2.13 us
  transfers between devices with their start and end apart: 6, of which 0 were waited for; matrix products, arithmetic and copies ran while one was open for 0% of the time, Pallas kernels for 32%

profile of v5, /device:TPU:0, one launch (start us, length us, event | category | flops | bytes accessed | tf_op | source)
XLA Modules:
  0.0 49.1 jit_solution(14095843480231793356)
XLA Ops:
  0.0 3.6 %y_messages.1 = (f32[32,16,256]{2,1,0:T(8,128)S(1)}, f32[32,16,256]{2,1,0:T(8,128)S(1)}) custom-call(s32[4,6]{1,0:T(4,128)} %split_ref.7, f32[2,32,48,256]{3,2,1,0:T(8,128)} %res.3, f32[2,32,48,256]{3,2,1,0:T(8,128)} %diag_hbm.1, f32[2,32,48,256]{3,2,1,0:T(8,128)} %crs_hbm.1, s32[32,48,256]{2,1,0:T(8,128)} %mask.5, f32[32,48,256]{2,1,0:T(8,128)} %tx_hbm.1, ...), custom_call_target="tpu_custom_call" | custom-call | tf_op jit(solution)/shard_map/y_messages/pallas_call | solution.py:863
  3.6 0.5 %collective-permute-start = (f32[32,16,256]{2,1,0:T(8,128)S(1)}, f32[32,16,256]{2,1,0:T(8,128)S(1)}, u32[]{:S(2)}, u32[]{:S(2)}) collective-permute-start(f32[32,16,256]{2,1,0:T(8,128)S(1)} %get-tuple-element.45), channel_id=1, source_target_pairs={{0,1},{1,0},{2,3},{3,2},{4,5},{5,4},{6,7},{7,6},{8,9},{9,8},{10,11... | collective-permute-start | bytes 1572872 | tf_op jit(solution)/shard_map/ppermute | solution.py:47
  4.1 0.0 copy-start.1
  4.1 0.8 %collective-permute-start.1 = (f32[32,16,256]{2,1,0:T(8,128)S(1)}, f32[32,16,256]{2,1,0:T(8,128)S(1)}, u32[]{:S(2)}, u32[]{:S(2)}) collective-permute-start(f32[32,16,256]{2,1,0:T(8,128)S(1)} %get-tuple-element.46), channel_id=1, source_target_pairs={{1,2},{2,1},{5,6},{6,5},{9,10},{10,9},{13,14},{14,13},{17,18},{18,... | collective-permute-start | bytes 1572872 | tf_op jit(solution)/shard_map/ppermute | solution.py:47
  4.9 6.3 %prep.1 = (f32[32,48,256]{2,1,0:T(8,128)S(1)}, f32[32,48,256]{2,1,0:T(8,128)S(1)}, f32[32,48,256]{2,1,0:T(8,128)S(1)}, f32[32,48,256]{2,1,0:T(8,128)S(1)}, f32[3...) custom-call(f32[2,32,48,256]{3,2,1,0:T(8,128)} %res.3, ...), custom_call_target="tpu_custom_call" | custom-call | flops 60000000 | bytes 30000000 | tf_op jit(solution)/shard_map/prep/pallas_call | solution.py:876
  11.3 0.0 collective-permute-done.ynear
  11.3 0.0 collective-permute-done.1.yfar
  11.3 0.0 copy-done.1
  11.3 0.0 copy-start
  11.3 0.0 copy-start.2
  11.3 0.0 copy-start.3
  11.3 0.0 copy-start.4
  11.4 0.2 x_messages.1
  11.5 2.6 %collective-permute-start.4 = (f32[304,256]{1,0:T(8,128)S(1)}, f32[304,256]{1,0:T(8,128)S(1)}, u32[]{:S(2)}, u32[]{:S(2)}) collective-permute-start(f32[304,256]{1,0:T(8,128)S(1)} %get-tuple-element.57), channel_id=1, source_target_pairs={{0,4},{4,0},{8,12},{12,8},{16,20},{20,16},{24,28},{28,24},{1,5},{5... | collective-permute-start | bytes 933896 | tf_op jit(solution)/shard_map/ppermute | solution.py:47
  14.1 0.7 %collective-permute-start.5 = (f32[304,256]{1,0:T(8,128)S(1)}, f32[304,256]{1,0:T(8,128)S(1)}, u32[]{:S(2)}, u32[]{:S(2)}) collective-permute-start(f32[304,256]{1,0:T(8,128)S(1)} %get-tuple-element.58), channel_id=1, source_target_pairs={{4,8},{8,4},{12,16},{16,12},{20,24},{24,20},{5,9},{9,5},{13,17},{1... | collective-permute-start | bytes 933896 | tf_op jit(solution)/shard_map/ppermute | solution.py:47
  14.8 0.0 copy-done
  14.8 0.0 copy-done.2
  14.8 0.0 copy-done.3
  14.8 0.0 copy-done.4
  14.8 7.2 %interior.1 = (f32[72,256]{1,0:T(8,128)S(1)}, f32[72,256]{1,0:T(8,128)S(1)}, f32[32,24,256]{2,1,0:T(8,128)S(1)}, f32[32,24,256]{2,1,0:T(8,128)S(1)}, f32[32,24,2...) custom-call(s32[4,6]{1,0:T(4,128)S(1)} %copy-done.4, ...), custom_call_target="tpu_custom_call" | custom-call | flops 60000000 | bytes 30000000 | tf_op jit(solution)/shard_map/interior/pallas_call | solution.py:900
  22.0 4.3 %collective-permute-start.2 = (f32[72,256]{1,0:T(8,128)S(1)}, f32[72,256]{1,0:T(8,128)S(1)}, u32[]{:S(2)}, u32[]{:S(2)}) collective-permute-start(f32[72,256]{1,0:T(8,128)S(1)} %get-tuple-element.55), channel_id=1, source_target_pairs={{0,4},{4,0},{8,12},{12,8},{16,20},{20,16},{24,28},{28,24},{1,5},{5... | collective-permute-start | bytes 221192 | tf_op jit(solution)/shard_map/ppermute | solution.py:47
  26.4 0.7 %collective-permute-start.3 = (f32[72,256]{1,0:T(8,128)S(1)}, f32[72,256]{1,0:T(8,128)S(1)}, u32[]{:S(2)}, u32[]{:S(2)}) collective-permute-start(f32[72,256]{1,0:T(8,128)S(1)} %get-tuple-element.56), channel_id=1, source_target_pairs={{4,8},{8,4},{12,16},{16,12},{20,24},{24,20},{5,9},{9,5},{13,17},{1... | collective-permute-start | bytes 221192 | tf_op jit(solution)/shard_map/ppermute | solution.py:47
  27.0 0.0 collective-permute-done.4.xnear
  27.0 0.0 collective-permute-done.5.xfar
  27.0 2.1 %edges.1 = (f32[32,48,256]{2,1,0:T(8,128)S(1)}, f32[32,48,256]{2,1,0:T(8,128)S(1)}, f32[32,48,256]{2,1,0:T(8,128)S(1)}, f32[32,48,256]{2,1,0:T(8,128)S(1)}, f32[...) custom-call(s32[4,6]{1,0:T(4,128)S(1)} %copy-done.4, ...), custom_call_target="tpu_custom_call", output_to_operand_aliasing={{0}: (23, {}), {1}: (24, {}), {2}: (25, {}), {3}: (26, {}),... | custom-call | tf_op jit(solution)/shard_map/edges/pallas_call | solution.py:922
  29.2 17.1 %all_to_all.11 = f32[32,1,256]{2,1,0:T(1,128)S(1)} all-to-all(f32[32,1,256]{2,1,0:T(1,128)S(1)} %copy.17), channel_id=1, replica_groups=mesh['gx'=8,'gy'=4] {'gx','gy'}, dimensions={0} | all-to-all | bytes 65536 | tf_op jit(solution)/shard_map/all_to_all | solution.py:943
  46.3 0.0 collective-permute-done.2.xnear
  46.3 0.0 collective-permute-done.3.xfar
  46.3 2.8 %final.1 = f32[2,32,48,256]{3,2,1,0:T(8,128)} custom-call(s32[4,6]{1,0:T(4,128)S(1)} %copy-done.4, f32[32,48,256]{2,1,0:T(8,128)S(1)} %copy-done.2, f32[1,192,192]{2,1,0:T(8,128)S(1)} %copy-done.3, f32[32,16,256]{2,1,0:T(8,128)S(1)} %collective-permute-done.ynear, f32[32,16,256]{2,1,0:T(8,128)S(1)} %collective-permute-done.1.yfar, ...), custom_call_target="tpu_custom_call" | custom-call | tf_op jit(solution)/shard_map/final/pallas_call | solution.py:945
  (2 shorter events, 0.0 us)
Async XLA Ops:
  3.6 7.7 %collective-permute-start = (f32[32,16,256]{2,1,0:T(8,128)S(1)}, f32[32,16,256]{2,1,0:T(8,128)S(1)}, u32[]{:S(2)}, u32[]{:S(2)}) collective-permute-start(f32[32,16,256]{2,1,0:T(8,128)S(1)} %get-tuple-element.45), channel_id=1, source_target_pairs={{0,1},{1,0},{2,3},{3,2},{4,5},{5,4},{6,7},{7,6},{8,9},{9,8},{10,11... | collective-permute-start | bytes 1572872 | tf_op jit(solution)/shard_map/ppermute | solution.py:47
  4.1 7.2 %copy-start.1 = (s32[32,48,256]{2,1,0:T(8,128)S(1)}, s32[32,48,256]{2,1,0:T(8,128)}, u32[]{:S(2)}) copy-start(s32[32,48,256]{2,1,0:T(8,128)} %mask.5) | copy-start | bytes 4718596
  4.1 7.2 %collective-permute-start.1 = (f32[32,16,256]{2,1,0:T(8,128)S(1)}, f32[32,16,256]{2,1,0:T(8,128)S(1)}, u32[]{:S(2)}, u32[]{:S(2)}) collective-permute-start(f32[32,16,256]{2,1,0:T(8,128)S(1)} %get-tuple-element.46), channel_id=1, source_target_pairs={{1,2},{2,1},{5,6},{6,5},{9,10},{10,9},{13,14},{14,13},{17,18},{18,... | collective-permute-start | bytes 1572872 | tf_op jit(solution)/shard_map/ppermute | solution.py:47
  11.3 3.5 %copy-start = (f32[2,32,48,256]{3,2,1,0:T(8,128)S(1)}, f32[2,32,48,256]{3,2,1,0:T(8,128)}, u32[]{:S(2)}) copy-start(f32[2,32,48,256]{3,2,1,0:T(8,128)} %res.3) | copy-start | bytes 9437188
  11.3 3.5 %copy-start.2 = (f32[32,48,256]{2,1,0:T(8,128)S(1)}, f32[32,48,256]{2,1,0:T(8,128)}, u32[]{:S(2)}) copy-start(f32[32,48,256]{2,1,0:T(8,128)} %frac.1) | copy-start | bytes 4718596
  11.3 3.5 %copy-start.3 = (f32[1,192,192]{2,1,0:T(8,128)S(1)}, f32[1,192,192]{2,1,0:T(8,128)}, u32[]{:S(2)}) copy-start(f32[1,192,192]{2,1,0:T(8,128)} %inv.3) | copy-start | bytes 442372
  11.3 3.5 %copy-start.4 = (s32[4,6]{1,0:T(4,128)S(1)}, s32[4,6]{1,0:T(4,128)}, u32[]{:S(2)}) copy-start(s32[4,6]{1,0:T(4,128)} %split_ref.7) | copy-start | bytes 292
  11.5 15.5 %collective-permute-start.4 = (f32[304,256]{1,0:T(8,128)S(1)}, f32[304,256]{1,0:T(8,128)S(1)}, u32[]{:S(2)}, u32[]{:S(2)}) collective-permute-start(f32[304,256]{1,0:T(8,128)S(1)} %get-tuple-element.57), channel_id=1, source_target_pairs={{0,4},{4,0},{8,12},{12,8},{16,20},{20,16},{24,28},{28,24},{1,5},{5... | collective-permute-start | bytes 933896 | tf_op jit(solution)/shard_map/ppermute | solution.py:47
  14.1 12.9 %collective-permute-start.5 = (f32[304,256]{1,0:T(8,128)S(1)}, f32[304,256]{1,0:T(8,128)S(1)}, u32[]{:S(2)}, u32[]{:S(2)}) collective-permute-start(f32[304,256]{1,0:T(8,128)S(1)} %get-tuple-element.58), channel_id=1, source_target_pairs={{4,8},{8,4},{12,16},{16,12},{20,24},{24,20},{5,9},{9,5},{13,17},{1... | collective-permute-start | bytes 933896 | tf_op jit(solution)/shard_map/ppermute | solution.py:47
  22.0 24.3 %collective-permute-start.2 = (f32[72,256]{1,0:T(8,128)S(1)}, f32[72,256]{1,0:T(8,128)S(1)}, u32[]{:S(2)}, u32[]{:S(2)}) collective-permute-start(f32[72,256]{1,0:T(8,128)S(1)} %get-tuple-element.55), channel_id=1, source_target_pairs={{0,4},{4,0},{8,12},{12,8},{16,20},{20,16},{24,28},{28,24},{1,5},{5... | collective-permute-start | bytes 221192 | tf_op jit(solution)/shard_map/ppermute | solution.py:47
  26.4 19.9 %collective-permute-start.3 = (f32[72,256]{1,0:T(8,128)S(1)}, f32[72,256]{1,0:T(8,128)S(1)}, u32[]{:S(2)}, u32[]{:S(2)}) collective-permute-start(f32[72,256]{1,0:T(8,128)S(1)} %get-tuple-element.56), channel_id=1, source_target_pairs={{4,8},{8,4},{12,16},{16,12},{20,24},{24,20},{5,9},{9,5},{13,17},{1... | collective-permute-start | bytes 221192 | tf_op jit(solution)/shard_map/ppermute | solution.py:47

commit v6 on v5

--- a/solution.py
+++ b/solution.py
@@ -47,92 +47,6 @@
     return lax.ppermute(message[0], axis, near), lax.ppermute(message[1], axis, far)
 
 
-def y_message_kernel(split_ref, *refs):
-    low, high = refs[:8], refs[8:16]
-    near_ref, far_ref = refs[16:]
-    even = lax.rem(lax.axis_index("gy"), 2) == 0
-    step = pl.program_id(0)
-
-    def fields(group):
-        res, diag, crs, mask, tx, ty, tz, ff = group
-        active = mask[...].astype(F32)
-        b, c = quasi_impes(active, res[0], res[1], diag[0], diag[1], crs[0], crs[1])
-        return active, b, c, tx[...], ty[...], tz[...], ff[...]
-
-    shape = low[3].shape
-    s = lax.broadcasted_iota(jnp.int32, shape, 1)
-    lane = lax.broadcasted_iota(jnp.int32, shape, 2)
-
-    def turn(v, k):
-        return jnp.stack([pltpu.roll(v[i], k, 0) for i in range(v.shape[0])])
-
-    a, b, c, tx, ty, tz, ff = fields(high)
-    splits = split_ref[pl.ds(step, 1), :]
-    lower = (lane < splits[:, -1:].reshape(1, 1, 1)).astype(F32)
-    up = (
-        jnp.where(s >= 5, a, jnp.where(s >= 2, turn(ty, 5), turn(tx, 2))),
-        jnp.where(
-            s >= 6,
-            b,
-            jnp.where(
-                s >= 4,
-                turn(c, 6),
-                jnp.where(s >= 2, turn(tz, 4), jnp.where(s == 1, turn(ff, 2), lower)),
-            ),
-        ),
-    )
-    a, b, c, tx, ty, tz, ff = fields(low)
-    lower = (lane < splits[:, :1].reshape(1, 1, 1)).astype(F32)
-    down = (
-        jnp.where(s < 3, a, jnp.where(s < 6, turn(ty, 3), turn(tx, 6))),
-        jnp.where(
-            s < 2,
-            b,
-            jnp.where(
-                s < 4,
-                turn(c, 2),
-                jnp.where(s < 6, turn(tz, 4), jnp.where(s == 6, turn(ff, 6), lower)),
-            ),
-        ),
-    )
-    for k in range(2):
-        near_ref[:, 8 * k : 8 * k + 8, :] = jnp.where(even, up[k], down[k])
-        far_ref[:, 8 * k : 8 * k + 8, :] = jnp.where(even, down[k], up[k])
-
-
-class Ghosts:
-    def __init__(self, near_ref, far_ref):
-        self.refs = near_ref, far_ref
-        self.even = lax.rem(lax.axis_index("gy"), 2) == 0
-
-    def tiles(self, x, k):
-        near, far = (ref[x, 8 * k : 8 * k + 8, :] for ref in self.refs)
-        return jnp.where(self.even, near, far), jnp.where(self.even, far, near)
-
-    def pick(self, tiles, high_turn, low_turn, rings):
-        high, low = tiles
-        s = lax.broadcasted_iota(jnp.int32, high.shape, 0)
-        high = pltpu.roll(high, high_turn, 0) if high_turn else high
-        low = pltpu.roll(low, low_turn, 0) if low_turn else low
-        return jnp.where(s < rings, high, jnp.where(s >= G - rings, low, 0.0))
-
-    def first(self, x):
-        t = self.tiles(x, 0)
-        return self.pick(t, 0, 0, 3), self.pick(t, 2, 6, 2), self.pick(t, 5, 3, 3)
-
-    def second(self, x):
-        t = self.tiles(x, 1)
-        c = jnp.maximum(self.pick(t, 6, 2, 2), 1.0)
-        return self.pick(t, 0, 0, 2), c, self.pick(t, 4, 4, 2)
-
-    def active(self, x):
-        return self.pick(self.tiles(x, 0), 0, 0, 3)
-
-    def frac_and_lower(self, x):
-        t = self.tiles(x, 1)
-        return self.pick(t, 2, 6, 1), self.pick(t, 1, 7, 1)
-
-
 def group(k):
     return slice(8 * k, 8 * k + 8)
 
@@ -162,9 +76,161 @@
     return jnp.where(lane < a.shape[1] - 1, tz * a * z_next(a), 0.0)
 
 
-def prep_kernel(res_hbm, diag_hbm, crs_hbm, mask_hbm, tx_hbm, ty_hbm, tz_hbm,
+Y_TURNS = {
+    "c": (6, 2),
+    "a": (4, 4),
+    "tx": (3, 5),
+    "e": (3, 6),
+    "tz": (1, 7),
+}
+Y_PLACES = {
+    "c": ((4, 5), (2, 3)),
+    "a": ((3,), (4,)),
+    "tx": ((2,), (5,)),
+    "e": ((1,), (6,)),
+    "tz": ((0,), (7,)),
+}
+
+
+def y_message_kernel(split_ref, *refs):
+    far, (near_ref, far_ref) = refs[:8], refs[8:10]
+    low, high, sems = refs[10:18], refs[18:26], refs[26]
+    n, _, wide = low[3].shape
+    own = far[3].shape[1]
+    even = lax.rem(lax.axis_index("gy"), 2) == 0
+    s, lane = places(wide)
+    chunk = 8
+
+    def copy(f, side, q):
+        rows, columns = pl.ds(chunk * q, chunk), pl.ds(own - 8 if side else 0, 8)
+        held = (high if side else low)[f]
+        if len(held.shape) == 4:
+            source, target = far[f].at[:, rows, columns], held.at[:, rows]
+        else:
+            source, target = far[f].at[rows, columns], held.at[rows]
+        return pltpu.make_async_copy(source, target, sems.at[q, f, side])
+
+    ahead = [(f, side) for f in (3,) for side in (0, 1)]
+    behind = [(f, side) for f in (0, 1, 2, 4, 5, 6, 7) for side in (0, 1)]
+    for q in range(n // chunk):
+        for f, side in ahead + behind:
+            copy(f, side, q).start()
+    for f, side in ahead:
+        copy(f, side, 0).wait()
+
+    def fields(group, x, side):
+        res, diag, crs, mask, tx, ty, tz, ff = group
+        first, last = x == 0, x == n - 1
+        before, after = jnp.maximum(x - 1, 0), jnp.minimum(x + 1, n - 1)
+        a = mask[x].astype(F32)
+        b, c = quasi_impes(a, res[0, x], res[1, x], diag[0, x], diag[1, x], crs[0, x], crs[1, x])
+        ty_a = ty[x] * a
+        ey = ty_a * turn_next(a)
+        ez = along_z(tz[x], a, lane)
+        more = ez + z_prev(ez) + jnp.where(last, 0.0, tx[x] * a * mask[after].astype(F32))
+        more = more + jnp.where(first, 0.0, tx[before] * mask[before].astype(F32) * a)
+        more = more + (ey if side else turn_prev(ey))
+        c = jnp.where(s == (1 if side else 6), c + more, c)
+        tile = b
+        for name, v in (("c", c), ("a", a), ("tx", tx[x]), ("e", ey), ("tz", tz[x])):
+            moved = pltpu.roll(v, Y_TURNS[name][side], 0)
+            for place in Y_PLACES[name][side]:
+                tile = jnp.where(s == place, moved, tile)
+        outer = slice(0, 1) if side else slice(7, 8)
+        return tile, ty_a[outer], ff[x][outer]
+
+    def put(rows, up, down):
+        near_ref[rows, :] = jnp.where(even, up, down)
+        far_ref[rows, :] = jnp.where(even, down, up)
+
+    def row(x):
+        up, down = fields(high, x, 0), fields(low, x, 1)
+        put(pl.ds(pl.multiple_of(8 * x, 8), 8), up[0], down[0])
+        put(pl.ds(8 * n + x, 1), up[1], down[1])
+        put(pl.ds(9 * n + x, 1), up[2], down[2])
+
+    def part(q, carry):
+        @pl.when(q < n // chunk - 1)
+        def _():
+            for f, side in ahead:
+                copy(f, side, q + 1).wait()
+
+        for f, side in behind:
+            copy(f, side, q).wait()
+
+        def some(k, v):
+            row(chunk * q + k)
+            return v
+
+        return lax.fori_loop(0, chunk, some, carry, unroll=4)
+
+    put(slice(10 * n, y_message_rows(n)), *[jnp.zeros((y_message_rows(n) - 10 * n, wide), F32)] * 2)
+    for q in range(n // 8):
+        splits = split_ref[q : q + 1, :]
+        up = (lane[:1] < splits[:, -1:]).astype(F32)
+        down = (lane[:1] < splits[:, :1]).astype(F32)
+        put(slice(10 * n + 2 + q, 10 * n + 3 + q), up, down)
+    lax.fori_loop(0, n // chunk, part, 0)
+    corners = [
+        (tx[n - 1, at, :] * mask[n - 1, at, :].astype(F32), mask[0, at, :].astype(F32))
+        for mask, tx, at in ((high[3], high[4], slice(6, 7)), (low[3], low[4], slice(1, 2)))
+    ]
+    for k in range(2):
+        put(slice(10 * n + k, 10 * n + k + 1), corners[0][k], corners[1][k])
+
+
+def y_message_rows(n):
+    return 10 * n + pl.cdiv(2 + n // 8, 8) * 8
+
+
+class Ghosts:
+    def __init__(self, near_ref, far_ref, n):
+        self.refs, self.n = (near_ref, far_ref), n
+        self.even = lax.rem(lax.axis_index("gy"), 2) == 0
+        self.s, _ = places(near_ref.shape[1])
+
+    def both(self, rows):
+        near, far = (ref[rows, :] for ref in self.refs)
+        return jnp.where(self.even, far, near), jnp.where(self.even, near, far)
+
+    def tiles(self, x):
+        return self.both(pl.ds(pl.multiple_of(8 * x, 8), 8))
+
+    def pick(self, tiles, name, low_at=(G - 1,), high_at=(0,)):
+        low, high = tiles
+        if name != "b":
+            up, down = Y_TURNS[name]
+            low, high = pltpu.roll(low, 8 - up, 0), pltpu.roll(high, 8 - down, 0)
+        picked = jnp.zeros_like(low)
+        for place in low_at:
+            picked = jnp.where(self.s == place, low, picked)
+        for place in high_at:
+            picked = jnp.where(self.s == place, high, picked)
+        return picked
+
+    def row(self, at, low_at=G - 1, high_at=0):
+        low, high = self.both(pl.ds(at, 1))
+        return jnp.where(self.s == low_at, low, jnp.where(self.s == high_at, high, 0.0))
+
+    def active(self, x):
+        return self.pick(self.tiles(x), "a")
+
+    def first_active(self):
+        return self.active(0) + self.row(10 * self.n + 1, G - 2, 1)
+
+    def last_trans(self):
+        return self.row(10 * self.n, G - 2, 1)
+
+    def frac(self, x):
+        return self.row(9 * self.n + x)
+
+    def lower(self, q):
+        return self.row(10 * self.n + 2 + q)
+
+
+def prep_kernel(res_hbm, diag_hbm, crs, mask_hbm, tx_hbm, ty_hbm, tz_hbm,
                 rhs, own_diag, tot, gain, one, fx, fy, fz, al0, al1, be0, be1,
-                res, diag, crs, mask, tx, ty, tz, sems):
+                res, diag, mask, tx, ty, tz, sems):
     n, own, wide = mask.shape
     groups = own // 8
     chunk = 4
@@ -175,7 +241,6 @@
         pairs = (
             (res_hbm.at[:, at], res.at[:, at]),
             (diag_hbm.at[:, at], diag.at[:, at]),
-            (crs_hbm.at[:, at], crs.at[:, at]),
             (tx_hbm.at[at], tx.at[at]),
             (ty_hbm.at[at], ty.at[at]),
             (tz_hbm.at[at], tz.at[at]),
@@ -260,16 +325,19 @@
     def __init__(self, x, n, ghosts, mask, rhs, tot, fx, fy, s, lane):
         groups = mask.shape[1] // 8
         first, last = x == 0, x == n - 1
-        ga, gtx, gty = ghosts.first(x)
-        gb, gc, gtz = ghosts.second(x)
+        tiles = ghosts.tiles(x)
+        ga, gtx, gtz = (ghosts.pick(tiles, name) for name in ("a", "tx", "tz"))
+        gb = ghosts.pick(tiles, "b", (G - 1, G - 2), (0, 1))
+        gc = jnp.maximum(ghosts.pick(tiles, "c", (G - 1, G - 2), (0, 1)), 1.0)
         before, after = jnp.maximum(x - 1, 0), jnp.minimum(x + 1, n - 1)
-        a_before, tx_before, _ = ghosts.first(before)
+        tiles_before = ghosts.tiles(before)
+        a_before, tx_before = ghosts.pick(tiles_before, "a"), ghosts.pick(tiles_before, "tx")
         a_after = ghosts.active(after)
-        turned = turn_next(ga)
         end = fy[x, group(groups - 1), :]
-        end = jnp.where(s == G - 1, end * turned, end)
-        a_first = mask[x, group(0), :].astype(F32)
-        ey = gty * ga * turned_next(turned, turn_next(a_first), s)
+        end = jnp.where(s == G - 1, end * turn_next(ga), end)
+        a_first = turn_next(mask[x, group(0), :].astype(F32))
+        ey = ghosts.pick(tiles, "e", (G - 2,), (0,))
+        ey = jnp.where(s == G - 1, ghosts.row(8 * n + x) * a_first, ey)
         ey_turned = turn_prev(ey)
         ez = along_z(gtz, ga, lane)
         t = gtx * ga
@@ -277,7 +345,7 @@
         total = gc + ez + z_prev(ez) + ey + turned_prev(ey_turned, turn_prev(end), s)
         total = total + jnp.where(last, 0.0, ex) + jnp.where(first, 0.0, tx_before * a_before * ga)
         self.end = end
-        self.fx, self.fy, self.fz = jnp.where(last, t, ex), ey, ez
+        self.fx, self.fy, self.fz = jnp.where(last, t + ghosts.last_trans(), ex), ey, ez
         self.rhs = gb
         self.total = (
             tot[x, group(0), :] + jnp.where(s == 0, ey_turned, 0.0),
@@ -296,7 +364,7 @@
     n, own, wide = mask.shape
     groups = own // 8
     s, lane = places(wide)
-    ghosts = Ghosts(ynear, yfar)
+    ghosts = Ghosts(ynear, yfar, n)
     finished = {x: Finished(x, n, ghosts, mask, rhs, tot, fx, fy, s, lane) for x in (0, 1, n - 2, n - 1)}
     for k in range(groups + 1):
         here = group(k)
@@ -318,7 +386,7 @@
 
         if k == groups:
             up = of(n - 1, finished[n - 1].fx)
-            down = of(0, ghosts.active(0))
+            down = of(0, ghosts.first_active())
         else:
             up = of(n - 1, fx[n - 1, here, :])
             down = of(0, mask[0, here, :].astype(F32))
@@ -536,7 +604,7 @@
     n, own, wide = mask.shape
     groups = own // 8
     s, lane = places(wide)
-    ghosts = Ghosts(ynear, yfar)
+    ghosts = Ghosts(ynear, yfar, n)
 
     def finish(x, carry):
         done = Finished(x, n, ghosts, mask, rhs, tot, fx, fy, s, lane)
@@ -546,7 +614,7 @@
             gain3[x, group(slot), :] = g
             one3[x, group(slot), :] = g * done.all_rhs[slot]
         end[x] = done.end
-        for k, v in enumerate((done.rhs, done.fx, done.fy, done.fz, ghosts.frac_and_lower(x)[0])):
+        for k, v in enumerate((done.rhs, done.fx, done.fy, done.fz, ghosts.frac(x))):
             six[k, x] = v
         return carry
 
@@ -638,11 +706,11 @@
     groups = own // 8
     s, lane = places(wide)
     planes = Planes(xnear, xfar, own)
-    ghosts = Ghosts(ynear, yfar)
+    ghosts = Ghosts(ynear, yfar, n)
     o = Edges(groups, ff, rhs, gain, one, fx, fy, fz, gain3, one3, six, end)
 
     def act(k):
-        return ghosts.active(0) if k == groups else mask[0, group(k), :].astype(F32)
+        return ghosts.first_active() if k == groups else mask[0, group(k), :].astype(F32)
 
     o.beyond(n, planes, act, tot, tot3, one_edge, gain_edge, edge_fx)
     depth = 5
@@ -725,7 +793,7 @@
     unknowns = inv.shape[2]
     rows_b, cols_b = split_ref.shape
     per_tile = 2 * rows_b * cols_b
-    ghosts = Ghosts(ynear, yfar)
+    ghosts = Ghosts(ynear, yfar, n)
     planes = Planes(xnear, xfar, own)
     s8, lane8 = places(wide)
 
@@ -759,7 +827,7 @@
             step_z[q, group(r), :] = jnp.where(
                 lane8 == split - 1, jump, jnp.where(lane8 == split, -jump, 0.0)
             )
-        below = ghosts.frac_and_lower(8 * q)[1] > 0.5
+        below = ghosts.lower(q) > 0.5
         k_high, k_low = 2 * q * cols_b, 2 * (q * cols_b + cols_b - 1)
         coarse[q + 1, own:ext, :] = jnp.where(
             s8 == 0,
@@ -849,41 +917,35 @@
     ext = own + G
     unknowns = coarse_inverse.shape[2]
     columns = (residual, accum_diag, accum_cross, mask, trans_x, trans_y, trans_z, frac_flow)
+    hbm = pl.BlockSpec(memory_space=pltpu.HBM)
     far_columns = [pltpu.with_memory_space_constraint(v, pltpu.HBM) for v in columns]
-    groups = own // 8
-
-    def group_spec(array, k):
-        lead = array.shape[:-3]
-        zero = (0,) * len(lead)
-        return pl.BlockSpec((*lead, 8, 8, wide), lambda x: (*zero, x, k, 0))
 
     def array(*shape):
         return jax.ShapeDtypeStruct(shape, F32)
 
     y_messages = pl.pallas_call(
         y_message_kernel,
-        grid=(n // 8,),
-        in_specs=[pl.BlockSpec(split_layer.shape, lambda x: (0, 0))]
-        + [group_spec(v, 0) for v in columns]
-        + [group_spec(v, groups - 1) for v in columns],
-        out_specs=[pl.BlockSpec((8, 16, wide), lambda x: (x, 0, 0))] * 2,
-        out_shape=[array(n, 16, wide)] * 2,
+        in_specs=[WHOLE] + [hbm] * 8,
+        out_specs=[WHOLE] * 2,
+        out_shape=[array(y_message_rows(n), wide)] * 2,
+        scratch_shapes=[pltpu.VMEM((*v.shape[:-2], 8, wide), v.dtype) for v in columns] * 2
+        + [pltpu.SemaphoreType.DMA((n // 8, 8, 2))],
         compiler_params=params(16),
         name="y_messages",
-    )(pltpu.with_memory_space_constraint(split_layer, pltpu.HBM), *far_columns, *far_columns)
+    )(pltpu.with_memory_space_constraint(split_layer, pltpu.HBM), *far_columns)
     ynear, yfar = swap(y_messages, "gy", tiles_y)
 
     rhs, own_diag, tot, gain, one, fx, fy, fz, al0, al1, be0, be1 = pl.pallas_call(
         prep_kernel,
-        in_specs=[pl.BlockSpec(memory_space=pltpu.HBM)] * 7,
+        in_specs=[hbm] * 2 + [WHOLE] + [hbm] * 4,
         out_specs=[WHOLE] * 12,
         out_shape=[array(n, own, wide)] * 12,
-        scratch_shapes=[pltpu.VMEM(v.shape, v.dtype) for v in columns[:7]]
-        + [pltpu.SemaphoreType.DMA((7, n // 4))],
-        compiler_params=params(18),
+        scratch_shapes=[pltpu.VMEM(v.shape, v.dtype) for v in columns[:2] + columns[3:7]]
+        + [pltpu.SemaphoreType.DMA((6, n // 4))],
+        compiler_params=params(16),
         cost_estimate=cost(60_000_000, 30_000_000),
         name="prep",
-    )(*far_columns[:7])
+    )(*far_columns[:2], accum_cross, *far_columns[3:7])
     shared = (rhs, tot, gain, one, fx, fy, fz)
 
     x_messages = pl.pallas_call(

time: 49.3 us -> 48.4 us (0.982)
  blocking collectives: 17.1 us -> 16 us
    all_to_all x1, blocking collectives: 17.1 us -> 16 us  [shards(): got = lax.all_to_all(sent, ('gx', 'gy'), 0, 0, tiled=True)]
  transfers between devices with their start and end apart: 6 -> 6, of which waited for: 0 -> 0; matrix products, arithmetic and copies ran while one was open for 0% -> 0% of each run, Pallas kernels for 32% -> 31%
where the time goes in v6:
time: 48.4 us; the launch traced here: 48.2 us
  Pallas kernels  22.4 us (46%)
  blocking collectives  16 us (33%)
  starting transfers between devices  9.56 us (20%)
    all_to_all x1, blocking collectives, shards(): got = lax.all_to_all(sent, ('gx', 'gy'), 0, 0, tiled=True)  16 us
    ppermute x3, starting transfers between devices, swap(): lax.ppermute(message[0], axis, near)  7.44 us
    pallas_call x1, Pallas kernels, shards(): pl.pallas_call(interior_kernel, in_specs=[SCALARS] + [WHOLE] * 14, out_sp...  7.21 us
    pallas_call x1, Pallas kernels, shards(): pl.pallas_call(prep_kernel, in_specs=[hbm] * 2 + [WHOLE] + [hbm] * 4, out...  5.38 us
    pallas_call x1, Pallas kernels, shards(): pl.pallas_call(y_message_kernel, in_specs=[WHOLE] + [hbm] * 8, out_specs=...  4.66 us
    pallas_call x1, Pallas kernels, shards(): pl.pallas_call(functools.partial(final_kernel, tiles_y), in_specs=[SCALAR...  2.8 us
    pallas_call x1, Pallas kernels, shards(): pl.pallas_call(edge_kernel, in_specs=[SCALARS] + [WHOLE] * (22 + FLUXES),...  2.14 us
    ppermute x3, starting transfers between devices, swap(): lax.ppermute(message[1], axis, far)  2.12 us
  transfers between devices with their start and end apart: 6, of which 0 were waited for; matrix products, arithmetic and copies ran while one was open for 0% of the time, Pallas kernels for 31%

profile of v6, /device:TPU:0, one launch (start us, length us, event | category | flops | bytes accessed | tf_op | source)
XLA Modules:
  0.0 48.2 jit_solution(4269723270325422988)
XLA Ops:
  0.0 0.0 copy-start.3
  0.0 4.7 %y_messages.1 = (f32[328,256]{1,0:T(8,128)S(1)}, f32[328,256]{1,0:T(8,128)S(1)}) custom-call(s32[4,6]{1,0:T(4,128)} %split_ref.7, f32[2,32,48,256]{3,2,1,0:T(8,128)} %res.3, f32[2,32,48,256]{3,2,1,0:T(8,128)} %diag_hbm.1, f32[2,32,48,256]{3,2,1,0:T(8,128)} %crs.1, s32[32,48,256]{2,1,0:T(8,128)} %mask.5, f32[32,48,256]{2,1,0:T(8,128)} %tx_hbm.1, ...), custom_call_target="tpu_custom_call" | custom-call | tf_op jit(solution)/shard_map/y_messages/pallas_call | solution.py:926
  4.7 0.5 %collective-permute-start = (f32[328,256]{1,0:T(8,128)S(1)}, f32[328,256]{1,0:T(8,128)S(1)}, u32[]{:S(2)}, u32[]{:S(2)}) collective-permute-start(f32[328,256]{1,0:T(8,128)S(1)} %get-tuple-element.45), channel_id=1, source_target_pairs={{0,1},{1,0},{2,3},{3,2},{4,5},{5,4},{6,7},{7,6},{8,9},{9,8},{10,11... | collective-permute-start | bytes 1007624 | tf_op jit(solution)/shard_map/ppermute | solution.py:47
  5.2 0.0 copy-start.1
  5.2 0.8 %collective-permute-start.1 = (f32[328,256]{1,0:T(8,128)S(1)}, f32[328,256]{1,0:T(8,128)S(1)}, u32[]{:S(2)}, u32[]{:S(2)}) collective-permute-start(f32[328,256]{1,0:T(8,128)S(1)} %get-tuple-element.46), channel_id=1, source_target_pairs={{1,2},{2,1},{5,6},{6,5},{9,10},{10,9},{13,14},{14,13},{17,18},{18,... | collective-permute-start | bytes 1007624 | tf_op jit(solution)/shard_map/ppermute | solution.py:47
  6.0 0.0 copy-done.3
  6.0 5.4 %prep.1 = (f32[32,48,256]{2,1,0:T(8,128)S(1)}, f32[32,48,256]{2,1,0:T(8,128)S(1)}, f32[32,48,256]{2,1,0:T(8,128)S(1)}, f32[32,48,256]{2,1,0:T(8,128)S(1)}, f32[3...) custom-call(f32[2,32,48,256]{3,2,1,0:T(8,128)} %res.3, ...), custom_call_target="tpu_custom_call" | custom-call | flops 60000000 | bytes 30000000 | tf_op jit(solution)/shard_map/prep/pallas_call | solution.py:938
  11.4 0.0 collective-permute-done.ynear
  11.4 0.0 collective-permute-done.1.yfar
  11.4 0.0 copy-done.1
  11.4 0.0 copy-start
  11.4 0.0 copy-start.2
  11.5 0.0 copy-start.4
  11.5 0.0 copy-start.5
  11.5 0.2 x_messages.1
  11.7 2.6 %collective-permute-start.4 = (f32[304,256]{1,0:T(8,128)S(1)}, f32[304,256]{1,0:T(8,128)S(1)}, u32[]{:S(2)}, u32[]{:S(2)}) collective-permute-start(f32[304,256]{1,0:T(8,128)S(1)} %get-tuple-element.57), channel_id=1, source_target_pairs={{0,4},{4,0},{8,12},{12,8},{16,20},{20,16},{24,28},{28,24},{1,5},{5... | collective-permute-start | bytes 933896 | tf_op jit(solution)/shard_map/ppermute | solution.py:47
  14.2 0.7 %collective-permute-start.5 = (f32[304,256]{1,0:T(8,128)S(1)}, f32[304,256]{1,0:T(8,128)S(1)}, u32[]{:S(2)}, u32[]{:S(2)}) collective-permute-start(f32[304,256]{1,0:T(8,128)S(1)} %get-tuple-element.58), channel_id=1, source_target_pairs={{4,8},{8,4},{12,16},{16,12},{20,24},{24,20},{5,9},{9,5},{13,17},{1... | collective-permute-start | bytes 933896 | tf_op jit(solution)/shard_map/ppermute | solution.py:47
  14.9 0.0 copy-done
  14.9 0.0 copy-done.2
  14.9 0.0 copy-done.4
  15.0 0.0 copy-done.5
  15.0 7.2 %interior.1 = (f32[72,256]{1,0:T(8,128)S(1)}, f32[72,256]{1,0:T(8,128)S(1)}, f32[32,24,256]{2,1,0:T(8,128)S(1)}, f32[32,24,256]{2,1,0:T(8,128)S(1)}, f32[32,24,2...) custom-call(s32[4,6]{1,0:T(4,128)S(1)} %copy-done.5, ...), custom_call_target="tpu_custom_call" | custom-call | flops 60000000 | bytes 30000000 | tf_op jit(solution)/shard_map/interior/pallas_call | solution.py:962
  22.2 4.3 %collective-permute-start.2 = (f32[72,256]{1,0:T(8,128)S(1)}, f32[72,256]{1,0:T(8,128)S(1)}, u32[]{:S(2)}, u32[]{:S(2)}) collective-permute-start(f32[72,256]{1,0:T(8,128)S(1)} %get-tuple-element.55), channel_id=1, source_target_pairs={{0,4},{4,0},{8,12},{12,8},{16,20},{20,16},{24,28},{28,24},{1,5},{5... | collective-permute-start | bytes 221192 | tf_op jit(solution)/shard_map/ppermute | solution.py:47
  26.5 0.7 %collective-permute-start.3 = (f32[72,256]{1,0:T(8,128)S(1)}, f32[72,256]{1,0:T(8,128)S(1)}, u32[]{:S(2)}, u32[]{:S(2)}) collective-permute-start(f32[72,256]{1,0:T(8,128)S(1)} %get-tuple-element.56), channel_id=1, source_target_pairs={{4,8},{8,4},{12,16},{16,12},{20,24},{24,20},{5,9},{9,5},{13,17},{1... | collective-permute-start | bytes 221192 | tf_op jit(solution)/shard_map/ppermute | solution.py:47
  27.2 0.0 collective-permute-done.4.xnear
  27.2 0.0 collective-permute-done.5.xfar
  27.2 2.1 %edges.1 = (f32[32,48,256]{2,1,0:T(8,128)S(1)}, f32[32,48,256]{2,1,0:T(8,128)S(1)}, f32[32,48,256]{2,1,0:T(8,128)S(1)}, f32[32,48,256]{2,1,0:T(8,128)S(1)}, f32[...) custom-call(s32[4,6]{1,0:T(4,128)S(1)} %copy-done.5, ...), custom_call_target="tpu_custom_call", output_to_operand_aliasing={{0}: (23, {}), {1}: (24, {}), {2}: (25, {}), {3}: (26, {}),... | custom-call | tf_op jit(solution)/shard_map/edges/pallas_call | solution.py:984
  29.4 16.0 %all_to_all.11 = f32[32,1,256]{2,1,0:T(1,128)S(1)} all-to-all(f32[32,1,256]{2,1,0:T(1,128)S(1)} %copy.17), channel_id=1, replica_groups=mesh['gx'=8,'gy'=4] {'gx','gy'}, dimensions={0} | all-to-all | bytes 65536 | tf_op jit(solution)/shard_map/all_to_all | solution.py:1005
  45.4 0.0 collective-permute-done.2.xnear
  45.4 0.0 collective-permute-done.3.xfar
  45.4 2.8 %final.1 = f32[2,32,48,256]{3,2,1,0:T(8,128)} custom-call(s32[4,6]{1,0:T(4,128)S(1)} %copy-done.5, f32[32,48,256]{2,1,0:T(8,128)S(1)} %copy-done.2, f32[1,192,192]{2,1,0:T(8,128)S(1)} %copy-done.4, f32[328,256]{1,0:T(8,128)S(1)} %collective-permute-done.ynear, f32[328,256]{1,0:T(8,128)S(1)} %collective-permute-done.1.yfar, ...), custom_call_target="tpu_custom_call" | custom-call | tf_op jit(solution)/shard_map/final/pallas_call | solution.py:1007
  (2 shorter events, 0.0 us)
Async XLA Ops:
  0.0 6.0 %copy-start.3 = (f32[2,32,48,256]{3,2,1,0:T(8,128)S(1)}, f32[2,32,48,256]{3,2,1,0:T(8,128)}, u32[]{:S(2)}) copy-start(f32[2,32,48,256]{3,2,1,0:T(8,128)} %crs.1) | copy-start | bytes 9437188
  4.7 6.7 %collective-permute-start = (f32[328,256]{1,0:T(8,128)S(1)}, f32[328,256]{1,0:T(8,128)S(1)}, u32[]{:S(2)}, u32[]{:S(2)}) collective-permute-start(f32[328,256]{1,0:T(8,128)S(1)} %get-tuple-element.45), channel_id=1, source_target_pairs={{0,1},{1,0},{2,3},{3,2},{4,5},{5,4},{6,7},{7,6},{8,9},{9,8},{10,11... | collective-permute-start | bytes 1007624 | tf_op jit(solution)/shard_map/ppermute | solution.py:47
  5.2 6.2 %copy-start.1 = (s32[32,48,256]{2,1,0:T(8,128)S(1)}, s32[32,48,256]{2,1,0:T(8,128)}, u32[]{:S(2)}) copy-start(s32[32,48,256]{2,1,0:T(8,128)} %mask.5) | copy-start | bytes 4718596
  5.2 6.2 %collective-permute-start.1 = (f32[328,256]{1,0:T(8,128)S(1)}, f32[328,256]{1,0:T(8,128)S(1)}, u32[]{:S(2)}, u32[]{:S(2)}) collective-permute-start(f32[328,256]{1,0:T(8,128)S(1)} %get-tuple-element.46), channel_id=1, source_target_pairs={{1,2},{2,1},{5,6},{6,5},{9,10},{10,9},{13,14},{14,13},{17,18},{18,... | collective-permute-start | bytes 1007624 | tf_op jit(solution)/shard_map/ppermute | solution.py:47
  11.4 3.5 %copy-start = (f32[2,32,48,256]{3,2,1,0:T(8,128)S(1)}, f32[2,32,48,256]{3,2,1,0:T(8,128)}, u32[]{:S(2)}) copy-start(f32[2,32,48,256]{3,2,1,0:T(8,128)} %res.3) | copy-start | bytes 9437188
  11.4 3.5 %copy-start.2 = (f32[32,48,256]{2,1,0:T(8,128)S(1)}, f32[32,48,256]{2,1,0:T(8,128)}, u32[]{:S(2)}) copy-start(f32[32,48,256]{2,1,0:T(8,128)} %frac.1) | copy-start | bytes 4718596
  11.5 3.5 %copy-start.4 = (f32[1,192,192]{2,1,0:T(8,128)S(1)}, f32[1,192,192]{2,1,0:T(8,128)}, u32[]{:S(2)}) copy-start(f32[1,192,192]{2,1,0:T(8,128)} %inv.3) | copy-start | bytes 442372
  11.5 3.5 %copy-start.5 = (s32[4,6]{1,0:T(4,128)S(1)}, s32[4,6]{1,0:T(4,128)}, u32[]{:S(2)}) copy-start(s32[4,6]{1,0:T(4,128)} %split_ref.7) | copy-start | bytes 292
  11.7 15.5 %collective-permute-start.4 = (f32[304,256]{1,0:T(8,128)S(1)}, f32[304,256]{1,0:T(8,128)S(1)}, u32[]{:S(2)}, u32[]{:S(2)}) collective-permute-start(f32[304,256]{1,0:T(8,128)S(1)} %get-tuple-element.57), channel_id=1, source_target_pairs={{0,4},{4,0},{8,12},{12,8},{16,20},{20,16},{24,28},{28,24},{1,5},{5... | collective-permute-start | bytes 933896 | tf_op jit(solution)/shard_map/ppermute | solution.py:47
  14.2 12.9 %collective-permute-start.5 = (f32[304,256]{1,0:T(8,128)S(1)}, f32[304,256]{1,0:T(8,128)S(1)}, u32[]{:S(2)}, u32[]{:S(2)}) collective-permute-start(f32[304,256]{1,0:T(8,128)S(1)} %get-tuple-element.58), channel_id=1, source_target_pairs={{4,8},{8,4},{12,16},{16,12},{20,24},{24,20},{5,9},{9,5},{13,17},{1... | collective-permute-start | bytes 933896 | tf_op jit(solution)/shard_map/ppermute | solution.py:47
  22.2 23.2 %collective-permute-start.2 = (f32[72,256]{1,0:T(8,128)S(1)}, f32[72,256]{1,0:T(8,128)S(1)}, u32[]{:S(2)}, u32[]{:S(2)}) collective-permute-start(f32[72,256]{1,0:T(8,128)S(1)} %get-tuple-element.55), channel_id=1, source_target_pairs={{0,4},{4,0},{8,12},{12,8},{16,20},{20,16},{24,28},{28,24},{1,5},{5... | collective-permute-start | bytes 221192 | tf_op jit(solution)/shard_map/ppermute | solution.py:47
  26.5 18.9 %collective-permute-start.3 = (f32[72,256]{1,0:T(8,128)S(1)}, f32[72,256]{1,0:T(8,128)S(1)}, u32[]{:S(2)}, u32[]{:S(2)}) collective-permute-start(f32[72,256]{1,0:T(8,128)S(1)} %get-tuple-element.56), channel_id=1, source_target_pairs={{4,8},{8,4},{12,16},{16,12},{20,24},{24,20},{5,9},{9,5},{13,17},{1... | collective-permute-start | bytes 221192 | tf_op jit(solution)/shard_map/ppermute | solution.py:47

commit v7 on v6

--- a/solution.py
+++ b/solution.py
@@ -93,90 +93,67 @@
 
 
 def y_message_kernel(split_ref, *refs):
-    far, (near_ref, far_ref) = refs[:8], refs[8:10]
-    low, high, sems = refs[10:18], refs[18:26], refs[26]
+    low, high, (near_ref, far_ref) = refs[:8], refs[8:16], refs[16:]
     n, _, wide = low[3].shape
-    own = far[3].shape[1]
     even = lax.rem(lax.axis_index("gy"), 2) == 0
-    s, lane = places(wide)
-    chunk = 8
-
-    def copy(f, side, q):
-        rows, columns = pl.ds(chunk * q, chunk), pl.ds(own - 8 if side else 0, 8)
-        held = (high if side else low)[f]
-        if len(held.shape) == 4:
-            source, target = far[f].at[:, rows, columns], held.at[:, rows]
-        else:
-            source, target = far[f].at[rows, columns], held.at[rows]
-        return pltpu.make_async_copy(source, target, sems.at[q, f, side])
-
-    ahead = [(f, side) for f in (3,) for side in (0, 1)]
-    behind = [(f, side) for f in (0, 1, 2, 4, 5, 6, 7) for side in (0, 1)]
-    for q in range(n // chunk):
-        for f, side in ahead + behind:
-            copy(f, side, q).start()
-    for f, side in ahead:
-        copy(f, side, 0).wait()
-
-    def fields(group, x, side):
+    step = pl.program_id(0)
+    x0 = pl.multiple_of(8 * step, 8)
+    shape = (8, G, wide)
+    row, s, lane = (lax.broadcasted_iota(jnp.int32, shape, k) for k in range(3))
+
+    def turn(v, k):
+        return jnp.stack([pltpu.roll(v[i], k, 0) for i in range(v.shape[0])])
+
+    def fields(group, side):
         res, diag, crs, mask, tx, ty, tz, ff = group
-        first, last = x == 0, x == n - 1
-        before, after = jnp.maximum(x - 1, 0), jnp.minimum(x + 1, n - 1)
-        a = mask[x].astype(F32)
-        b, c = quasi_impes(a, res[0, x], res[1, x], diag[0, x], diag[1, x], crs[0, x], crs[1, x])
-        ty_a = ty[x] * a
-        ey = ty_a * turn_next(a)
-        ez = along_z(tz[x], a, lane)
-        more = ez + z_prev(ez) + jnp.where(last, 0.0, tx[x] * a * mask[after].astype(F32))
-        more = more + jnp.where(first, 0.0, tx[before] * mask[before].astype(F32) * a)
-        more = more + (ey if side else turn_prev(ey))
+        before, after = jnp.maximum(x0 - 1, 0), jnp.minimum(x0 + 8, n - 1)
+        a, trans = mask[pl.ds(x0, 8)].astype(F32), tx[pl.ds(x0, 8)]
+        t = trans * a
+        a_after = jnp.concatenate([a[1:], mask[pl.ds(after, 1)].astype(F32)], axis=0)
+        t_before = jnp.concatenate([tx[pl.ds(before, 1)] * mask[pl.ds(before, 1)].astype(F32), t[:7]], axis=0)
+        b, c = quasi_impes(a, res[0], res[1], diag[0], diag[1], crs[0], crs[1])
+        ty_a = ty[...] * a
+        ey = ty_a * turn(a, G - 1)
+        a_above = jnp.stack([z_next(a[i]) for i in range(8)])
+        ez = jnp.where(lane < wide - 1, tz[...] * a * a_above, 0.0)
+        more = ez + jnp.stack([z_prev(ez[i]) for i in range(8)])
+        more = more + jnp.where(row + x0 == n - 1, 0.0, t * a_after)
+        more = more + jnp.where(row + x0 == 0, 0.0, t_before * a)
+        more = more + (ey if side else turn(ey, 1))
         c = jnp.where(s == (1 if side else 6), c + more, c)
         tile = b
-        for name, v in (("c", c), ("a", a), ("tx", tx[x]), ("e", ey), ("tz", tz[x])):
-            moved = pltpu.roll(v, Y_TURNS[name][side], 0)
+        for name, v in (("c", c), ("a", a), ("tx", trans), ("e", ey), ("tz", tz[...])):
+            moved = turn(v, Y_TURNS[name][side])
             for place in Y_PLACES[name][side]:
                 tile = jnp.where(s == place, moved, tile)
         outer = slice(0, 1) if side else slice(7, 8)
-        return tile, ty_a[outer], ff[x][outer]
+        return tile, ty_a[:, outer], ff[:, outer, :]
 
     def put(rows, up, down):
         near_ref[rows, :] = jnp.where(even, up, down)
         far_ref[rows, :] = jnp.where(even, down, up)
 
-    def row(x):
-        up, down = fields(high, x, 0), fields(low, x, 1)
-        put(pl.ds(pl.multiple_of(8 * x, 8), 8), up[0], down[0])
-        put(pl.ds(8 * n + x, 1), up[1], down[1])
-        put(pl.ds(9 * n + x, 1), up[2], down[2])
-
-    def part(q, carry):
-        @pl.when(q < n // chunk - 1)
-        def _():
-            for f, side in ahead:
-                copy(f, side, q + 1).wait()
-
-        for f, side in behind:
-            copy(f, side, q).wait()
-
-        def some(k, v):
-            row(chunk * q + k)
-            return v
-
-        return lax.fori_loop(0, chunk, some, carry, unroll=4)
-
-    put(slice(10 * n, y_message_rows(n)), *[jnp.zeros((y_message_rows(n) - 10 * n, wide), F32)] * 2)
-    for q in range(n // 8):
-        splits = split_ref[q : q + 1, :]
-        up = (lane[:1] < splits[:, -1:]).astype(F32)
-        down = (lane[:1] < splits[:, :1]).astype(F32)
-        put(slice(10 * n + 2 + q, 10 * n + 3 + q), up, down)
-    lax.fori_loop(0, n // chunk, part, 0)
-    corners = [
-        (tx[n - 1, at, :] * mask[n - 1, at, :].astype(F32), mask[0, at, :].astype(F32))
-        for mask, tx, at in ((high[3], high[4], slice(6, 7)), (low[3], low[4], slice(1, 2)))
-    ]
-    for k in range(2):
-        put(slice(10 * n + k, 10 * n + k + 1), corners[0][k], corners[1][k])
+    up, down = fields(high, 0), fields(low, 1)
+    for k in range(8):
+        put(pl.ds(pl.multiple_of(8 * (x0 + k), 8), 8), up[0][k], down[0][k])
+        put(pl.ds(8 * n + x0 + k, 1), up[1][k], down[1][k])
+        put(pl.ds(9 * n + x0 + k, 1), up[2][k], down[2][k])
+
+    @pl.when(step == 0)
+    def _():
+        put(slice(10 * n, y_message_rows(n)), *[jnp.zeros((y_message_rows(n) - 10 * n, wide), F32)] * 2)
+        first_lane = lax.broadcasted_iota(jnp.int32, (1, wide), 1)
+        for q in range(n // 8):
+            splits = split_ref[q : q + 1, :]
+            above = (first_lane < splits[:, -1:]).astype(F32)
+            below = (first_lane < splits[:, :1]).astype(F32)
+            put(slice(10 * n + 2 + q, 10 * n + 3 + q), above, below)
+        corners = [
+            (tx[n - 1, at, :] * mask[n - 1, at, :].astype(F32), mask[0, at, :].astype(F32))
+            for mask, tx, at in ((high[3], high[4], slice(6, 7)), (low[3], low[4], slice(1, 2)))
+        ]
+        for k in range(2):
+            put(slice(10 * n + k, 10 * n + k + 1), corners[0][k], corners[1][k])
 
 
 def y_message_rows(n):
@@ -923,16 +900,23 @@
     def array(*shape):
         return jax.ShapeDtypeStruct(shape, F32)
 
+    def group_spec(k, f):
+        if f in (3, 4):
+            return pl.BlockSpec((n, G, wide), lambda x: (0, k, 0))
+        lead = columns[f].shape[:-3]
+        return pl.BlockSpec((*lead, 8, G, wide), lambda x: (*(0,) * len(lead), x, k, 0))
+
     y_messages = pl.pallas_call(
         y_message_kernel,
-        in_specs=[WHOLE] + [hbm] * 8,
+        grid=(n // 8,),
+        in_specs=[pl.BlockSpec(split_layer.shape, lambda x: (0, 0))]
+        + [group_spec(0, f) for f in range(8)]
+        + [group_spec(own // 8 - 1, f) for f in range(8)],
         out_specs=[WHOLE] * 2,
         out_shape=[array(y_message_rows(n), wide)] * 2,
-        scratch_shapes=[pltpu.VMEM((*v.shape[:-2], 8, wide), v.dtype) for v in columns] * 2
-        + [pltpu.SemaphoreType.DMA((n // 8, 8, 2))],
         compiler_params=params(16),
         name="y_messages",
-    )(pltpu.with_memory_space_constraint(split_layer, pltpu.HBM), *far_columns)
+    )(pltpu.with_memory_space_constraint(split_layer, pltpu.HBM), *far_columns, *far_columns)
     ynear, yfar = swap(y_messages, "gy", tiles_y)
 
     rhs, own_diag, tot, gain, one, fx, fy, fz, al0, al1, be0, be1 = pl.pallas_call(

time: 48.4 us -> 48 us (level)
  no operation moved by 1% of the time
where the time goes in v7:
time: 48 us; the launch traced here: 47.8 us
  Pallas kernels  22 us (46%)
  blocking collectives  16 us (33%)
  starting transfers between devices  9.56 us (20%)
    all_to_all x1, blocking collectives, shards(): got = lax.all_to_all(sent, ('gx', 'gy'), 0, 0, tiled=True)  16 us
    ppermute x3, starting transfers between devices, swap(): lax.ppermute(message[0], axis, near)  7.44 us
    pallas_call x1, Pallas kernels, shards(): pl.pallas_call(interior_kernel, in_specs=[SCALARS] + [WHOLE] * 14, out_sp...  7.2 us
    pallas_call x1, Pallas kernels, shards(): pl.pallas_call(prep_kernel, in_specs=[hbm] * 2 + [WHOLE] + [hbm] * 4, out...  5.38 us
    pallas_call x1, Pallas kernels, shards(): pl.pallas_call(y_message_kernel, grid=(n // 8,), in_specs=[pl.BlockSpec(s...  4.28 us
    pallas_call x1, Pallas kernels, shards(): pl.pallas_call(functools.partial(final_kernel, tiles_y), in_specs=[SCALAR...  2.78 us
    pallas_call x1, Pallas kernels, shards(): pl.pallas_call(edge_kernel, in_specs=[SCALARS] + [WHOLE] * (22 + FLUXES),...  2.14 us
    ppermute x3, starting transfers between devices, swap(): lax.ppermute(message[1], axis, far)  2.12 us
  transfers between devices with their start and end apart: 6, of which 0 were waited for; matrix products, arithmetic and copies ran while one was open for 0% of the time, Pallas kernels for 31%

profile of v7, /device:TPU:0, one launch (start us, length us, event | category | flops | bytes accessed | tf_op | source)
XLA Modules:
  0.0 47.8 jit_solution(6634496790078244573)
XLA Ops:
  0.0 0.0 copy-start.3
  0.0 4.3 %y_messages.1 = (f32[328,256]{1,0:T(8,128)S(1)}, f32[328,256]{1,0:T(8,128)S(1)}) custom-call(s32[4,6]{1,0:T(4,128)} %split_ref.7, f32[2,32,48,256]{3,2,1,0:T(8,128)} %res.3, f32[2,32,48,256]{3,2,1,0:T(8,128)} %diag_hbm.1, f32[2,32,48,256]{3,2,1,0:T(8,128)} %crs.1, s32[32,48,256]{2,1,0:T(8,128)} %mask.5, f32[32,48,256]{2,1,0:T(8,128)} %tx_hbm.1, ...), custom_call_target="tpu_custom_call" | custom-call | tf_op jit(solution)/shard_map/y_messages/pallas_call | solution.py:909
  4.3 0.5 %collective-permute-start = (f32[328,256]{1,0:T(8,128)S(1)}, f32[328,256]{1,0:T(8,128)S(1)}, u32[]{:S(2)}, u32[]{:S(2)}) collective-permute-start(f32[328,256]{1,0:T(8,128)S(1)} %get-tuple-element.45), channel_id=1, source_target_pairs={{0,1},{1,0},{2,3},{3,2},{4,5},{5,4},{6,7},{7,6},{8,9},{9,8},{10,11... | collective-permute-start | bytes 1007624 | tf_op jit(solution)/shard_map/ppermute | solution.py:47
  4.8 0.0 copy-start.1
  4.8 0.8 %collective-permute-start.1 = (f32[328,256]{1,0:T(8,128)S(1)}, f32[328,256]{1,0:T(8,128)S(1)}, u32[]{:S(2)}, u32[]{:S(2)}) collective-permute-start(f32[328,256]{1,0:T(8,128)S(1)} %get-tuple-element.46), channel_id=1, source_target_pairs={{1,2},{2,1},{5,6},{6,5},{9,10},{10,9},{13,14},{14,13},{17,18},{18,... | collective-permute-start | bytes 1007624 | tf_op jit(solution)/shard_map/ppermute | solution.py:47
  5.6 0.0 copy-done.3
  5.6 5.4 %prep.1 = (f32[32,48,256]{2,1,0:T(8,128)S(1)}, f32[32,48,256]{2,1,0:T(8,128)S(1)}, f32[32,48,256]{2,1,0:T(8,128)S(1)}, f32[32,48,256]{2,1,0:T(8,128)S(1)}, f32[3...) custom-call(f32[2,32,48,256]{3,2,1,0:T(8,128)} %res.3, ...), custom_call_target="tpu_custom_call" | custom-call | flops 60000000 | bytes 30000000 | tf_op jit(solution)/shard_map/prep/pallas_call | solution.py:922
  11.0 0.0 collective-permute-done.ynear
  11.0 0.0 collective-permute-done.1.yfar
  11.0 0.0 copy-done.1
  11.1 0.0 copy-start
  11.1 0.0 copy-start.2
  11.1 0.0 copy-start.4
  11.1 0.0 copy-start.5
  11.1 0.2 x_messages.1
  11.3 2.6 %collective-permute-start.4 = (f32[304,256]{1,0:T(8,128)S(1)}, f32[304,256]{1,0:T(8,128)S(1)}, u32[]{:S(2)}, u32[]{:S(2)}) collective-permute-start(f32[304,256]{1,0:T(8,128)S(1)} %get-tuple-element.57), channel_id=1, source_target_pairs={{0,4},{4,0},{8,12},{12,8},{16,20},{20,16},{24,28},{28,24},{1,5},{5... | collective-permute-start | bytes 933896 | tf_op jit(solution)/shard_map/ppermute | solution.py:47
  13.9 0.7 %collective-permute-start.5 = (f32[304,256]{1,0:T(8,128)S(1)}, f32[304,256]{1,0:T(8,128)S(1)}, u32[]{:S(2)}, u32[]{:S(2)}) collective-permute-start(f32[304,256]{1,0:T(8,128)S(1)} %get-tuple-element.58), channel_id=1, source_target_pairs={{4,8},{8,4},{12,16},{16,12},{20,24},{24,20},{5,9},{9,5},{13,17},{1... | collective-permute-start | bytes 933896 | tf_op jit(solution)/shard_map/ppermute | solution.py:47
  14.5 0.0 copy-done
  14.6 0.0 copy-done.2
  14.6 0.0 copy-done.4
  14.6 0.0 copy-done.5
  14.6 7.2 %interior.1 = (f32[72,256]{1,0:T(8,128)S(1)}, f32[72,256]{1,0:T(8,128)S(1)}, f32[32,24,256]{2,1,0:T(8,128)S(1)}, f32[32,24,256]{2,1,0:T(8,128)S(1)}, f32[32,24,2...) custom-call(s32[4,6]{1,0:T(4,128)S(1)} %copy-done.5, ...), custom_call_target="tpu_custom_call" | custom-call | flops 60000000 | bytes 30000000 | tf_op jit(solution)/shard_map/interior/pallas_call | solution.py:946
  21.8 4.3 %collective-permute-start.2 = (f32[72,256]{1,0:T(8,128)S(1)}, f32[72,256]{1,0:T(8,128)S(1)}, u32[]{:S(2)}, u32[]{:S(2)}) collective-permute-start(f32[72,256]{1,0:T(8,128)S(1)} %get-tuple-element.55), channel_id=1, source_target_pairs={{0,4},{4,0},{8,12},{12,8},{16,20},{20,16},{24,28},{28,24},{1,5},{5... | collective-permute-start | bytes 221192 | tf_op jit(solution)/shard_map/ppermute | solution.py:47
  26.1 0.7 %collective-permute-start.3 = (f32[72,256]{1,0:T(8,128)S(1)}, f32[72,256]{1,0:T(8,128)S(1)}, u32[]{:S(2)}, u32[]{:S(2)}) collective-permute-start(f32[72,256]{1,0:T(8,128)S(1)} %get-tuple-element.56), channel_id=1, source_target_pairs={{4,8},{8,4},{12,16},{16,12},{20,24},{24,20},{5,9},{9,5},{13,17},{1... | collective-permute-start | bytes 221192 | tf_op jit(solution)/shard_map/ppermute | solution.py:47
  26.8 0.0 collective-permute-done.4.xnear
  26.8 0.0 collective-permute-done.5.xfar
  26.8 2.1 %edges.1 = (f32[32,48,256]{2,1,0:T(8,128)S(1)}, f32[32,48,256]{2,1,0:T(8,128)S(1)}, f32[32,48,256]{2,1,0:T(8,128)S(1)}, f32[32,48,256]{2,1,0:T(8,128)S(1)}, f32[...) custom-call(s32[4,6]{1,0:T(4,128)S(1)} %copy-done.5, ...), custom_call_target="tpu_custom_call", output_to_operand_aliasing={{0}: (23, {}), {1}: (24, {}), {2}: (25, {}), {3}: (26, {}),... | custom-call | tf_op jit(solution)/shard_map/edges/pallas_call | solution.py:968
  29.0 16.0 %all_to_all.11 = f32[32,1,256]{2,1,0:T(1,128)S(1)} all-to-all(f32[32,1,256]{2,1,0:T(1,128)S(1)} %copy.17), channel_id=1, replica_groups=mesh['gx'=8,'gy'=4] {'gx','gy'}, dimensions={0} | all-to-all | bytes 65536 | tf_op jit(solution)/shard_map/all_to_all | solution.py:989
  45.0 0.0 collective-permute-done.2.xnear
  45.0 0.0 collective-permute-done.3.xfar
  45.0 2.8 %final.1 = f32[2,32,48,256]{3,2,1,0:T(8,128)} custom-call(s32[4,6]{1,0:T(4,128)S(1)} %copy-done.5, f32[32,48,256]{2,1,0:T(8,128)S(1)} %copy-done.2, f32[1,192,192]{2,1,0:T(8,128)S(1)} %copy-done.4, f32[328,256]{1,0:T(8,128)S(1)} %collective-permute-done.ynear, f32[328,256]{1,0:T(8,128)S(1)} %collective-permute-done.1.yfar, ...), custom_call_target="tpu_custom_call" | custom-call | tf_op jit(solution)/shard_map/final/pallas_call | solution.py:991
  (2 shorter events, 0.0 us)
Async XLA Ops:
  0.0 5.6 %copy-start.3 = (f32[2,32,48,256]{3,2,1,0:T(8,128)S(1)}, f32[2,32,48,256]{3,2,1,0:T(8,128)}, u32[]{:S(2)}) copy-start(f32[2,32,48,256]{3,2,1,0:T(8,128)} %crs.1) | copy-start | bytes 9437188
  4.3 6.7 %collective-permute-start = (f32[328,256]{1,0:T(8,128)S(1)}, f32[328,256]{1,0:T(8,128)S(1)}, u32[]{:S(2)}, u32[]{:S(2)}) collective-permute-start(f32[328,256]{1,0:T(8,128)S(1)} %get-tuple-element.45), channel_id=1, source_target_pairs={{0,1},{1,0},{2,3},{3,2},{4,5},{5,4},{6,7},{7,6},{8,9},{9,8},{10,11... | collective-permute-start | bytes 1007624 | tf_op jit(solution)/shard_map/ppermute | solution.py:47
  4.8 6.2 %copy-start.1 = (s32[32,48,256]{2,1,0:T(8,128)S(1)}, s32[32,48,256]{2,1,0:T(8,128)}, u32[]{:S(2)}) copy-start(s32[32,48,256]{2,1,0:T(8,128)} %mask.5) | copy-start | bytes 4718596
  4.8 6.2 %collective-permute-start.1 = (f32[328,256]{1,0:T(8,128)S(1)}, f32[328,256]{1,0:T(8,128)S(1)}, u32[]{:S(2)}, u32[]{:S(2)}) collective-permute-start(f32[328,256]{1,0:T(8,128)S(1)} %get-tuple-element.46), channel_id=1, source_target_pairs={{1,2},{2,1},{5,6},{6,5},{9,10},{10,9},{13,14},{14,13},{17,18},{18,... | collective-permute-start | bytes 1007624 | tf_op jit(solution)/shard_map/ppermute | solution.py:47
  11.1 3.5 %copy-start = (f32[2,32,48,256]{3,2,1,0:T(8,128)S(1)}, f32[2,32,48,256]{3,2,1,0:T(8,128)}, u32[]{:S(2)}) copy-start(f32[2,32,48,256]{3,2,1,0:T(8,128)} %res.3) | copy-start | bytes 9437188
  11.1 3.5 %copy-start.2 = (f32[32,48,256]{2,1,0:T(8,128)S(1)}, f32[32,48,256]{2,1,0:T(8,128)}, u32[]{:S(2)}) copy-start(f32[32,48,256]{2,1,0:T(8,128)} %frac.1) | copy-start | bytes 4718596
  11.1 3.5 %copy-start.4 = (f32[1,192,192]{2,1,0:T(8,128)S(1)}, f32[1,192,192]{2,1,0:T(8,128)}, u32[]{:S(2)}) copy-start(f32[1,192,192]{2,1,0:T(8,128)} %inv.3) | copy-start | bytes 442372
  11.1 3.5 %copy-start.5 = (s32[4,6]{1,0:T(4,128)S(1)}, s32[4,6]{1,0:T(4,128)}, u32[]{:S(2)}) copy-start(s32[4,6]{1,0:T(4,128)} %split_ref.7) | copy-start | bytes 292
  11.3 15.5 %collective-permute-start.4 = (f32[304,256]{1,0:T(8,128)S(1)}, f32[304,256]{1,0:T(8,128)S(1)}, u32[]{:S(2)}, u32[]{:S(2)}) collective-permute-start(f32[304,256]{1,0:T(8,128)S(1)} %get-tuple-element.57), channel_id=1, source_target_pairs={{0,4},{4,0},{8,12},{12,8},{16,20},{20,16},{24,28},{28,24},{1,5},{5... | collective-permute-start | bytes 933896 | tf_op jit(solution)/shard_map/ppermute | solution.py:47
  13.9 12.9 %collective-permute-start.5 = (f32[304,256]{1,0:T(8,128)S(1)}, f32[304,256]{1,0:T(8,128)S(1)}, u32[]{:S(2)}, u32[]{:S(2)}) collective-permute-start(f32[304,256]{1,0:T(8,128)S(1)} %get-tuple-element.58), channel_id=1, source_target_pairs={{4,8},{8,4},{12,16},{16,12},{20,24},{24,20},{5,9},{9,5},{13,17},{1... | collective-permute-start | bytes 933896 | tf_op jit(solution)/shard_map/ppermute | solution.py:47
  21.8 23.2 %collective-permute-start.2 = (f32[72,256]{1,0:T(8,128)S(1)}, f32[72,256]{1,0:T(8,128)S(1)}, u32[]{:S(2)}, u32[]{:S(2)}) collective-permute-start(f32[72,256]{1,0:T(8,128)S(1)} %get-tuple-element.55), channel_id=1, source_target_pairs={{0,4},{4,0},{8,12},{12,8},{16,20},{20,16},{24,28},{28,24},{1,5},{5... | collective-permute-start | bytes 221192 | tf_op jit(solution)/shard_map/ppermute | solution.py:47
  26.1 18.9 %collective-permute-start.3 = (f32[72,256]{1,0:T(8,128)S(1)}, f32[72,256]{1,0:T(8,128)S(1)}, u32[]{:S(2)}, u32[]{:S(2)}) collective-permute-start(f32[72,256]{1,0:T(8,128)S(1)} %get-tuple-element.56), channel_id=1, source_target_pairs={{4,8},{8,4},{12,16},{16,12},{20,24},{24,20},{5,9},{9,5},{13,17},{1... | collective-permute-start | bytes 221192 | tf_op jit(solution)/shard_map/ppermute | solution.py:47

commit v8 on v7

--- a/solution.py
+++ b/solution.py
@@ -12,6 +12,7 @@
 WHOLE = pl.BlockSpec(memory_space=pltpu.VMEM)
 SCALARS = pl.BlockSpec(memory_space=pltpu.SMEM)
 G = 8
+STEP = 16
 PLANES = 6
 
 
@@ -97,8 +98,8 @@
     n, _, wide = low[3].shape
     even = lax.rem(lax.axis_index("gy"), 2) == 0
     step = pl.program_id(0)
-    x0 = pl.multiple_of(8 * step, 8)
-    shape = (8, G, wide)
+    x0 = pl.multiple_of(STEP * step, 8)
+    shape = (STEP, G, wide)
     row, s, lane = (lax.broadcasted_iota(jnp.int32, shape, k) for k in range(3))
 
     def turn(v, k):
@@ -106,17 +107,17 @@
 
     def fields(group, side):
         res, diag, crs, mask, tx, ty, tz, ff = group
-        before, after = jnp.maximum(x0 - 1, 0), jnp.minimum(x0 + 8, n - 1)
-        a, trans = mask[pl.ds(x0, 8)].astype(F32), tx[pl.ds(x0, 8)]
+        before, after = jnp.maximum(x0 - 1, 0), jnp.minimum(x0 + STEP, n - 1)
+        a, trans = mask[pl.ds(x0, STEP)].astype(F32), tx[pl.ds(x0, STEP)]
         t = trans * a
         a_after = jnp.concatenate([a[1:], mask[pl.ds(after, 1)].astype(F32)], axis=0)
-        t_before = jnp.concatenate([tx[pl.ds(before, 1)] * mask[pl.ds(before, 1)].astype(F32), t[:7]], axis=0)
+        t_before = jnp.concatenate([tx[pl.ds(before, 1)] * mask[pl.ds(before, 1)].astype(F32), t[:-1]], axis=0)
         b, c = quasi_impes(a, res[0], res[1], diag[0], diag[1], crs[0], crs[1])
         ty_a = ty[...] * a
         ey = ty_a * turn(a, G - 1)
-        a_above = jnp.stack([z_next(a[i]) for i in range(8)])
+        a_above = jnp.stack([z_next(a[i]) for i in range(STEP)])
         ez = jnp.where(lane < wide - 1, tz[...] * a * a_above, 0.0)
-        more = ez + jnp.stack([z_prev(ez[i]) for i in range(8)])
+        more = ez + jnp.stack([z_prev(ez[i]) for i in range(STEP)])
         more = more + jnp.where(row + x0 == n - 1, 0.0, t * a_after)
         more = more + jnp.where(row + x0 == 0, 0.0, t_before * a)
         more = more + (ey if side else turn(ey, 1))
@@ -134,7 +135,7 @@
         far_ref[rows, :] = jnp.where(even, down, up)
 
     up, down = fields(high, 0), fields(low, 1)
-    for k in range(8):
+    for k in range(STEP):
         put(pl.ds(pl.multiple_of(8 * (x0 + k), 8), 8), up[0][k], down[0][k])
         put(pl.ds(8 * n + x0 + k, 1), up[1][k], down[1][k])
         put(pl.ds(9 * n + x0 + k, 1), up[2][k], down[2][k])
@@ -299,7 +300,7 @@
 
 
 class Finished:
-    def __init__(self, x, n, ghosts, mask, rhs, tot, fx, fy, s, lane):
+    def __init__(self, x, n, ghosts, mask, rhs, tot, fx, fy, s, lane, ex_before=None):
         groups = mask.shape[1] // 8
         first, last = x == 0, x == n - 1
         tiles = ghosts.tiles(x)
@@ -307,8 +308,10 @@
         gb = ghosts.pick(tiles, "b", (G - 1, G - 2), (0, 1))
         gc = jnp.maximum(ghosts.pick(tiles, "c", (G - 1, G - 2), (0, 1)), 1.0)
         before, after = jnp.maximum(x - 1, 0), jnp.minimum(x + 1, n - 1)
-        tiles_before = ghosts.tiles(before)
-        a_before, tx_before = ghosts.pick(tiles_before, "a"), ghosts.pick(tiles_before, "tx")
+        if ex_before is None:
+            tiles_before = ghosts.tiles(before)
+            ex_before = ghosts.pick(tiles_before, "a") * ghosts.pick(tiles_before, "tx") * ga
+            ex_before = jnp.where(first, 0.0, ex_before)
         a_after = ghosts.active(after)
         end = fy[x, group(groups - 1), :]
         end = jnp.where(s == G - 1, end * turn_next(ga), end)
@@ -320,7 +323,8 @@
         t = gtx * ga
         ex = t * a_after
         total = gc + ez + z_prev(ez) + ey + turned_prev(ey_turned, turn_prev(end), s)
-        total = total + jnp.where(last, 0.0, ex) + jnp.where(first, 0.0, tx_before * a_before * ga)
+        total = total + jnp.where(last, 0.0, ex) + ex_before
+        self.ex = ex
         self.end = end
         self.fx, self.fy, self.fz = jnp.where(last, t + ghosts.last_trans(), ex), ey, ez
         self.rhs = gb
@@ -584,7 +588,7 @@
     ghosts = Ghosts(ynear, yfar, n)
 
     def finish(x, carry):
-        done = Finished(x, n, ghosts, mask, rhs, tot, fx, fy, s, lane)
+        done = Finished(x, n, ghosts, mask, rhs, tot, fx, fy, s, lane, carry)
         for slot in range(3):
             g = relaxation / done.total[slot]
             tot3[x, group(slot), :] = done.total[slot]
@@ -593,9 +597,9 @@
         end[x] = done.end
         for k, v in enumerate((done.rhs, done.fx, done.fy, done.fz, ghosts.frac(x))):
             six[k, x] = v
-        return carry
-
-    lax.fori_loop(0, n, finish, 0, unroll=8)
+        return done.ex
+
+    lax.fori_loop(0, n, finish, jnp.zeros((G, wide), F32), unroll=8)
     o = Inside(groups, ff, rhs, gain, one, fx, fy, fz, gain3, one3, six, end)
 
     def second(x, carry):
@@ -904,11 +908,11 @@
         if f in (3, 4):
             return pl.BlockSpec((n, G, wide), lambda x: (0, k, 0))
         lead = columns[f].shape[:-3]
-        return pl.BlockSpec((*lead, 8, G, wide), lambda x: (*(0,) * len(lead), x, k, 0))
+        return pl.BlockSpec((*lead, STEP, G, wide), lambda x: (*(0,) * len(lead), x, k, 0))
 
     y_messages = pl.pallas_call(
         y_message_kernel,
-        grid=(n // 8,),
+        grid=(n // STEP,),
         in_specs=[pl.BlockSpec(split_layer.shape, lambda x: (0, 0))]
         + [group_spec(0, f) for f in range(8)]
         + [group_spec(own // 8 - 1, f) for f in range(8)],

time: 48 us -> 47 us (0.979)
  Pallas kernels: 22 us -> 20.9 us
    pallas_call x1, Pallas kernels: 4.28 us -> 3.34 us  [shards(): pl.pallas_call(y_message_kernel, grid=(n // STEP,), in_specs=[pl.BlockSpe...]
where the time goes in v8:
time: 47 us; the launch traced here: 46.8 us
  Pallas kernels  20.9 us (44%)
  blocking collectives  16 us (34%)
  starting transfers between devices  9.56 us (20%)
    all_to_all x1, blocking collectives, shards(): got = lax.all_to_all(sent, ('gx', 'gy'), 0, 0, tiled=True)  16 us
    ppermute x3, starting transfers between devices, swap(): lax.ppermute(message[0], axis, near)  7.44 us
    pallas_call x1, Pallas kernels, shards(): pl.pallas_call(interior_kernel, in_specs=[SCALARS] + [WHOLE] * 14, out_sp...  7.13 us
    pallas_call x1, Pallas kernels, shards(): pl.pallas_call(prep_kernel, in_specs=[hbm] * 2 + [WHOLE] + [hbm] * 4, out...  5.38 us
    pallas_call x1, Pallas kernels, shards(): pl.pallas_call(y_message_kernel, grid=(n // STEP,), in_specs=[pl.BlockSpe...  3.34 us
    pallas_call x1, Pallas kernels, shards(): pl.pallas_call(functools.partial(final_kernel, tiles_y), in_specs=[SCALAR...  2.78 us
    pallas_call x1, Pallas kernels, shards(): pl.pallas_call(edge_kernel, in_specs=[SCALARS] + [WHOLE] * (22 + FLUXES),...  2.14 us
    ppermute x3, starting transfers between devices, swap(): lax.ppermute(message[1], axis, far)  2.12 us
  transfers between devices with their start and end apart: 6, of which 0 were waited for; matrix products, arithmetic and copies ran while one was open for 0% of the time, Pallas kernels for 31%

profile of v8, /device:TPU:0, one launch (start us, length us, event | category | flops | bytes accessed | tf_op | source)
XLA Modules:
  0.0 46.8 jit_solution(2693368840148404204)
XLA Ops:
  0.0 0.0 copy-start.3
  0.0 3.3 %y_messages.1 = (f32[328,256]{1,0:T(8,128)S(1)}, f32[328,256]{1,0:T(8,128)S(1)}) custom-call(s32[4,6]{1,0:T(4,128)} %split_ref.7, f32[2,32,48,256]{3,2,1,0:T(8,128)} %res.3, f32[2,32,48,256]{3,2,1,0:T(8,128)} %diag_hbm.1, f32[2,32,48,256]{3,2,1,0:T(8,128)} %crs.1, s32[32,48,256]{2,1,0:T(8,128)} %mask.5, f32[32,48,256]{2,1,0:T(8,128)} %tx_hbm.1, ...), custom_call_target="tpu_custom_call" | custom-call | tf_op jit(solution)/shard_map/y_messages/pallas_call | solution.py:913
  3.4 0.5 %collective-permute-start = (f32[328,256]{1,0:T(8,128)S(1)}, f32[328,256]{1,0:T(8,128)S(1)}, u32[]{:S(2)}, u32[]{:S(2)}) collective-permute-start(f32[328,256]{1,0:T(8,128)S(1)} %get-tuple-element.45), channel_id=1, source_target_pairs={{0,1},{1,0},{2,3},{3,2},{4,5},{5,4},{6,7},{7,6},{8,9},{9,8},{10,11... | collective-permute-start | bytes 1007624 | tf_op jit(solution)/shard_map/ppermute | solution.py:48
  3.9 0.0 copy-start.1
  3.9 0.8 %collective-permute-start.1 = (f32[328,256]{1,0:T(8,128)S(1)}, f32[328,256]{1,0:T(8,128)S(1)}, u32[]{:S(2)}, u32[]{:S(2)}) collective-permute-start(f32[328,256]{1,0:T(8,128)S(1)} %get-tuple-element.46), channel_id=1, source_target_pairs={{1,2},{2,1},{5,6},{6,5},{9,10},{10,9},{13,14},{14,13},{17,18},{18,... | collective-permute-start | bytes 1007624 | tf_op jit(solution)/shard_map/ppermute | solution.py:48
  4.7 0.0 copy-done.3
  4.7 5.4 %prep.1 = (f32[32,48,256]{2,1,0:T(8,128)S(1)}, f32[32,48,256]{2,1,0:T(8,128)S(1)}, f32[32,48,256]{2,1,0:T(8,128)S(1)}, f32[32,48,256]{2,1,0:T(8,128)S(1)}, f32[3...) custom-call(f32[2,32,48,256]{3,2,1,0:T(8,128)} %res.3, ...), custom_call_target="tpu_custom_call" | custom-call | flops 60000000 | bytes 30000000 | tf_op jit(solution)/shard_map/prep/pallas_call | solution.py:926
  10.1 0.0 collective-permute-done.ynear
  10.1 0.0 collective-permute-done.1.yfar
  10.1 0.0 copy-done.1
  10.1 0.0 copy-start
  10.1 0.0 copy-start.2
  10.1 0.0 copy-start.4
  10.1 0.0 copy-start.5
  10.2 0.2 x_messages.1
  10.3 2.6 %collective-permute-start.4 = (f32[304,256]{1,0:T(8,128)S(1)}, f32[304,256]{1,0:T(8,128)S(1)}, u32[]{:S(2)}, u32[]{:S(2)}) collective-permute-start(f32[304,256]{1,0:T(8,128)S(1)} %get-tuple-element.57), channel_id=1, source_target_pairs={{0,4},{4,0},{8,12},{12,8},{16,20},{20,16},{24,28},{28,24},{1,5},{5... | collective-permute-start | bytes 933896 | tf_op jit(solution)/shard_map/ppermute | solution.py:48
  12.9 0.7 %collective-permute-start.5 = (f32[304,256]{1,0:T(8,128)S(1)}, f32[304,256]{1,0:T(8,128)S(1)}, u32[]{:S(2)}, u32[]{:S(2)}) collective-permute-start(f32[304,256]{1,0:T(8,128)S(1)} %get-tuple-element.58), channel_id=1, source_target_pairs={{4,8},{8,4},{12,16},{16,12},{20,24},{24,20},{5,9},{9,5},{13,17},{1... | collective-permute-start | bytes 933896 | tf_op jit(solution)/shard_map/ppermute | solution.py:48
  13.6 0.0 copy-done
  13.6 0.0 copy-done.2
  13.6 0.0 copy-done.4
  13.6 0.0 copy-done.5
  13.6 7.1 %interior.1 = (f32[72,256]{1,0:T(8,128)S(1)}, f32[72,256]{1,0:T(8,128)S(1)}, f32[32,24,256]{2,1,0:T(8,128)S(1)}, f32[32,24,256]{2,1,0:T(8,128)S(1)}, f32[32,24,2...) custom-call(s32[4,6]{1,0:T(4,128)S(1)} %copy-done.5, ...), custom_call_target="tpu_custom_call" | custom-call | flops 60000000 | bytes 30000000 | tf_op jit(solution)/shard_map/interior/pallas_call | solution.py:950
  20.8 4.3 %collective-permute-start.2 = (f32[72,256]{1,0:T(8,128)S(1)}, f32[72,256]{1,0:T(8,128)S(1)}, u32[]{:S(2)}, u32[]{:S(2)}) collective-permute-start(f32[72,256]{1,0:T(8,128)S(1)} %get-tuple-element.55), channel_id=1, source_target_pairs={{0,4},{4,0},{8,12},{12,8},{16,20},{20,16},{24,28},{28,24},{1,5},{5... | collective-permute-start | bytes 221192 | tf_op jit(solution)/shard_map/ppermute | solution.py:48
  25.1 0.7 %collective-permute-start.3 = (f32[72,256]{1,0:T(8,128)S(1)}, f32[72,256]{1,0:T(8,128)S(1)}, u32[]{:S(2)}, u32[]{:S(2)}) collective-permute-start(f32[72,256]{1,0:T(8,128)S(1)} %get-tuple-element.56), channel_id=1, source_target_pairs={{4,8},{8,4},{12,16},{16,12},{20,24},{24,20},{5,9},{9,5},{13,17},{1... | collective-permute-start | bytes 221192 | tf_op jit(solution)/shard_map/ppermute | solution.py:48
  25.8 0.0 collective-permute-done.4.xnear
  25.8 0.0 collective-permute-done.5.xfar
  25.8 2.1 %edges.1 = (f32[32,48,256]{2,1,0:T(8,128)S(1)}, f32[32,48,256]{2,1,0:T(8,128)S(1)}, f32[32,48,256]{2,1,0:T(8,128)S(1)}, f32[32,48,256]{2,1,0:T(8,128)S(1)}, f32[...) custom-call(s32[4,6]{1,0:T(4,128)S(1)} %copy-done.5, ...), custom_call_target="tpu_custom_call", output_to_operand_aliasing={{0}: (23, {}), {1}: (24, {}), {2}: (25, {}), {3}: (26, {}),... | custom-call | tf_op jit(solution)/shard_map/edges/pallas_call | solution.py:972
  28.0 16.0 %all_to_all.11 = f32[32,1,256]{2,1,0:T(1,128)S(1)} all-to-all(f32[32,1,256]{2,1,0:T(1,128)S(1)} %copy.17), channel_id=1, replica_groups=mesh['gx'=8,'gy'=4] {'gx','gy'}, dimensions={0} | all-to-all | bytes 65536 | tf_op jit(solution)/shard_map/all_to_all | solution.py:993
  44.0 0.0 collective-permute-done.2.xnear
  44.0 0.0 collective-permute-done.3.xfar
  44.0 2.8 %final.1 = f32[2,32,48,256]{3,2,1,0:T(8,128)} custom-call(s32[4,6]{1,0:T(4,128)S(1)} %copy-done.5, f32[32,48,256]{2,1,0:T(8,128)S(1)} %copy-done.2, f32[1,192,192]{2,1,0:T(8,128)S(1)} %copy-done.4, f32[328,256]{1,0:T(8,128)S(1)} %collective-permute-done.ynear, f32[328,256]{1,0:T(8,128)S(1)} %collective-permute-done.1.yfar, ...), custom_call_target="tpu_custom_call" | custom-call | tf_op jit(solution)/shard_map/final/pallas_call | solution.py:995
  (2 shorter events, 0.0 us)
Async XLA Ops:
  0.0 4.7 %copy-start.3 = (f32[2,32,48,256]{3,2,1,0:T(8,128)S(1)}, f32[2,32,48,256]{3,2,1,0:T(8,128)}, u32[]{:S(2)}) copy-start(f32[2,32,48,256]{3,2,1,0:T(8,128)} %crs.1) | copy-start | bytes 9437188
  3.4 6.7 %collective-permute-start = (f32[328,256]{1,0:T(8,128)S(1)}, f32[328,256]{1,0:T(8,128)S(1)}, u32[]{:S(2)}, u32[]{:S(2)}) collective-permute-start(f32[328,256]{1,0:T(8,128)S(1)} %get-tuple-element.45), channel_id=1, source_target_pairs={{0,1},{1,0},{2,3},{3,2},{4,5},{5,4},{6,7},{7,6},{8,9},{9,8},{10,11... | collective-permute-start | bytes 1007624 | tf_op jit(solution)/shard_map/ppermute | solution.py:48
  3.9 6.2 %copy-start.1 = (s32[32,48,256]{2,1,0:T(8,128)S(1)}, s32[32,48,256]{2,1,0:T(8,128)}, u32[]{:S(2)}) copy-start(s32[32,48,256]{2,1,0:T(8,128)} %mask.5) | copy-start | bytes 4718596
  3.9 6.2 %collective-permute-start.1 = (f32[328,256]{1,0:T(8,128)S(1)}, f32[328,256]{1,0:T(8,128)S(1)}, u32[]{:S(2)}, u32[]{:S(2)}) collective-permute-start(f32[328,256]{1,0:T(8,128)S(1)} %get-tuple-element.46), channel_id=1, source_target_pairs={{1,2},{2,1},{5,6},{6,5},{9,10},{10,9},{13,14},{14,13},{17,18},{18,... | collective-permute-start | bytes 1007624 | tf_op jit(solution)/shard_map/ppermute | solution.py:48
  10.1 3.5 %copy-start = (f32[2,32,48,256]{3,2,1,0:T(8,128)S(1)}, f32[2,32,48,256]{3,2,1,0:T(8,128)}, u32[]{:S(2)}) copy-start(f32[2,32,48,256]{3,2,1,0:T(8,128)} %res.3) | copy-start | bytes 9437188
  10.1 3.5 %copy-start.2 = (f32[32,48,256]{2,1,0:T(8,128)S(1)}, f32[32,48,256]{2,1,0:T(8,128)}, u32[]{:S(2)}) copy-start(f32[32,48,256]{2,1,0:T(8,128)} %frac.1) | copy-start | bytes 4718596
  10.1 3.5 %copy-start.4 = (f32[1,192,192]{2,1,0:T(8,128)S(1)}, f32[1,192,192]{2,1,0:T(8,128)}, u32[]{:S(2)}) copy-start(f32[1,192,192]{2,1,0:T(8,128)} %inv.3) | copy-start | bytes 442372
  10.1 3.5 %copy-start.5 = (s32[4,6]{1,0:T(4,128)S(1)}, s32[4,6]{1,0:T(4,128)}, u32[]{:S(2)}) copy-start(s32[4,6]{1,0:T(4,128)} %split_ref.7) | copy-start | bytes 292
  10.3 15.4 %collective-permute-start.4 = (f32[304,256]{1,0:T(8,128)S(1)}, f32[304,256]{1,0:T(8,128)S(1)}, u32[]{:S(2)}, u32[]{:S(2)}) collective-permute-start(f32[304,256]{1,0:T(8,128)S(1)} %get-tuple-element.57), channel_id=1, source_target_pairs={{0,4},{4,0},{8,12},{12,8},{16,20},{20,16},{24,28},{28,24},{1,5},{5... | collective-permute-start | bytes 933896 | tf_op jit(solution)/shard_map/ppermute | solution.py:48
  12.9 12.9 %collective-permute-start.5 = (f32[304,256]{1,0:T(8,128)S(1)}, f32[304,256]{1,0:T(8,128)S(1)}, u32[]{:S(2)}, u32[]{:S(2)}) collective-permute-start(f32[304,256]{1,0:T(8,128)S(1)} %get-tuple-element.58), channel_id=1, source_target_pairs={{4,8},{8,4},{12,16},{16,12},{20,24},{24,20},{5,9},{9,5},{13,17},{1... | collective-permute-start | bytes 933896 | tf_op jit(solution)/shard_map/ppermute | solution.py:48
  20.8 23.2 %collective-permute-start.2 = (f32[72,256]{1,0:T(8,128)S(1)}, f32[72,256]{1,0:T(8,128)S(1)}, u32[]{:S(2)}, u32[]{:S(2)}) collective-permute-start(f32[72,256]{1,0:T(8,128)S(1)} %get-tuple-element.55), channel_id=1, source_target_pairs={{0,4},{4,0},{8,12},{12,8},{16,20},{20,16},{24,28},{28,24},{1,5},{5... | collective-permute-start | bytes 221192 | tf_op jit(solution)/shard_map/ppermute | solution.py:48
  25.1 18.9 %collective-permute-start.3 = (f32[72,256]{1,0:T(8,128)S(1)}, f32[72,256]{1,0:T(8,128)S(1)}, u32[]{:S(2)}, u32[]{:S(2)}) collective-permute-start(f32[72,256]{1,0:T(8,128)S(1)} %get-tuple-element.56), channel_id=1, source_target_pairs={{4,8},{8,4},{12,16},{16,12},{20,24},{24,20},{5,9},{9,5},{13,17},{1... | collective-permute-start | bytes 221192 | tf_op jit(solution)/shard_map/ppermute | solution.py:48

commit v9 on v8

--- a/solution.py
+++ b/solution.py
@@ -207,7 +207,7 @@
 
 
 def prep_kernel(res_hbm, diag_hbm, crs, mask_hbm, tx_hbm, ty_hbm, tz_hbm,
-                rhs, own_diag, tot, gain, one, fx, fy, fz, al0, al1, be0, be1,
+                rhs, own_diag, tot, gain, one, fx, fy, fz, al0, al1, be0, be1, fzb,
                 res, diag, mask, tx, ty, tz, sems):
     n, own, wide = mask.shape
     groups = own // 8
@@ -266,7 +266,9 @@
             total = total + jnp.where(first, 0.0, fx[before, here, :])
             ez = along_z(tz[x, here, :], a, lane)
             fz[x, here, :] = ez
-            total = total + ez + z_prev(ez)
+            ez_before = z_prev(ez)
+            fzb[x, here, :] = ez_before
+            total = total + ez + ez_before
             ey = ty[x, here, :] * a
             if k < groups - 1:
                 a_after = mask[x, group(k + 1), :].astype(F32)
@@ -520,7 +522,7 @@
     return ex * step, wx * step
 
 
-def flux_row(o, x, s, lane, two, res, own_diag, split, carried, put):
+def flux_row(o, x, s, lane, two, res, own_diag, fzb, split, carried, put):
     groups = o.groups
 
     def faces_y(k, p, p_turned, p_after, f, f_turned, f_after):
@@ -547,7 +549,8 @@
         ez = o.fz(x, k)
         wz = ez * (f + z_next(f))
         dz = z_next(p) - p
-        ez_before, wz_before, dz_before = z_prev(ez), z_prev(wz), z_prev(dz)
+        wz_before, dz_before = z_prev(wz), z_prev(dz)
+        ez_before = fzb[x, here, :]
         qx, sx = x_flux(o, x, k, two)
         if carried is None:
             qx_before, sx_before = x_flux(o, x - 1, k, two)
@@ -578,7 +581,7 @@
 FLUXES = 6
 
 
-def interior_kernel(split_ref, inv, res, mask, ff, rhs, own_diag, tot, gain, one, fx, fy, fz, ynear, yfar,
+def interior_kernel(split_ref, inv, fzb, res, mask, ff, rhs, own_diag, tot, gain, one, fx, fy, fz, ynear, yfar,
                     late_near, late_far, tot3, gain3, one3, six, end, two, acc, *flux_and_carried):
     flux, carried = flux_and_carried[:FLUXES], flux_and_carried[FLUXES]
     late_messages(split_ref, ff, inv, late_near, late_far)
@@ -624,7 +627,7 @@
             for f, v in enumerate(values):
                 flux[f][x, group(k), :] = v
 
-        flux_row(o, x, s, lane, two_of, res, own_diag, lambda k: split_ref[x // 8, k], carried, put)
+        flux_row(o, x, s, lane, two_of, res, own_diag, fzb, lambda k: split_ref[x // 8, k], carried, put)
         return carry
 
     lax.fori_loop(3, n - 3, row, 0, unroll=2)
@@ -679,7 +682,7 @@
         return self.planes.field(5, k, 1) if x == self.n else super().after(x, k)
 
 
-def edge_kernel(split_ref, res, mask, ff, rhs, own_diag, tot, gain, one, fx, fy, fz, ynear, yfar, xnear, xfar,
+def edge_kernel(split_ref, fzb, res, mask, ff, rhs, own_diag, tot, gain, one, fx, fy, fz, ynear, yfar, xnear, xfar,
                 tot3, gain3, one3, six, end, two, acc, *others):
     flux = others[FLUXES : 2 * FLUXES]
     sent, edge_fx, edge_step, one_edge, gain_edge, two_edge, near_fx, total_acc = others[2 * FLUXES :]
@@ -740,7 +743,7 @@
             for f, v in enumerate(values):
                 flux[f][x, group(k), :] = v
 
-        flux_row(plain, x, s, lane, two_of, res, own_diag, lambda k: split_ref[x // 8, k], None, put)
+        flux_row(plain, x, s, lane, two_of, res, own_diag, fzb, lambda k: split_ref[x // 8, k], None, put)
         return carry
 
     lax.fori_loop(0, 2 * (depth - 2), row, 0, unroll=2)
@@ -923,11 +926,11 @@
     )(pltpu.with_memory_space_constraint(split_layer, pltpu.HBM), *far_columns, *far_columns)
     ynear, yfar = swap(y_messages, "gy", tiles_y)
 
-    rhs, own_diag, tot, gain, one, fx, fy, fz, al0, al1, be0, be1 = pl.pallas_call(
+    rhs, own_diag, tot, gain, one, fx, fy, fz, al0, al1, be0, be1, fzb = pl.pallas_call(
         prep_kernel,
         in_specs=[hbm] * 2 + [WHOLE] + [hbm] * 4,
-        out_specs=[WHOLE] * 12,
-        out_shape=[array(n, own, wide)] * 12,
+        out_specs=[WHOLE] * 13,
+        out_shape=[array(n, own, wide)] * 13,
         scratch_shapes=[pltpu.VMEM(v.shape, v.dtype) for v in columns[:2] + columns[3:7]]
         + [pltpu.SemaphoreType.DMA((6, n // 4))],
         compiler_params=params(16),
@@ -949,7 +952,7 @@
     shared = (residual, mask, frac_flow, rhs, own_diag, tot, gain, one, fx, fy, fz, ynear, yfar)
     late_near, late_far, tot3, gain3, one3, six, end, two, acc, *flux = pl.pallas_call(
         interior_kernel,
-        in_specs=[SCALARS] + [WHOLE] * 14,
+        in_specs=[SCALARS] + [WHOLE] * 15,
         out_specs=[WHOLE] * (9 + FLUXES),
         out_shape=[array(late_rows(own, unknowns, wide), wide)] * 2
         + [array(n, 3 * G, wide)] * 3
@@ -964,14 +967,14 @@
         compiler_params=params(8),
         cost_estimate=cost(60_000_000, 30_000_000),
         name="interior",
-    )(split_layer, coarse_inverse, *shared)
+    )(split_layer, coarse_inverse, fzb, *shared)
     late_near, late_far = swap((late_near, late_far), "gx", tiles_x)
 
     devices = tiles_x * tiles_y
     span = pl.cdiv(unknowns, 128) * 128
     *flux, sent, edge_fx, edge_step = pl.pallas_call(
         edge_kernel,
-        in_specs=[SCALARS] + [WHOLE] * (22 + FLUXES),
+        in_specs=[SCALARS] + [WHOLE] * (23 + FLUXES),
         out_specs=[WHOLE] * (3 + FLUXES),
         out_shape=[array(n, own, wide)] * FLUXES
         + [
@@ -986,10 +989,10 @@
             pltpu.VMEM((2, 10, own, wide), F32),
             pltpu.VMEM((n // 8, own, wide), F32),
         ],
-        input_output_aliases={23 + f: f for f in range(FLUXES)},
+        input_output_aliases={24 + f: f for f in range(FLUXES)},
         compiler_params=params(8),
         name="edges",
-    )(split_layer, *shared, xnear, xfar, tot3, gain3, one3, six, end, two, acc, *flux)
+    )(split_layer, fzb, *shared, xnear, xfar, tot3, gain3, one3, six, end, two, acc, *flux)
     got = lax.all_to_all(sent, ("gx", "gy"), 0, 0, tiled=True)
 
     return pl.pallas_call(

time: 47 us -> 46.7 us (level)
  no operation moved by 1% of the time
where the time goes in v9:
time: 46.7 us; the launch traced here: 46.6 us
  Pallas kernels  20.7 us (44%)
  blocking collectives  16 us (34%)
  starting transfers between devices  9.56 us (20%)
    all_to_all x1, blocking collectives, shards(): got = lax.all_to_all(sent, ('gx', 'gy'), 0, 0, tiled=True)  16 us
    ppermute x3, starting transfers between devices, swap(): lax.ppermute(message[0], axis, near)  7.44 us
    pallas_call x1, Pallas kernels, shards(): pl.pallas_call(interior_kernel, in_specs=[SCALARS] + [WHOLE] * 15, out_sp...  6.82 us
    pallas_call x1, Pallas kernels, shards(): pl.pallas_call(prep_kernel, in_specs=[hbm] * 2 + [WHOLE] + [hbm] * 4, out...  5.38 us
    pallas_call x1, Pallas kernels, shards(): pl.pallas_call(y_message_kernel, grid=(n // STEP,), in_specs=[pl.BlockSpe...  3.34 us
    pallas_call x1, Pallas kernels, shards(): pl.pallas_call(functools.partial(final_kernel, tiles_y), in_specs=[SCALAR...  2.94 us
    ppermute x3, starting transfers between devices, swap(): lax.ppermute(message[1], axis, far)  2.12 us
    pallas_call x1, Pallas kernels, shards(): pl.pallas_call(edge_kernel, in_specs=[SCALARS] + [WHOLE] * (23 + FLUXES),...  2.08 us
  transfers between devices with their start and end apart: 6, of which 0 were waited for; matrix products, arithmetic and copies ran while one was open for 0% of the time, Pallas kernels for 31%

profile of v9, /device:TPU:0, one launch (start us, length us, event | category | flops | bytes accessed | tf_op | source)
XLA Modules:
  0.0 46.6 jit_solution(1127638798664973000)
XLA Ops:
  0.0 0.0 copy-start.3
  0.0 3.3 %y_messages.1 = (f32[328,256]{1,0:T(8,128)S(1)}, f32[328,256]{1,0:T(8,128)S(1)}) custom-call(s32[4,6]{1,0:T(4,128)} %split_ref.7, f32[2,32,48,256]{3,2,1,0:T(8,128)} %res.3, f32[2,32,48,256]{3,2,1,0:T(8,128)} %diag_hbm.1, f32[2,32,48,256]{3,2,1,0:T(8,128)} %crs.1, s32[32,48,256]{2,1,0:T(8,128)} %mask.5, f32[32,48,256]{2,1,0:T(8,128)} %tx_hbm.1, ...), custom_call_target="tpu_custom_call" | custom-call | tf_op jit(solution)/shard_map/y_messages/pallas_call | solution.py:916
  3.4 0.5 %collective-permute-start = (f32[328,256]{1,0:T(8,128)S(1)}, f32[328,256]{1,0:T(8,128)S(1)}, u32[]{:S(2)}, u32[]{:S(2)}) collective-permute-start(f32[328,256]{1,0:T(8,128)S(1)} %get-tuple-element.46), channel_id=1, source_target_pairs={{0,1},{1,0},{2,3},{3,2},{4,5},{5,4},{6,7},{7,6},{8,9},{9,8},{10,11... | collective-permute-start | bytes 1007624 | tf_op jit(solution)/shard_map/ppermute | solution.py:48
  3.9 0.0 copy-start.1
  3.9 0.8 %collective-permute-start.1 = (f32[328,256]{1,0:T(8,128)S(1)}, f32[328,256]{1,0:T(8,128)S(1)}, u32[]{:S(2)}, u32[]{:S(2)}) collective-permute-start(f32[328,256]{1,0:T(8,128)S(1)} %get-tuple-element.47), channel_id=1, source_target_pairs={{1,2},{2,1},{5,6},{6,5},{9,10},{10,9},{13,14},{14,13},{17,18},{18,... | collective-permute-start | bytes 1007624 | tf_op jit(solution)/shard_map/ppermute | solution.py:48
  4.7 0.0 copy-done.3
  4.7 5.4 %prep.1 = (f32[32,48,256]{2,1,0:T(8,128)S(1)}, f32[32,48,256]{2,1,0:T(8,128)S(1)}, f32[32,48,256]{2,1,0:T(8,128)S(1)}, f32[32,48,256]{2,1,0:T(8,128)S(1)}, f32[3...) custom-call(f32[2,32,48,256]{3,2,1,0:T(8,128)} %res.3, ...), custom_call_target="tpu_custom_call" | custom-call | flops 60000000 | bytes 30000000 | tf_op jit(solution)/shard_map/prep/pallas_call | solution.py:929
  10.1 0.0 collective-permute-done.ynear
  10.1 0.0 collective-permute-done.1.yfar
  10.1 0.0 copy-done.1
  10.1 0.0 copy-start
  10.1 0.0 copy-start.2
  10.1 0.0 copy-start.4
  10.2 0.0 copy-start.5
  10.2 0.2 x_messages.1
  10.3 2.6 %collective-permute-start.4 = (f32[304,256]{1,0:T(8,128)S(1)}, f32[304,256]{1,0:T(8,128)S(1)}, u32[]{:S(2)}, u32[]{:S(2)}) collective-permute-start(f32[304,256]{1,0:T(8,128)S(1)} %get-tuple-element.59), channel_id=1, source_target_pairs={{0,4},{4,0},{8,12},{12,8},{16,20},{20,16},{24,28},{28,24},{1,5},{5... | collective-permute-start | bytes 933896 | tf_op jit(solution)/shard_map/ppermute | solution.py:48
  12.9 0.7 %collective-permute-start.5 = (f32[304,256]{1,0:T(8,128)S(1)}, f32[304,256]{1,0:T(8,128)S(1)}, u32[]{:S(2)}, u32[]{:S(2)}) collective-permute-start(f32[304,256]{1,0:T(8,128)S(1)} %get-tuple-element.60), channel_id=1, source_target_pairs={{4,8},{8,4},{12,16},{16,12},{20,24},{24,20},{5,9},{9,5},{13,17},{1... | collective-permute-start | bytes 933896 | tf_op jit(solution)/shard_map/ppermute | solution.py:48
  13.6 0.0 copy-done
  13.6 0.0 copy-done.2
  13.6 0.0 copy-done.4
  13.6 0.0 copy-done.5
  13.6 6.8 %interior.1 = (f32[72,256]{1,0:T(8,128)S(1)}, f32[72,256]{1,0:T(8,128)S(1)}, f32[32,24,256]{2,1,0:T(8,128)S(1)}, f32[32,24,256]{2,1,0:T(8,128)S(1)}, f32[32,24,2...) custom-call(s32[4,6]{1,0:T(4,128)S(1)} %copy-done.5, ...), custom_call_target="tpu_custom_call" | custom-call | flops 60000000 | bytes 30000000 | tf_op jit(solution)/shard_map/interior/pallas_call | solution.py:953
  20.5 4.3 %collective-permute-start.2 = (f32[72,256]{1,0:T(8,128)S(1)}, f32[72,256]{1,0:T(8,128)S(1)}, u32[]{:S(2)}, u32[]{:S(2)}) collective-permute-start(f32[72,256]{1,0:T(8,128)S(1)} %get-tuple-element.57), channel_id=1, source_target_pairs={{0,4},{4,0},{8,12},{12,8},{16,20},{20,16},{24,28},{28,24},{1,5},{5... | collective-permute-start | bytes 221192 | tf_op jit(solution)/shard_map/ppermute | solution.py:48
  24.8 0.7 %collective-permute-start.3 = (f32[72,256]{1,0:T(8,128)S(1)}, f32[72,256]{1,0:T(8,128)S(1)}, u32[]{:S(2)}, u32[]{:S(2)}) collective-permute-start(f32[72,256]{1,0:T(8,128)S(1)} %get-tuple-element.58), channel_id=1, source_target_pairs={{4,8},{8,4},{12,16},{16,12},{20,24},{24,20},{5,9},{9,5},{13,17},{1... | collective-permute-start | bytes 221192 | tf_op jit(solution)/shard_map/ppermute | solution.py:48
  25.5 0.0 collective-permute-done.4.xnear
  25.5 0.0 collective-permute-done.5.xfar
  25.5 2.1 %edges.1 = (f32[32,48,256]{2,1,0:T(8,128)S(1)}, f32[32,48,256]{2,1,0:T(8,128)S(1)}, f32[32,48,256]{2,1,0:T(8,128)S(1)}, f32[32,48,256]{2,1,0:T(8,128)S(1)}, f32[...) custom-call(s32[4,6]{1,0:T(4,128)S(1)} %copy-done.5, ...), custom_call_target="tpu_custom_call", output_to_operand_aliasing={{0}: (24, {}), {1}: (25, {}), {2}: (26, {}), {3}: (27, {}),... | custom-call | tf_op jit(solution)/shard_map/edges/pallas_call | solution.py:975
  27.6 16.0 %all_to_all.11 = f32[32,1,256]{2,1,0:T(1,128)S(1)} all-to-all(f32[32,1,256]{2,1,0:T(1,128)S(1)} %copy.17), channel_id=1, replica_groups=mesh['gx'=8,'gy'=4] {'gx','gy'}, dimensions={0} | all-to-all | bytes 65536 | tf_op jit(solution)/shard_map/all_to_all | solution.py:996
  43.6 0.0 collective-permute-done.2.xnear
  43.6 0.0 collective-permute-done.3.xfar
  43.6 2.9 %final.1 = f32[2,32,48,256]{3,2,1,0:T(8,128)} custom-call(s32[4,6]{1,0:T(4,128)S(1)} %copy-done.5, f32[32,48,256]{2,1,0:T(8,128)S(1)} %copy-done.2, f32[1,192,192]{2,1,0:T(8,128)S(1)} %copy-done.4, f32[328,256]{1,0:T(8,128)S(1)} %collective-permute-done.ynear, f32[328,256]{1,0:T(8,128)S(1)} %collective-permute-done.1.yfar, ...), custom_call_target="tpu_custom_call" | custom-call | tf_op jit(solution)/shard_map/final/pallas_call | solution.py:998
  (2 shorter events, 0.0 us)
Async XLA Ops:
  0.0 4.7 %copy-start.3 = (f32[2,32,48,256]{3,2,1,0:T(8,128)S(1)}, f32[2,32,48,256]{3,2,1,0:T(8,128)}, u32[]{:S(2)}) copy-start(f32[2,32,48,256]{3,2,1,0:T(8,128)} %crs.1) | copy-start | bytes 9437188
  3.4 6.7 %collective-permute-start = (f32[328,256]{1,0:T(8,128)S(1)}, f32[328,256]{1,0:T(8,128)S(1)}, u32[]{:S(2)}, u32[]{:S(2)}) collective-permute-start(f32[328,256]{1,0:T(8,128)S(1)} %get-tuple-element.46), channel_id=1, source_target_pairs={{0,1},{1,0},{2,3},{3,2},{4,5},{5,4},{6,7},{7,6},{8,9},{9,8},{10,11... | collective-permute-start | bytes 1007624 | tf_op jit(solution)/shard_map/ppermute | solution.py:48
  3.9 6.2 %copy-start.1 = (s32[32,48,256]{2,1,0:T(8,128)S(1)}, s32[32,48,256]{2,1,0:T(8,128)}, u32[]{:S(2)}) copy-start(s32[32,48,256]{2,1,0:T(8,128)} %mask.5) | copy-start | bytes 4718596
  3.9 6.2 %collective-permute-start.1 = (f32[328,256]{1,0:T(8,128)S(1)}, f32[328,256]{1,0:T(8,128)S(1)}, u32[]{:S(2)}, u32[]{:S(2)}) collective-permute-start(f32[328,256]{1,0:T(8,128)S(1)} %get-tuple-element.47), channel_id=1, source_target_pairs={{1,2},{2,1},{5,6},{6,5},{9,10},{10,9},{13,14},{14,13},{17,18},{18,... | collective-permute-start | bytes 1007624 | tf_op jit(solution)/shard_map/ppermute | solution.py:48
  10.1 3.5 %copy-start = (f32[2,32,48,256]{3,2,1,0:T(8,128)S(1)}, f32[2,32,48,256]{3,2,1,0:T(8,128)}, u32[]{:S(2)}) copy-start(f32[2,32,48,256]{3,2,1,0:T(8,128)} %res.3) | copy-start | bytes 9437188
  10.1 3.5 %copy-start.2 = (f32[32,48,256]{2,1,0:T(8,128)S(1)}, f32[32,48,256]{2,1,0:T(8,128)}, u32[]{:S(2)}) copy-start(f32[32,48,256]{2,1,0:T(8,128)} %frac.1) | copy-start | bytes 4718596
  10.1 3.5 %copy-start.4 = (f32[1,192,192]{2,1,0:T(8,128)S(1)}, f32[1,192,192]{2,1,0:T(8,128)}, u32[]{:S(2)}) copy-start(f32[1,192,192]{2,1,0:T(8,128)} %inv.3) | copy-start | bytes 442372
  10.2 3.5 %copy-start.5 = (s32[4,6]{1,0:T(4,128)S(1)}, s32[4,6]{1,0:T(4,128)}, u32[]{:S(2)}) copy-start(s32[4,6]{1,0:T(4,128)} %split_ref.7) | copy-start | bytes 292
  10.3 15.1 %collective-permute-start.4 = (f32[304,256]{1,0:T(8,128)S(1)}, f32[304,256]{1,0:T(8,128)S(1)}, u32[]{:S(2)}, u32[]{:S(2)}) collective-permute-start(f32[304,256]{1,0:T(8,128)S(1)} %get-tuple-element.59), channel_id=1, source_target_pairs={{0,4},{4,0},{8,12},{12,8},{16,20},{20,16},{24,28},{28,24},{1,5},{5... | collective-permute-start | bytes 933896 | tf_op jit(solution)/shard_map/ppermute | solution.py:48
  12.9 12.5 %collective-permute-start.5 = (f32[304,256]{1,0:T(8,128)S(1)}, f32[304,256]{1,0:T(8,128)S(1)}, u32[]{:S(2)}, u32[]{:S(2)}) collective-permute-start(f32[304,256]{1,0:T(8,128)S(1)} %get-tuple-element.60), channel_id=1, source_target_pairs={{4,8},{8,4},{12,16},{16,12},{20,24},{24,20},{5,9},{9,5},{13,17},{1... | collective-permute-start | bytes 933896 | tf_op jit(solution)/shard_map/ppermute | solution.py:48
  20.5 23.2 %collective-permute-start.2 = (f32[72,256]{1,0:T(8,128)S(1)}, f32[72,256]{1,0:T(8,128)S(1)}, u32[]{:S(2)}, u32[]{:S(2)}) collective-permute-start(f32[72,256]{1,0:T(8,128)S(1)} %get-tuple-element.57), channel_id=1, source_target_pairs={{0,4},{4,0},{8,12},{12,8},{16,20},{20,16},{24,28},{28,24},{1,5},{5... | collective-permute-start | bytes 221192 | tf_op jit(solution)/shard_map/ppermute | solution.py:48
  24.8 18.8 %collective-permute-start.3 = (f32[72,256]{1,0:T(8,128)S(1)}, f32[72,256]{1,0:T(8,128)S(1)}, u32[]{:S(2)}, u32[]{:S(2)}) collective-permute-start(f32[72,256]{1,0:T(8,128)S(1)} %get-tuple-element.58), channel_id=1, source_target_pairs={{4,8},{8,4},{12,16},{16,12},{20,24},{24,20},{5,9},{9,5},{13,17},{1... | collective-permute-start | bytes 221192 | tf_op jit(solution)/shard_map/ppermute | solution.py:48

commit v10 on v9

--- a/solution.py
+++ b/solution.py
@@ -889,7 +889,7 @@
             copy.start()
         return carry
 
-    lax.fori_loop(0, rows_b, block, 0)
+    lax.fori_loop(0, rows_b, block, 0, unroll=2)
     for q in range(2 * rows_b):
         for copy in copies(q):
             copy.wait()

time: 46.7 us -> 46.7 us (level)
  no operation moved by 1% of the time
where the time goes in v10:
time: 46.7 us; the launch traced here: 46.5 us
  Pallas kernels  20.7 us (44%)
  blocking collectives  16 us (34%)
  starting transfers between devices  9.56 us (20%)
    all_to_all x1, blocking collectives, shards(): got = lax.all_to_all(sent, ('gx', 'gy'), 0, 0, tiled=True)  16 us
    ppermute x3, starting transfers between devices, swap(): lax.ppermute(message[0], axis, near)  7.44 us
    pallas_call x1, Pallas kernels, shards(): pl.pallas_call(interior_kernel, in_specs=[SCALARS] + [WHOLE] * 15, out_sp...  6.82 us
    pallas_call x1, Pallas kernels, shards(): pl.pallas_call(prep_kernel, in_specs=[hbm] * 2 + [WHOLE] + [hbm] * 4, out...  5.38 us
    pallas_call x1, Pallas kernels, shards(): pl.pallas_call(y_message_kernel, grid=(n // STEP,), in_specs=[pl.BlockSpe...  3.34 us
    pallas_call x1, Pallas kernels, shards(): pl.pallas_call(functools.partial(final_kernel, tiles_y), in_specs=[SCALAR...  2.92 us
    ppermute x3, starting transfers between devices, swap(): lax.ppermute(message[1], axis, far)  2.12 us
    pallas_call x1, Pallas kernels, shards(): pl.pallas_call(edge_kernel, in_specs=[SCALARS] + [WHOLE] * (23 + FLUXES),...  2.08 us
  transfers between devices with their start and end apart: 6, of which 0 were waited for; matrix products, arithmetic and copies ran while one was open for 0% of the time, Pallas kernels for 31%

profile of v10, /device:TPU:0, one launch (start us, length us, event | category | flops | bytes accessed | tf_op | source)
XLA Modules:
  0.0 46.5 jit_solution(8359422188729471492)
XLA Ops:
  0.0 0.0 copy-start.3
  0.0 3.3 %y_messages.1 = (f32[328,256]{1,0:T(8,128)S(1)}, f32[328,256]{1,0:T(8,128)S(1)}) custom-call(s32[4,6]{1,0:T(4,128)} %split_ref.7, f32[2,32,48,256]{3,2,1,0:T(8,128)} %res.3, f32[2,32,48,256]{3,2,1,0:T(8,128)} %diag_hbm.1, f32[2,32,48,256]{3,2,1,0:T(8,128)} %crs.1, s32[32,48,256]{2,1,0:T(8,128)} %mask.5, f32[32,48,256]{2,1,0:T(8,128)} %tx_hbm.1, ...), custom_call_target="tpu_custom_call" | custom-call | tf_op jit(solution)/shard_map/y_messages/pallas_call | solution.py:916
  3.4 0.5 %collective-permute-start = (f32[328,256]{1,0:T(8,128)S(1)}, f32[328,256]{1,0:T(8,128)S(1)}, u32[]{:S(2)}, u32[]{:S(2)}) collective-permute-start(f32[328,256]{1,0:T(8,128)S(1)} %get-tuple-element.46), channel_id=1, source_target_pairs={{0,1},{1,0},{2,3},{3,2},{4,5},{5,4},{6,7},{7,6},{8,9},{9,8},{10,11... | collective-permute-start | bytes 1007624 | tf_op jit(solution)/shard_map/ppermute | solution.py:48
  3.9 0.0 copy-start.1
  3.9 0.8 %collective-permute-start.1 = (f32[328,256]{1,0:T(8,128)S(1)}, f32[328,256]{1,0:T(8,128)S(1)}, u32[]{:S(2)}, u32[]{:S(2)}) collective-permute-start(f32[328,256]{1,0:T(8,128)S(1)} %get-tuple-element.47), channel_id=1, source_target_pairs={{1,2},{2,1},{5,6},{6,5},{9,10},{10,9},{13,14},{14,13},{17,18},{18,... | collective-permute-start | bytes 1007624 | tf_op jit(solution)/shard_map/ppermute | solution.py:48
  4.7 0.0 copy-done.3
  4.7 5.4 %prep.1 = (f32[32,48,256]{2,1,0:T(8,128)S(1)}, f32[32,48,256]{2,1,0:T(8,128)S(1)}, f32[32,48,256]{2,1,0:T(8,128)S(1)}, f32[32,48,256]{2,1,0:T(8,128)S(1)}, f32[3...) custom-call(f32[2,32,48,256]{3,2,1,0:T(8,128)} %res.3, ...), custom_call_target="tpu_custom_call" | custom-call | flops 60000000 | bytes 30000000 | tf_op jit(solution)/shard_map/prep/pallas_call | solution.py:929
  10.1 0.0 collective-permute-done.ynear
  10.1 0.0 collective-permute-done.1.yfar
  10.1 0.0 copy-done.1
  10.1 0.0 copy-start
  10.1 0.0 copy-start.2
  10.1 0.0 copy-start.4
  10.2 0.0 copy-start.5
  10.2 0.2 x_messages.1
  10.3 2.6 %collective-permute-start.4 = (f32[304,256]{1,0:T(8,128)S(1)}, f32[304,256]{1,0:T(8,128)S(1)}, u32[]{:S(2)}, u32[]{:S(2)}) collective-permute-start(f32[304,256]{1,0:T(8,128)S(1)} %get-tuple-element.59), channel_id=1, source_target_pairs={{0,4},{4,0},{8,12},{12,8},{16,20},{20,16},{24,28},{28,24},{1,5},{5... | collective-permute-start | bytes 933896 | tf_op jit(solution)/shard_map/ppermute | solution.py:48
  12.9 0.7 %collective-permute-start.5 = (f32[304,256]{1,0:T(8,128)S(1)}, f32[304,256]{1,0:T(8,128)S(1)}, u32[]{:S(2)}, u32[]{:S(2)}) collective-permute-start(f32[304,256]{1,0:T(8,128)S(1)} %get-tuple-element.60), channel_id=1, source_target_pairs={{4,8},{8,4},{12,16},{16,12},{20,24},{24,20},{5,9},{9,5},{13,17},{1... | collective-permute-start | bytes 933896 | tf_op jit(solution)/shard_map/ppermute | solution.py:48
  13.6 0.0 copy-done
  13.6 0.0 copy-done.2
  13.6 0.0 copy-done.4
  13.6 0.0 copy-done.5
  13.6 6.8 %interior.1 = (f32[72,256]{1,0:T(8,128)S(1)}, f32[72,256]{1,0:T(8,128)S(1)}, f32[32,24,256]{2,1,0:T(8,128)S(1)}, f32[32,24,256]{2,1,0:T(8,128)S(1)}, f32[32,24,2...) custom-call(s32[4,6]{1,0:T(4,128)S(1)} %copy-done.5, ...), custom_call_target="tpu_custom_call" | custom-call | flops 60000000 | bytes 30000000 | tf_op jit(solution)/shard_map/interior/pallas_call | solution.py:953
  20.5 4.3 %collective-permute-start.2 = (f32[72,256]{1,0:T(8,128)S(1)}, f32[72,256]{1,0:T(8,128)S(1)}, u32[]{:S(2)}, u32[]{:S(2)}) collective-permute-start(f32[72,256]{1,0:T(8,128)S(1)} %get-tuple-element.57), channel_id=1, source_target_pairs={{0,4},{4,0},{8,12},{12,8},{16,20},{20,16},{24,28},{28,24},{1,5},{5... | collective-permute-start | bytes 221192 | tf_op jit(solution)/shard_map/ppermute | solution.py:48
  24.8 0.7 %collective-permute-start.3 = (f32[72,256]{1,0:T(8,128)S(1)}, f32[72,256]{1,0:T(8,128)S(1)}, u32[]{:S(2)}, u32[]{:S(2)}) collective-permute-start(f32[72,256]{1,0:T(8,128)S(1)} %get-tuple-element.58), channel_id=1, source_target_pairs={{4,8},{8,4},{12,16},{16,12},{20,24},{24,20},{5,9},{9,5},{13,17},{1... | collective-permute-start | bytes 221192 | tf_op jit(solution)/shard_map/ppermute | solution.py:48
  25.5 0.0 collective-permute-done.4.xnear
  25.5 0.0 collective-permute-done.5.xfar
  25.5 2.1 %edges.1 = (f32[32,48,256]{2,1,0:T(8,128)S(1)}, f32[32,48,256]{2,1,0:T(8,128)S(1)}, f32[32,48,256]{2,1,0:T(8,128)S(1)}, f32[32,48,256]{2,1,0:T(8,128)S(1)}, f32[...) custom-call(s32[4,6]{1,0:T(4,128)S(1)} %copy-done.5, ...), custom_call_target="tpu_custom_call", output_to_operand_aliasing={{0}: (24, {}), {1}: (25, {}), {2}: (26, {}), {3}: (27, {}),... | custom-call | tf_op jit(solution)/shard_map/edges/pallas_call | solution.py:975
  27.6 16.0 %all_to_all.11 = f32[32,1,256]{2,1,0:T(1,128)S(1)} all-to-all(f32[32,1,256]{2,1,0:T(1,128)S(1)} %copy.17), channel_id=1, replica_groups=mesh['gx'=8,'gy'=4] {'gx','gy'}, dimensions={0} | all-to-all | bytes 65536 | tf_op jit(solution)/shard_map/all_to_all | solution.py:996
  43.6 0.0 collective-permute-done.2.xnear
  43.6 0.0 collective-permute-done.3.xfar
  43.6 2.9 %final.1 = f32[2,32,48,256]{3,2,1,0:T(8,128)} custom-call(s32[4,6]{1,0:T(4,128)S(1)} %copy-done.5, f32[32,48,256]{2,1,0:T(8,128)S(1)} %copy-done.2, f32[1,192,192]{2,1,0:T(8,128)S(1)} %copy-done.4, f32[328,256]{1,0:T(8,128)S(1)} %collective-permute-done.ynear, f32[328,256]{1,0:T(8,128)S(1)} %collective-permute-done.1.yfar, ...), custom_call_target="tpu_custom_call" | custom-call | tf_op jit(solution)/shard_map/final/pallas_call | solution.py:998
  (2 shorter events, 0.0 us)
Async XLA Ops:
  0.0 4.7 %copy-start.3 = (f32[2,32,48,256]{3,2,1,0:T(8,128)S(1)}, f32[2,32,48,256]{3,2,1,0:T(8,128)}, u32[]{:S(2)}) copy-start(f32[2,32,48,256]{3,2,1,0:T(8,128)} %crs.1) | copy-start | bytes 9437188
  3.4 6.7 %collective-permute-start = (f32[328,256]{1,0:T(8,128)S(1)}, f32[328,256]{1,0:T(8,128)S(1)}, u32[]{:S(2)}, u32[]{:S(2)}) collective-permute-start(f32[328,256]{1,0:T(8,128)S(1)} %get-tuple-element.46), channel_id=1, source_target_pairs={{0,1},{1,0},{2,3},{3,2},{4,5},{5,4},{6,7},{7,6},{8,9},{9,8},{10,11... | collective-permute-start | bytes 1007624 | tf_op jit(solution)/shard_map/ppermute | solution.py:48
  3.9 6.2 %copy-start.1 = (s32[32,48,256]{2,1,0:T(8,128)S(1)}, s32[32,48,256]{2,1,0:T(8,128)}, u32[]{:S(2)}) copy-start(s32[32,48,256]{2,1,0:T(8,128)} %mask.5) | copy-start | bytes 4718596
  3.9 6.2 %collective-permute-start.1 = (f32[328,256]{1,0:T(8,128)S(1)}, f32[328,256]{1,0:T(8,128)S(1)}, u32[]{:S(2)}, u32[]{:S(2)}) collective-permute-start(f32[328,256]{1,0:T(8,128)S(1)} %get-tuple-element.47), channel_id=1, source_target_pairs={{1,2},{2,1},{5,6},{6,5},{9,10},{10,9},{13,14},{14,13},{17,18},{18,... | collective-permute-start | bytes 1007624 | tf_op jit(solution)/shard_map/ppermute | solution.py:48
  10.1 3.5 %copy-start = (f32[2,32,48,256]{3,2,1,0:T(8,128)S(1)}, f32[2,32,48,256]{3,2,1,0:T(8,128)}, u32[]{:S(2)}) copy-start(f32[2,32,48,256]{3,2,1,0:T(8,128)} %res.3) | copy-start | bytes 9437188
  10.1 3.5 %copy-start.2 = (f32[32,48,256]{2,1,0:T(8,128)S(1)}, f32[32,48,256]{2,1,0:T(8,128)}, u32[]{:S(2)}) copy-start(f32[32,48,256]{2,1,0:T(8,128)} %frac.1) | copy-start | bytes 4718596
  10.1 3.5 %copy-start.4 = (f32[1,192,192]{2,1,0:T(8,128)S(1)}, f32[1,192,192]{2,1,0:T(8,128)}, u32[]{:S(2)}) copy-start(f32[1,192,192]{2,1,0:T(8,128)} %inv.3) | copy-start | bytes 442372
  10.2 3.5 %copy-start.5 = (s32[4,6]{1,0:T(4,128)S(1)}, s32[4,6]{1,0:T(4,128)}, u32[]{:S(2)}) copy-start(s32[4,6]{1,0:T(4,128)} %split_ref.7) | copy-start | bytes 292
  10.3 15.1 %collective-permute-start.4 = (f32[304,256]{1,0:T(8,128)S(1)}, f32[304,256]{1,0:T(8,128)S(1)}, u32[]{:S(2)}, u32[]{:S(2)}) collective-permute-start(f32[304,256]{1,0:T(8,128)S(1)} %get-tuple-element.59), channel_id=1, source_target_pairs={{0,4},{4,0},{8,12},{12,8},{16,20},{20,16},{24,28},{28,24},{1,5},{5... | collective-permute-start | bytes 933896 | tf_op jit(solution)/shard_map/ppermute | solution.py:48
  12.9 12.5 %collective-permute-start.5 = (f32[304,256]{1,0:T(8,128)S(1)}, f32[304,256]{1,0:T(8,128)S(1)}, u32[]{:S(2)}, u32[]{:S(2)}) collective-permute-start(f32[304,256]{1,0:T(8,128)S(1)} %get-tuple-element.60), channel_id=1, source_target_pairs={{4,8},{8,4},{12,16},{16,12},{20,24},{24,20},{5,9},{9,5},{13,17},{1... | collective-permute-start | bytes 933896 | tf_op jit(solution)/shard_map/ppermute | solution.py:48
  20.5 23.2 %collective-permute-start.2 = (f32[72,256]{1,0:T(8,128)S(1)}, f32[72,256]{1,0:T(8,128)S(1)}, u32[]{:S(2)}, u32[]{:S(2)}) collective-permute-start(f32[72,256]{1,0:T(8,128)S(1)} %get-tuple-element.57), channel_id=1, source_target_pairs={{0,4},{4,0},{8,12},{12,8},{16,20},{20,16},{24,28},{28,24},{1,5},{5... | collective-permute-start | bytes 221192 | tf_op jit(solution)/shard_map/ppermute | solution.py:48
  24.8 18.8 %collective-permute-start.3 = (f32[72,256]{1,0:T(8,128)S(1)}, f32[72,256]{1,0:T(8,128)S(1)}, u32[]{:S(2)}, u32[]{:S(2)}) collective-permute-start(f32[72,256]{1,0:T(8,128)S(1)} %get-tuple-element.58), channel_id=1, source_target_pairs={{4,8},{8,4},{12,16},{16,12},{20,24},{24,20},{5,9},{9,5},{13,17},{1... | collective-permute-start | bytes 221192 | tf_op jit(solution)/shard_map/ppermute | solution.py:48
